TPU v7x, 512 devices: a whole 4x8x8 slice. The times are simulated.
512 devices in a mesh: dp: 8 (over z_lo, core), expert: 64 (over x, y, z_hi).
Axes of the slice: x: 4, y: 8, z: 8 (z_hi: 2, z_lo: 4; z = z_hi * 4 + z_lo), core: 2. Of those that a mesh axis runs over, the one named last changes fastest.
Arguments:
- tokens: bfloat16 [10240, 2048], P('expert', 'dp'), may hold values from -6 to 6
- grad_out: bfloat16 [10240, 2048], P('expert', 'dp'), may hold values from -6 to 6
- expert_ids: int32 [10240, 2], P('expert'), may hold values from 0 to 63, all different within a row; in each aligned block of 160 rows (0 to 159, 160 to 319, ...) at most 7 rows name the same one
- gate_probs: float32 [10240, 2], P('expert'), may hold values from 0.1 to 1
- gate_weight: bfloat16 [64, 2048, 1024], P('expert', None, 'dp'), may hold values from -0.125 to 0.125
- up_weight: bfloat16 [64, 2048, 1024], P('expert', None, 'dp'), may hold values from -0.125 to 0.125
- down_weight: bfloat16 [64, 1024, 2048], P('expert', 'dp'), may hold values from -0.1875 to 0.1875
Outputs:
- layer_out: bfloat16 [10240, 2048], P('expert', 'dp')
- grad_tokens: bfloat16 [10240, 2048], P('expert', 'dp')
- grad_gate_weight: bfloat16 [64, 2048, 1024], P('expert', None, 'dp')
- grad_up_weight: bfloat16 [64, 2048, 1024], P('expert', None, 'dp')
- grad_down_weight: bfloat16 [64, 1024, 2048], P('expert', 'dp')
Inputs may be any that keep to these rules, and one draw needn't show every extreme that they name: `expert_ids`: the two ids of a row differ. In every aligned block of 160 rows no expert is named by more than 7 rows, a bound that some block reaches.
All inputs are finite; a program needn't handle non-finite values.
Results may differ from a plain program's by a relative error of at most 0.015.
Values may be sent and summed in bfloat16 or wider, within the bound.
No kernel may reach another device: no remote copies, remote signals or barrier semaphores. Data moves between devices by JAX's collectives and lax.ppermute only.
A program may use at most 64 MiB of HBM per device.

v0:
```python
import jax
import jax.numpy as jnp
from jax import lax
from jax.sharding import PartitionSpec as P


def in_one_piece(arrays, axis, split_dim, concat_dim, along):
    both = jnp.concatenate(arrays, axis=along)
    filled, at, gathered = (
        lax.all_to_all(both, axis, split_axis=split_dim, concat_axis=concat_dim, tiled=True),
        0,
        [],
    )
    for a in arrays:
        gathered.append(lax.slice_in_dim(filled, at, at + a.shape[along], axis=along))
        at += a.shape[along]
    return tuple(gathered)


def in_one_piece_2(arrays, axis, dim, along):
    both = jnp.concatenate(arrays, axis=along)
    filled, at, gathered = (lax.all_gather(both, axis, axis=dim, tiled=True), 0, [])
    for a in arrays:
        gathered.append(lax.slice_in_dim(filled, at, at + a.shape[along], axis=along))
        at += a.shape[along]
    return tuple(gathered)


def in_one_piece_3(arrays, axis, dim, along):
    both = jnp.concatenate(arrays, axis=along)
    filled, at, gathered = (lax.psum_scatter(both, axis, scatter_dimension=dim, tiled=True), 0, [])
    for a in arrays:
        gathered.append(lax.slice_in_dim(filled, at, at + a.shape[along], axis=along))
        at += a.shape[along]
    return tuple(gathered)


def route_slots(expert_ids, experts_all, capacity):
    row_count = expert_ids.shape[0]
    flat_ids = expert_ids.reshape(row_count * 2)
    onehot = (flat_ids[:, None] == jnp.arange(experts_all, dtype=jnp.int32)[None, :]).astype(
        jnp.int32
    )
    before = jnp.cumsum(onehot, axis=0) - onehot
    slot_index = jnp.sum(before * onehot, axis=1)
    position = flat_ids * capacity + slot_index
    owner_table = (
        jnp.full((experts_all * capacity,), -1, jnp.int32)
        .at[position]
        .set(jnp.arange(row_count * 2, dtype=jnp.int32))
    )
    return (position, owner_table)


def fill_buffers(values, grads, flat_probs, owner_table):
    is_valid = owner_table >= 0
    safe_index = jnp.maximum(owner_table, 0)
    row_index = safe_index // 2
    picked = jnp.where(
        is_valid[:, None], jnp.take(values, row_index, axis=0), jnp.zeros((), values.dtype)
    )
    factor = jnp.where(is_valid, jnp.take(flat_probs, safe_index), jnp.zeros((), flat_probs.dtype))
    scaled = (jnp.take(grads, row_index, axis=0).astype(jnp.float32) * factor[:, None]).astype(
        jnp.bfloat16
    )
    return (picked, scaled)


def combine_rows(returned, position, flat_probs, weighted):
    taken = jnp.take(returned, position, axis=0)
    if weighted:
        taken = taken * flat_probs[:, None]
    return taken.reshape(position.shape[0] // 2, 2, taken.shape[1]).sum(axis=1)


def expert_work(routed, routed_grad, gate_mat, up_mat, down_mat):
    contract_last = (((1,), (1,)), ((), ()))
    contract_first = (((0,), (0,)), ((), ()))
    gate_pre = jnp.dot(routed, gate_mat, preferred_element_type=jnp.float32)
    up_pre = jnp.dot(routed, up_mat, preferred_element_type=jnp.float32)
    sigmoid_gate = jax.nn.sigmoid(gate_pre)
    activated = gate_pre * sigmoid_gate
    hidden = (activated * up_pre).astype(jnp.bfloat16)
    part_rows = jnp.dot(hidden, down_mat, preferred_element_type=jnp.float32).astype(jnp.bfloat16)
    grad_hidden = lax.dot_general(
        routed_grad, down_mat, contract_last, preferred_element_type=jnp.float32
    )
    grad_gate_pre = (
        grad_hidden * up_pre * sigmoid_gate * (1.0 + gate_pre * (1.0 - sigmoid_gate))
    ).astype(jnp.bfloat16)
    grad_up_pre = (grad_hidden * activated).astype(jnp.bfloat16)
    back_rows = lax.dot_general(
        grad_gate_pre, gate_mat, contract_last, preferred_element_type=jnp.float32
    )
    back_rows = (
        back_rows
        + lax.dot_general(grad_up_pre, up_mat, contract_last, preferred_element_type=jnp.float32)
    ).astype(jnp.bfloat16)
    grad_down = lax.dot_general(
        hidden, routed_grad, contract_first, preferred_element_type=jnp.float32
    ).astype(jnp.bfloat16)
    grad_gate = lax.dot_general(
        routed, grad_gate_pre, contract_first, preferred_element_type=jnp.float32
    ).astype(jnp.bfloat16)
    grad_up = lax.dot_general(
        routed, grad_up_pre, contract_first, preferred_element_type=jnp.float32
    ).astype(jnp.bfloat16)
    return (part_rows, back_rows, grad_gate, grad_up, grad_down)


def per_device(tokens, grad_out, expert_ids, gate_probs, gate_weight, up_weight, down_weight):
    experts_all = lax.axis_size("expert")
    row_count = expert_ids.shape[0]
    capacity = max(2, 3 * row_count // experts_all)
    position, owner_table = route_slots(expert_ids, experts_all, capacity)
    flat_probs = gate_probs.reshape(row_count * 2)
    send_rows, send_grads = fill_buffers(tokens, grad_out, flat_probs, owner_table)
    slice_rows, slice_grads = in_one_piece((send_rows, send_grads), "expert", 0, 0, 1)
    routed, routed_grad = in_one_piece_2((slice_rows, slice_grads), "dp", 1, 0)
    part_rows, back_rows, grad_gate, grad_up, grad_down = expert_work(
        routed, routed_grad, gate_weight[0], up_weight[0], down_weight[0]
    )
    part_total, back_total = tuple(
        (part.astype(jnp.float32) for part in in_one_piece_3((part_rows, back_rows), "dp", 1, 0))
    )
    part_back, grad_back = tuple(
        (
            part.astype(jnp.float32)
            for part in in_one_piece(
                (part_total.astype(jnp.bfloat16), back_total.astype(jnp.bfloat16)),
                "expert",
                0,
                0,
                1,
            )
        )
    )
    out_total = combine_rows(part_back, position, flat_probs, True)
    grad_total = combine_rows(grad_back, position, flat_probs, False)
    return (
        out_total.astype(jnp.bfloat16),
        grad_total.astype(jnp.bfloat16),
        grad_gate[None],
        grad_up[None],
        grad_down[None],
    )


def solution(mesh):
    return jax.shard_map(
        per_device,
        mesh=mesh,
        in_specs=(
            P("expert", "dp"),
            P("expert", "dp"),
            P("expert", None),
            P("expert", None),
            P("expert", None, "dp"),
            P("expert", None, "dp"),
            P("expert", "dp", None),
        ),
        out_specs=(
            P("expert", "dp"),
            P("expert", "dp"),
            P("expert", None, "dp"),
            P("expert", None, "dp"),
            P("expert", "dp", None),
        ),
        check_vma=False,
    )
```

profile of v0, /device:TPU:1, one launch (start us, length us, event | category | flops | bytes accessed | tf_op | source)
XLA Modules:
  0.0 220.8 jit_solution(11814088893083296864)
XLA Ops:
  7.2 0.8 broadcast_multiply_fusion
  8.0 0.8 copy.12
  9.2 0.9 reduce-window.6
  10.2 0.2 slice_reduce_fusion
  10.6 2.9 %scatter_custom_fusion = s32[448]{0:T(512)S(1)} fusion(s32[320]{0:T(512)S(1)} %fusion.23, s32[320]{0:T(512)S(1)} %iota.8, s32[]{:T(128)} %constant.45.clone.1), kind=kCustom, calls=%fused_computation.72 | custom fusion | bytes 1796 | tf_op jit(solution)/shard_map/scatter | solution.py:50
  13.5 0.8 copy.16
  14.5 3.2 %gather_fusion = f32[448]{0:T(512)S(1)} fusion(f32[320]{0:T(512)S(1)} %reshape.84, s32[1024]{0:T(1024)S(1)} %pad_clamp_fusion.1), kind=kCustom, calls=%fused_computation.4 | custom fusion | bytes 5376 | tf_op jit(solution)/shard_map/jit(_take)/gather | solution.py:62
  17.7 2.1 gather_fusion.2
  19.8 2.1 gather_fusion.1
  22.5 39.2 %all_to_all.24 = bf16[64,7,512]{2,1,0:T(8,128)(2,1)S(1)} all-to-all(bf16[64,7,512]{2,1,0:T(8,128)(2,1)S(1)} %all_to_all.16), channel_id=1, replica_groups=mesh['dp'=8,'expert'=64] {'expert'}, dimensions={0} | all-to-all | bytes 917504 | tf_op jit(solution)/shard_map/all_to_all | solution.py:10
  61.9 0.8 pad_maximum_fusion.2
  62.8 50.0 %all-gather.2.cloned.1.call-done = bf16[896,2048]{1,0:T(8,128)(2,1)} async-done(((bf16[896,256]{1,0:T(8,128)(2,1)}), bf16[896,2048]{1,0:T(8,128)(2,1)}) %all-gather.2.cloned.1.call-update) | async-done | bytes 3670032 | tf_op jit(solution)/shard_map/all_gather | solution.py:22
  112.8 2.3 %fusion.4 = f32[448,128]{1,0:T(8,128)S(1)} fusion(bf16[896,2048]{1,0:T(8,128)(2,1)} %all-gather.2.cloned.1.call-done, bf16[1,128,2048]{2,1,0:T(8,128)(2,1)S(1)} %copy-done.5), kind=kOutput, calls=%fused_computation.16 | convolution fusion | flops 234881024 | bytes 2588672 | tf_op jit(solution)/shard_map/dot_general | solution.py:85
  115.2 2.1 fusion.10
  117.3 0.7 multiply_convert_fusion.3
  118.0 0.6 convolution_convert_fusion
  118.6 0.6 fusion.16
  119.3 0.7 add_convert_fusion
  119.9 2.3 %pad_maximum_fusion = bf16[896,2048]{1,0:T(8,128)(2,1)} fusion(bf16[448,2048]{1,0:T(8,128)(2,1)S(1)} %add_convert_fusion, bf16[448,2048]{1,0:T(8,128)(2,1)S(1)} %convolution_convert_fusion), kind=kLoop, calls=%fused_computation.6 | loop fusion | flops 7340032 | bytes 7340032 | tf_op jit(solution)/shard_map/concatenate | solution.py:30
  122.2 48.6 %reduce-scatter.2.cloned.1.call-done = bf16[896,256]{1,0:T(8,128)(2,1)} async-done(((bf16[896,2048]{1,0:T(8,128)(2,1)}), bf16[896,256]{1,0:T(8,128)(2,1)}) %reduce-scatter.2.cloned.1.call-update) | async-done | bytes 458768 | tf_op jit(solution)/shard_map/reduce_scatter | solution.py:31
  170.8 1.1 fusion.26
  171.9 1.0 all_to_all.19
  172.9 15.5 %all-to-all-start.1 = ((bf16[64,7,512]{2,1,0:T(8,128)(2,1)}), bf16[64,7,512]{2,1,0:T(8,128)(2,1)S(1)}, u32[]{:S(2)}, u32[]{:S(2)}) async-start(bf16[64,7,512]{2,1,0:T(8,128)(2,1)} %all_to_all.19), calls=%async_computation.2 | async-start | bytes 1048576 | tf_op jit(solution)/shard_map/all_to_all | solution.py:10
  188.5 2.9 %fusion.2 = bf16[1,128,2048]{2,1,0:T(8,128)(2,1)} fusion(bf16[448,128]{1,0:T(8,128)(2,1)S(1)} %get-tuple-element.17, bf16[896,2048]{1,0:T(8,128)(2,1)} %all-gather.2.cloned.1.call-done), kind=kOutput, calls=%fused_computation.14 | convolution fusion | flops 235143168 | bytes 2473984 | tf_op jit(solution)/shard_map/dot_general | solution.py:99
  191.4 3.1 %fusion = bf16[1,2048,128]{2,1,0:T(8,128)(2,1)} fusion(bf16[448,128]{1,0:T(8,128)(2,1)S(1)} %get-tuple-element.18, bf16[896,2048]{1,0:T(8,128)(2,1)} %all-gather.2.cloned.1.call-done), kind=kOutput, calls=%fused_computation.12 | convolution fusion | flops 235143168 | bytes 2473984 | tf_op jit(solution)/shard_map/dot_general | solution.py:102
  194.5 1.6 fusion.1
  196.1 11.7 %all-to-all-done.1 = bf16[64,7,512]{2,1,0:T(8,128)(2,1)S(1)} async-done(((bf16[64,7,512]{2,1,0:T(8,128)(2,1)}), bf16[64,7,512]{2,1,0:T(8,128)(2,1)S(1)}, u32[]{:S(2)}, u32[]{:S(2)}) %all-to-all-start.1) | async-done | bytes 458784 | tf_op jit(solution)/shard_map/all_to_all | solution.py:10
  208.0 1.6 gather_fusion.4
  209.7 1.6 gather_fusion.3
  211.4 0.2 reshape.86
  211.8 1.0 reduce_sum.32
  212.9 1.0 reduce_sum.31
  (47 shorter events, 2.3 us)
Async XLA Ops:
  7.2 110.1 %copy-start = (bf16[1,2048,128]{2,1,0:T(8,128)(2,1)S(1)}, bf16[1,2048,128]{2,1,0:T(8,128)(2,1)}, u32[]{:S(2)}) copy-start(bf16[1,2048,128]{2,1,0:T(8,128)(2,1)} %param.16) | copy-start | bytes 1572868
  7.2 10.5 %copy-start.1 = (bf16[160,256]{1,0:T(8,128)(2,1)S(1)}, bf16[160,256]{1,0:T(8,128)(2,1)}, u32[]{:S(2)}) copy-start(bf16[160,256]{1,0:T(8,128)(2,1)} %param.12) | copy-start | bytes 245764
  7.2 12.6 %copy-start.2 = (bf16[160,256]{1,0:T(8,128)(2,1)S(1)}, bf16[160,256]{1,0:T(8,128)(2,1)}, u32[]{:S(2)}) copy-start(bf16[160,256]{1,0:T(8,128)(2,1)} %param.11) | copy-start | bytes 245764
  7.2 105.6 %all-gather.2.cloned.1.call-start = ((), (), s32[]{:S(2)}) async-start(), calls=%async_computation.3 | async-start | bytes 4128768 | tf_op jit(solution)/shard_map/all_gather | solution.py:22
  21.9 90.9 %copy-start.5 = (bf16[1,128,2048]{2,1,0:T(8,128)(2,1)S(1)}, bf16[1,128,2048]{2,1,0:T(8,128)(2,1)}, u32[]{:S(2)}) copy-start(bf16[1,128,2048]{2,1,0:T(8,128)(2,1)} %param.17) | copy-start | bytes 1572868
  22.5 92.6 %copy-start.6 = (bf16[1,2048,128]{2,1,0:T(8,128)(2,1)S(1)}, bf16[1,2048,128]{2,1,0:T(8,128)(2,1)}, u32[]{:S(2)}) copy-start(bf16[1,2048,128]{2,1,0:T(8,128)(2,1)} %param.15) | copy-start | bytes 1572868
  62.8 108.1 %reduce-scatter.2.cloned.1.call-start = ((), (), s32[]{:S(2)}) async-start(), calls=%async_computation.4 | async-start | bytes 4128768 | tf_op jit(solution)/shard_map/reduce_scatter | solution.py:31
  112.8 4.5 %copy-start.3 = (bf16[896,2048]{1,0:T(8,128)(2,1)S(1)}, bf16[896,2048]{1,0:T(8,128)(2,1)}, u32[]{:S(2)}) copy-start(bf16[896,2048]{1,0:T(8,128)(2,1)} %all-gather.2.cloned.1.call-done) | copy-start | bytes 11010052
  172.9 34.9 %all-to-all-start.1 = ((bf16[64,7,512]{2,1,0:T(8,128)(2,1)}), bf16[64,7,512]{2,1,0:T(8,128)(2,1)S(1)}, u32[]{:S(2)}, u32[]{:S(2)}) async-start(bf16[64,7,512]{2,1,0:T(8,128)(2,1)} %all_to_all.19), calls=%async_computation.2 | async-start | bytes 1048576 | tf_op jit(solution)/shard_map/all_to_all | solution.py:10
  188.4 6.1 %copy-start.4 = (bf16[896,2048]{1,0:T(8,128)(2,1)S(1)}, bf16[896,2048]{1,0:T(8,128)(2,1)}, u32[]{:S(2)}) copy-start(bf16[896,2048]{1,0:T(8,128)(2,1)} %all-gather.2.cloned.1.call-done) | copy-start | bytes 11010052
Sparse Core Ops, SparseCore 0:
  62.9 49.9 all-gather.1
  122.3 48.4 reduce-scatter.1
where the time goes:
time: 222 us; the launch traced here: 221 us
  waiting for transfers between devices  110 us (50%)
  blocking collectives  39.2 us (18%)
  local copies, waits for them, and re-layouts  18.8 us (8%)
  starting transfers between devices  15.6 us (7%)
  matrix products  14.6 us (7%)
  between operations  14.4 us (6%)
  other arithmetic  7.74 us (3%)
    all_gather x1, waiting for transfers between devices, in_one_piece_2(): lax.all_gather(both, axis, axis=dim, tiled=True)  50 us
    reduce_scatter x1, waiting for transfers between devices, in_one_piece_3(): lax.psum_scatter(both, axis, scatter_dimension=dim, tiled=True)  48.6 us
    all_to_all x1, blocking collectives, in_one_piece(): lax.all_to_all(both, axis, split_axis=split_dim, concat_axis=concat_dim,...  39.2 us
    all_to_all x1, starting transfers between devices, in_one_piece(): lax.all_to_all(both, axis, split_axis=split_dim, concat_axis=concat_dim,...  15.5 us
    all_to_all x1, waiting for transfers between devices, in_one_piece(): lax.all_to_all(both, axis, split_axis=split_dim, concat_axis=concat_dim,...  11.7 us
  transfers between devices with their start and end apart: 3, of which 3 were waited for; matrix products, arithmetic and copies ran while one was open for 3% of the time, Pallas kernels for 0%

commit v1 on v0

v1 whole, which is shorter than its diff:
```python
import functools

import jax
import jax.numpy as jnp
from jax import lax
from jax.experimental import pallas as pl
from jax.experimental.pallas import tpu as pltpu
from jax.sharding import PartitionSpec as P

BF16, F32, I32 = jnp.bfloat16, jnp.float32, jnp.int32
PAD = 8


def dot(a, b, ca=1, cb=0):
    return lax.dot_general(a, b, (((ca,), (cb,)), ((), ())), preferred_element_type=F32)


def call(body, outs, args, flops, in_specs=None):
    moved = sum(a.size * a.dtype.itemsize for a in args)
    moved += sum(o.size * o.dtype.itemsize for o in outs)
    vmem = pl.BlockSpec(memory_space=pltpu.VMEM)
    return pl.pallas_call(
        body,
        out_shape=outs,
        in_specs=in_specs or [vmem] * len(args),
        out_specs=[vmem] * len(outs),
        cost_estimate=pl.CostEstimate(flops=flops, bytes_accessed=moved, transcendentals=0),
    )(*args)


def iota(shape, dim):
    return lax.broadcasted_iota(I32, shape, dim)


def route_body(experts, capacity, ids_ref, probs_ref, tok_ref, grad_ref, out_ref, pos_ref):
    ids, probs = ids_ref[...], probs_ref[...]
    rows = ids.shape[1]
    width = tok_ref.shape[1]
    named = [iota((experts, rows), 0) == ids[k : k + 1, :] for k in range(2)]
    both = (named[0].astype(F32) + named[1].astype(F32)).astype(BF16)
    earlier = (iota((rows, rows), 0) < iota((rows, rows), 1)).astype(F32).astype(BF16)
    before = dot(both, earlier)
    place = iota((experts * PAD, rows), 0)
    here = []
    for k in range(2):
        slot = jnp.sum(jnp.where(named[k], before, 0.0), axis=0, keepdims=True).astype(I32)
        pos_ref[k : k + 1, :] = ids[k : k + 1, :] * capacity + slot
        here.append(place == ids[k : k + 1, :] * PAD + slot)
    picks = (here[0] | here[1]).astype(F32).astype(BF16)
    factor = jnp.sum(
        jnp.where(here[0], probs[0:1, :], jnp.where(here[1], probs[1:2, :], 0.0)),
        axis=1,
        keepdims=True,
    )
    out_ref[:, :width] = dot(picks, tok_ref[...]).astype(BF16)
    out_ref[:, width:] = (dot(picks, grad_ref[...]) * factor).astype(BF16)


def combine_body(pos_ref, probs_ref, back_ref, out_ref, grad_ref):
    pos, probs = pos_ref[...], probs_ref[...]
    rows = pos.shape[1]
    width = out_ref.shape[1]
    returned = back_ref[...]
    place = iota((returned.shape[0], rows), 0)
    rows_of = [
        dot((place == pos[k : k + 1, :]).astype(F32).astype(BF16), returned, 0, 0)
        for k in range(2)
    ]
    out_ref[...] = (
        rows_of[0][:, :width] * probs[:, 0:1] + rows_of[1][:, :width] * probs[:, 1:2]
    ).astype(BF16)
    grad_ref[...] = (rows_of[0][:, width:] + rows_of[1][:, width:]).astype(BF16)


def block_of(me_ref, mask, width):
    return pl.ds(pl.multiple_of((me_ref[0] ^ mask) * width, width), width)


def partial_pre(me_ref, mask, x, gate_ref, up_ref, down_ref):
    width = x.shape[1] // 2
    at = block_of(me_ref, mask, width)
    both = jnp.concatenate([gate_ref[at, :], up_ref[at, :]], axis=1)
    return dot(x[:, :width], both), dot(x[:, width:], down_ref[:, at], 1, 1)


def first_body(masks, me_ref, *refs):
    xs, (gate_ref, up_ref, down_ref, pre_ref, hid_ref) = refs[: len(masks)], refs[len(masks) :]
    pre, hid = 0.0, 0.0
    for mask, x_ref in zip(masks, xs):
        a, b = partial_pre(me_ref, mask, x_ref[...], gate_ref, up_ref, down_ref)
        pre, hid = pre + a, hid + b
    pre_ref[...] = pre
    hid_ref[...] = hid


def shares(me_ref, mask, width, hidden, pre_grads, gate_ref, up_ref, down_ref, out_ref, row):
    at = block_of(me_ref, mask, width)
    rows = pl.ds(row, hidden.shape[0])
    out_ref[rows, :width] = dot(hidden, down_ref[:, at]).astype(BF16)
    both = jnp.concatenate([gate_ref[at, :], up_ref[at, :]], axis=1)
    out_ref[rows, width:] = dot(pre_grads, both, 1, 1).astype(BF16)


def second_body(masks, me_ref, *refs):
    xs, rest = refs[: len(masks)], refs[len(masks) :]
    pre_ref, hid_ref, gate_ref, up_ref, down_ref, h_ref, g_ref, near_ref, far_ref = rest
    pre, hid = pre_ref[...], hid_ref[...]
    for mask, x_ref in zip(masks, xs):
        a, b = partial_pre(me_ref, mask, x_ref[...], gate_ref, up_ref, down_ref)
        pre, hid = pre + a, hid + b
    units = hid.shape[1]
    gate, up = pre[:, :units], pre[:, units:]
    sig = jax.nn.sigmoid(gate)
    silu = gate * sig
    hidden = (silu * up).astype(BF16)
    gate_grad = (hid * up * sig * (1.0 + gate * (1.0 - sig))).astype(BF16)
    up_grad = (hid * silu).astype(BF16)
    grads = jnp.concatenate([gate_grad, up_grad], axis=1)
    h_ref[...] = hidden
    g_ref[...] = grads
    width = near_ref.shape[1] // 2
    n = hidden.shape[0]
    shares(me_ref, 5, width, hidden, grads, gate_ref, up_ref, down_ref, near_ref, 0)
    for i, mask in enumerate((7, 3, 1)):
        shares(me_ref, mask, width, hidden, grads, gate_ref, up_ref, down_ref, far_ref, i * n)


def third_body(me_ref, h_ref, g_ref, gate_ref, up_ref, down_ref, own_ref):
    width = own_ref.shape[1] // 2
    hidden, grads = h_ref[...], g_ref[...]
    n = hidden.shape[0]
    for i, mask in enumerate((4, 6, 2, 0)):
        shares(me_ref, mask, width, hidden, grads, gate_ref, up_ref, down_ref, own_ref, i * n)


def weight_grads_body(masks, me_ref, *refs):
    xs, (h_ref, g_ref, gate_out, up_out, down_out) = refs[: len(masks)], refs[len(masks) :]
    hidden, grads = h_ref[...], g_ref[...]
    units = hidden.shape[1]
    for mask, x_ref in zip(masks, xs):
        x = x_ref[...]
        width = x.shape[1] // 2
        at = block_of(me_ref, mask, width)
        both = dot(x[:, :width], grads, 0, 0)
        gate_out[at, :] = both[:, :units].astype(BF16)
        up_out[at, :] = both[:, units:].astype(BF16)
        down_out[:, at] = dot(hidden, x[:, width:], 0, 0).astype(BF16)


def per_device(tokens, grad_out, expert_ids, gate_probs, gate_weight, up_weight, down_weight):
    experts, parts = lax.axis_size("expert"), lax.axis_size("dp")
    rows, width = tokens.shape
    capacity = max(2, 3 * rows // experts)
    n = experts * capacity
    gate, up, down = gate_weight[0], up_weight[0], down_weight[0]
    units, model = down.shape
    me = lax.axis_index("dp").astype(I32).reshape(1)
    sds = jax.ShapeDtypeStruct

    def swap(x, mask):
        return lax.ppermute(x, "dp", [(j, j ^ mask) for j in range(parts)])

    smem, vmem = pl.BlockSpec(memory_space=pltpu.SMEM), pl.BlockSpec(memory_space=pltpu.VMEM)

    send, pos = call(
        functools.partial(route_body, experts, capacity),
        [sds((experts * PAD, 2 * width), BF16), sds((2, rows), I32)],
        [expert_ids.T, gate_probs.T, tokens, grad_out],
        4 * experts * PAD * rows * width,
    )
    filled = lax.all_to_all(
        send.reshape(experts, PAD, 2 * width), "expert", split_axis=0, concat_axis=0, tiled=True
    )
    x = {0: filled[:, :capacity].reshape(n, 2 * width)}
    x[6] = swap(x[0], 6)
    x[2] = swap(x[0], 2)
    x[1] = swap(x[0], 1)
    x[4] = swap(x[6], 2)
    x[7] = swap(x[6], 1)
    x[3] = swap(x[2], 1)
    x[5] = swap(x[4], 1)

    weights = [gate, up, down]
    early, late = (0, 1, 2, 3, 6, 7), (4, 5)
    per_mask = 6 * n * width * units
    pre, hid = call(
        functools.partial(first_body, early),
        [sds((n, 2 * units), F32), sds((n, units), F32)],
        [me, *[x[m] for m in early], *weights],
        len(early) * per_mask,
        [smem] + [vmem] * (len(early) + 3),
    )
    hidden, grads, near, far = call(
        functools.partial(second_body, late),
        [
            sds((n, units), BF16),
            sds((n, 2 * units), BF16),
            sds((n, 2 * width), BF16),
            sds((3 * n, 2 * width), BF16),
        ],
        [me, *[x[m] for m in late], pre, hid, *weights],
        (len(late) + 4) * per_mask,
        [smem] + [vmem] * (len(late) + 5),
    )
    near_in = swap(near, 1)
    far_in = swap(far, 1)
    (own,) = call(
        third_body,
        [sds((4 * n, 2 * width), BF16)],
        [me, hidden, grads, *weights],
        4 * per_mask,
        [smem] + [vmem] * 5,
    )

    def own_of(i):
        return own[i * n : (i + 1) * n].astype(F32)

    def far_of(i):
        return far_in[i * n : (i + 1) * n].astype(F32)

    across = swap((own_of(0) + near_in.astype(F32)).astype(BF16), 2)
    side = swap((own_of(2) + far_of(1)).astype(BF16), 2)
    over = swap((own_of(1) + far_of(0) + across.astype(F32)).astype(BF16), 6)
    total = own_of(3) + far_of(2) + side.astype(F32) + over.astype(F32)

    gate_grad, up_grad, down_grad = call(
        functools.partial(weight_grads_body, tuple(range(parts))),
        [sds((model, units), BF16), sds((model, units), BF16), sds((units, model), BF16)],
        [me, *[x[m] for m in range(parts)], hidden, grads],
        parts * per_mask,
        [smem] + [vmem] * (parts + 2),
    )

    returned = lax.all_to_all(
        total.astype(BF16).reshape(experts, capacity, 2 * width),
        "expert",
        split_axis=0,
        concat_axis=0,
        tiled=True,
    ).reshape(n, 2 * width)
    layer_out, grad_tokens = call(
        combine_body,
        [sds((rows, width), BF16), sds((rows, width), BF16)],
        [pos, gate_probs, returned],
        8 * n * rows * width,
    )
    return layer_out, grad_tokens, gate_grad[None], up_grad[None], down_grad[None]


def solution(mesh):
    return jax.shard_map(
        per_device,
        mesh=mesh,
        in_specs=(
            P("expert", "dp"),
            P("expert", "dp"),
            P("expert", None),
            P("expert", None),
            P("expert", None, "dp"),
            P("expert", None, "dp"),
            P("expert", "dp", None),
        ),
        out_specs=(
            P("expert", "dp"),
            P("expert", "dp"),
            P("expert", None, "dp"),
            P("expert", None, "dp"),
            P("expert", "dp", None),
        ),
        check_vma=False,
    )
```

time: 222 us -> 175 us (0.79)
  waiting for transfers between devices: 110 us -> 54 us
  starting transfers between devices: 15.6 us -> 52.3 us
  Pallas kernels: 0 us -> 19.9 us
  local copies, waits for them, and re-layouts: 18.8 us -> 3.85 us
  matrix products: 14.6 us -> 0 us
  between operations: 14.4 us -> 0.88 us
  other arithmetic: 7.74 us -> 3.86 us
    all_gather x1 -> x0, waiting for transfers between devices: 50 us -> none  [in_one_piece_2(): lax.all_gather(both, axis, axis=dim, tiled=True)]
    reduce_scatter x1 -> x0, waiting for transfers between devices: 48.6 us -> none  [in_one_piece_3(): lax.psum_scatter(both, axis, scatter_dimension=dim, tiled=True)]
    ppermute x0 -> x12, starting transfers between devices: none -> 44.9 us  [swap(): return lax.ppermute(x, 'dp', [(j, j ^ mask) for j in range(parts)])]
    ppermute x0 -> x12, waiting for transfers between devices: none -> 39.3 us  [swap(): return lax.ppermute(x, 'dp', [(j, j ^ mask) for j in range(parts)])]
    pallas_call x0 -> x6, Pallas kernels: none -> 19.9 us  [call(): pl.pallas_call(body, out_shape=outs, in_specs=in_specs or [vmem] * len(ar...]
    dot_general x9 -> x0, matrix products: 14.6 us -> none  [the longest x1 3.09 us: expert_work(): lax.dot_general(routed, grad_gate_pre, contract_first, preferred_element_...]
    gather x5 -> x0, local copies, waits for them, and re-layouts: 10.6 us -> none  [the longest x2 3.26 us: combine_rows(): taken = jnp.take(returned, position, axis=0)]
    all_to_all x1, starting transfers between devices: 15.5 us -> 7.45 us  [per_device(): lax.all_to_all(total.astype(BF16).reshape(experts, capacity, 2 * width),...]
  transfers between devices with their start and end apart: 3 -> 13, of which waited for: 3 -> 6; matrix products, arithmetic and copies ran while one was open for 3% -> 1% of each run, Pallas kernels for 0% -> 7%
where the time goes in v1:
time: 175 us; the launch traced here: 174 us
  waiting for transfers between devices  54 us (31%)
  starting transfers between devices  52.3 us (30%)
  blocking collectives  39.3 us (22%)
  Pallas kernels  19.9 us (11%)
  other arithmetic  3.86 us (2%)
  local copies, waits for them, and re-layouts  3.85 us (2%)
    ppermute x12, starting transfers between devices, swap(): return lax.ppermute(x, 'dp', [(j, j ^ mask) for j in range(parts)])  44.9 us
    ppermute x12, waiting for transfers between devices, swap(): return lax.ppermute(x, 'dp', [(j, j ^ mask) for j in range(parts)])  39.3 us
    all_to_all x1, blocking collectives, per_device(): lax.all_to_all(send.reshape(experts, PAD, 2 * width), 'expert', split_axi...  39.3 us
    pallas_call x6, Pallas kernels, call(): pl.pallas_call(body, out_shape=outs, in_specs=in_specs or [vmem] * len(ar...  19.9 us
    all_to_all x1, waiting for transfers between devices, per_device(): lax.all_to_all(total.astype(BF16).reshape(experts, capacity, 2 * width),...  14.7 us
    all_to_all x1, starting transfers between devices, per_device(): lax.all_to_all(total.astype(BF16).reshape(experts, capacity, 2 * width),...  7.45 us
  transfers between devices with their start and end apart: 13, of which 6 were waited for; matrix products, arithmetic and copies ran while one was open for 1% of the time, Pallas kernels for 7%

profile of v1, /device:TPU:1, one launch (start us, length us, event | category | flops | bytes accessed | tf_op | source)
XLA Modules:
  0.0 174.1 jit_solution(4912361769147249467)
XLA Ops:
  0.6 2.3 %shard_map.110 = (bf16[512,512]{1,0:T(8,128)(2,1)}, s32[2,160]{1,0:T(2,128)}) custom-call(s32[2,160]{1,0:T(2,128)} %bitcast.26, f32[2,160]{1,0:T(2,128)} %bitcast.22, bf16[160,256]{1,0:T(8,128)(2,1)} %tok_ref.1, bf16[160,256]{1,0:T(8,128)(2,1)} %grad_ref.1), custom_call_target="tpu_custom_call" | custom-call | flops 83886080 | bytes 691968 | tf_op jit(solution)/shard_map/pallas_call | solution.py:22
  2.9 39.3 %all_to_all.10 = bf16[64,8,512]{2,1,0:T(8,128)(2,1)S(1)} all-to-all(bf16[64,8,512]{2,1,0:T(8,128)(2,1)} %bitcast.21), channel_id=1, replica_groups=mesh['dp'=8,'expert'=64] {'expert'}, dimensions={0} | all-to-all | bytes 1048576 | tf_op jit(solution)/shard_map/all_to_all | solution.py:171
  42.3 4.9 %collective-permute-start = (bf16[448,512]{1,0:T(8,128)(2,1)S(1)}, bf16[448,512]{1,0:T(8,128)(2,1)S(1)}, u32[]{:S(2)}, u32[]{:S(2)}) collective-permute-start(bf16[448,512]{1,0:T(8,128)(2,1)S(1)} %reshape.27.refs_0_), channel_id=1, source_target_pairs={{0,384},{64,448},{128,256},{192,320},{256,128},{320,192},{384,0},{... | collective-permute-start | bytes 1376264 | tf_op jit(solution)/shard_map/ppermute | solution.py:161
  47.3 1.9 %collective-permute-start.4 = (bf16[448,512]{1,0:T(8,128)(2,1)S(1)}, bf16[448,512]{1,0:T(8,128)(2,1)S(1)}, u32[]{:S(2)}, u32[]{:S(2)}) collective-permute-start(bf16[448,512]{1,0:T(8,128)(2,1)S(1)} %reshape.27.refs_0_), channel_id=1, source_target_pairs={{0,128},{64,192},{128,0},{192,64},{256,384},{320,448},{384,256},{4... | collective-permute-start | bytes 1376264 | tf_op jit(solution)/shard_map/ppermute | solution.py:161
  49.2 6.3 %collective-permute-done.refs_4_.refs_6_ = bf16[448,512]{1,0:T(8,128)(2,1)S(1)} collective-permute-done((bf16[448,512]{1,0:T(8,128)(2,1)S(1)}, bf16[448,512]{1,0:T(8,128)(2,1)S(1)}, u32[]{:S(2)}, u32[]{:S(2)}) %collective-permute-start) | collective-permute-done | bytes 458784 | tf_op jit(solution)/shard_map/ppermute | solution.py:161
  55.5 13.4 %collective-permute-start.1 = (bf16[448,512]{1,0:T(8,128)(2,1)S(1)}, bf16[448,512]{1,0:T(8,128)(2,1)S(1)}, u32[]{:S(2)}, u32[]{:S(2)}) collective-permute-start(bf16[448,512]{1,0:T(8,128)(2,1)S(1)} %collective-permute-done.refs_4_.refs_6_), channel_id=1, source_target_pairs={{0,128},{64,192},{128,0},{192,64},{256,384},{320,448},{384,256},{4... | collective-permute-start | bytes 1376264 | tf_op jit(solution)/shard_map/ppermute | solution.py:161
  68.9 3.5 %collective-permute-start.3 = (bf16[448,512]{1,0:T(8,128)(2,1)S(1)}, bf16[448,512]{1,0:T(8,128)(2,1)S(1)}, u32[]{:S(2)}, u32[]{:S(2)}) collective-permute-start(bf16[448,512]{1,0:T(8,128)(2,1)S(1)} %reshape.27.refs_0_), channel_id=1, source_target_pairs={{0,64},{64,0},{128,192},{192,128},{256,320},{320,256},{384,448},{4... | collective-permute-start | bytes 1376264 | tf_op jit(solution)/shard_map/ppermute | solution.py:161
  72.4 1.9 %collective-permute-start.6 = (bf16[448,512]{1,0:T(8,128)(2,1)S(1)}, bf16[448,512]{1,0:T(8,128)(2,1)S(1)}, u32[]{:S(2)}, u32[]{:S(2)}) collective-permute-start(bf16[448,512]{1,0:T(8,128)(2,1)S(1)} %collective-permute-done.refs_4_.refs_6_), channel_id=1, source_target_pairs={{0,64},{64,0},{128,192},{192,128},{256,320},{320,256},{384,448},{4... | collective-permute-start | bytes 1376264 | tf_op jit(solution)/shard_map/ppermute | solution.py:161
  74.3 2.4 %collective-permute-start.5 = (bf16[448,512]{1,0:T(8,128)(2,1)S(1)}, bf16[448,512]{1,0:T(8,128)(2,1)S(1)}, u32[]{:S(2)}, u32[]{:S(2)}) collective-permute-start(bf16[448,512]{1,0:T(8,128)(2,1)S(1)} %collective-permute-done.4.refs_2_), channel_id=1, source_target_pairs={{0,64},{64,0},{128,192},{192,128},{256,320},{320,256},{384,448},{4... | collective-permute-start | bytes 1376264 | tf_op jit(solution)/shard_map/ppermute | solution.py:161
  76.7 1.7 collective-permute-done.1.refs_0_.refs_4_
  78.5 3.8 %collective-permute-start.2 = (bf16[448,512]{1,0:T(8,128)(2,1)S(1)}, bf16[448,512]{1,0:T(8,128)(2,1)}, u32[]{:S(2)}, u32[]{:S(2)}) collective-permute-start(bf16[448,512]{1,0:T(8,128)(2,1)S(1)} %collective-permute-done.1.refs_0_.refs_4_), channel_id=1, source_target_pairs={{0,64},{64,0},{128,192},{192,128},{256,320},{320,256},{384,448},{4... | collective-permute-start | bytes 1376264 | tf_op jit(solution)/shard_map/ppermute | solution.py:161
  83.4 3.9 %shard_map.111 = (f32[448,256]{1,0:T(8,128)}, f32[448,128]{1,0:T(8,128)}) custom-call(s32[1]{0:T(128)} %bitcast.2.me_ref, bf16[448,512]{1,0:T(8,128)(2,1)} %copy-done, bf16[448,512]{1,0:T(8,128)(2,1)} %copy-done.3, bf16[448,512]{1,0:T(8,128)(2,1)} %copy-done.2, bf16[448,512]{1,0:T(8,128)(2,1)} %copy-done.5, bf16[448,512]{1,0:T(8,128)(2,1)} %copy-done.1, ...), custom_call_target="tpu_custom_call" | custom-call | flops 528482304 | bytes 5013508 | tf_op jit(solution)/shard_map/pallas_call | solution.py:22
  87.3 3.9 %shard_map.112 = (bf16[448,128]{1,0:T(8,128)(2,1)}, bf16[448,256]{1,0:T(8,128)(2,1)}, bf16[448,512]{1,0:T(8,128)(2,1)}, bf16[1344,512]{1,0:T(8,128)(2,1)}) custom-call(s32[1]{0:T(128)} %bitcast.2.me_ref, bf16[448,512]{1,0:T(8,128)(2,1)} %copy-done.6, bf16[448,512]{1,0:T(8,128)(2,1)} %collective-permute-done.2.refs_1_.refs_5_, ...), custom_call_target="tpu_custom_call" | custom-call | flops 528482304 | bytes 5357572 | tf_op jit(solution)/shard_map/pallas_call | solution.py:22
  91.2 1.9 %collective-permute-start.7 = (bf16[1344,512]{1,0:T(8,128)(2,1)}, bf16[1344,512]{1,0:T(8,128)(2,1)S(1)}, u32[]{:S(2)}, u32[]{:S(2)}) collective-permute-start(bf16[1344,512]{1,0:T(8,128)(2,1)} %get-tuple-element.24), channel_id=1, source_target_pairs={{0,64},{64,0},{128,192},{192,128},{256,320},{320,256},{384,448},{4... | collective-permute-start | bytes 4128776 | tf_op jit(solution)/shard_map/ppermute | solution.py:161
  93.1 2.4 %collective-permute-start.9 = (bf16[448,512]{1,0:T(8,128)(2,1)}, bf16[448,512]{1,0:T(8,128)(2,1)S(1)}, u32[]{:S(2)}, u32[]{:S(2)}) collective-permute-start(bf16[448,512]{1,0:T(8,128)(2,1)} %get-tuple-element.25), channel_id=1, source_target_pairs={{0,64},{64,0},{128,192},{192,128},{256,320},{320,256},{384,448},{4... | collective-permute-start | bytes 1376264 | tf_op jit(solution)/shard_map/ppermute | solution.py:161
  95.5 3.4 %shard_map.113 = bf16[1792,512]{1,0:T(8,128)(2,1)} custom-call(s32[1]{0:T(128)} %bitcast.2.me_ref, bf16[448,128]{1,0:T(8,128)(2,1)} %get-tuple-element.22.h_ref.refs_8_, bf16[448,256]{1,0:T(8,128)(2,1)} %get-tuple-element.23.g_ref.refs_9_, bf16[2048,128]{1,0:T(8,128)(2,1)} %bitcast.13, bf16[2048,128]{1,0:T(8,128)(2,1)} %bitcast.16, bf16[128,2048]{1,0:T(8,128)(2,1)} %bitcast.19), custom_call_target="tpu_custom_call" | custom-call | flops 352321536 | bytes 3751940 | tf_op jit(solution)/shard_map/pallas_call | solution.py:22
  98.9 1.1 add_convert_fusion.2
  100.1 3.4 %collective-permute-start.10 = (bf16[448,512]{1,0:T(8,128)(2,1)S(1)}, bf16[448,512]{1,0:T(8,128)(2,1)S(1)}, u32[]{:S(2)}, u32[]{:S(2)}) collective-permute-start(bf16[448,512]{1,0:T(8,128)(2,1)S(1)} %add_convert_fusion.2), channel_id=1, source_target_pairs={{0,128},{64,192},{128,0},{192,64},{256,384},{320,448},{384,256},{4... | collective-permute-start | bytes 1376264 | tf_op jit(solution)/shard_map/ppermute | solution.py:161
  103.4 10.6 %collective-permute-done.10 = bf16[448,512]{1,0:T(8,128)(2,1)S(1)} collective-permute-done((bf16[448,512]{1,0:T(8,128)(2,1)S(1)}, bf16[448,512]{1,0:T(8,128)(2,1)S(1)}, u32[]{:S(2)}, u32[]{:S(2)}) %collective-permute-start.10) | collective-permute-done | bytes 458784 | tf_op jit(solution)/shard_map/ppermute | solution.py:161
  114.0 1.5 add_convert_fusion.3
  115.5 3.3 %collective-permute-start.11 = (bf16[448,512]{1,0:T(8,128)(2,1)S(1)}, bf16[448,512]{1,0:T(8,128)(2,1)S(1)}, u32[]{:S(2)}, u32[]{:S(2)}) collective-permute-start(bf16[448,512]{1,0:T(8,128)(2,1)S(1)} %get-tuple-element.32), channel_id=1, source_target_pairs={{0,384},{64,448},{128,256},{192,320},{256,128},{320,192},{384,0},{... | collective-permute-start | bytes 1376264 | tf_op jit(solution)/shard_map/ppermute | solution.py:161
  118.8 2.1 %collective-permute-start.8 = (bf16[448,512]{1,0:T(8,128)(2,1)S(1)}, bf16[448,512]{1,0:T(8,128)(2,1)S(1)}, u32[]{:S(2)}, u32[]{:S(2)}) collective-permute-start(bf16[448,512]{1,0:T(8,128)(2,1)S(1)} %get-tuple-element.31), channel_id=1, source_target_pairs={{0,128},{64,192},{128,0},{192,64},{256,384},{320,448},{384,256},{4... | collective-permute-start | bytes 1376264 | tf_op jit(solution)/shard_map/ppermute | solution.py:161
  120.9 9.7 %collective-permute-done.11 = bf16[448,512]{1,0:T(8,128)(2,1)S(1)} collective-permute-done((bf16[448,512]{1,0:T(8,128)(2,1)S(1)}, bf16[448,512]{1,0:T(8,128)(2,1)S(1)}, u32[]{:S(2)}, u32[]{:S(2)}) %collective-permute-start.11) | collective-permute-done | bytes 458784 | tf_op jit(solution)/shard_map/ppermute | solution.py:161
  130.6 11.0 %collective-permute-done.8 = bf16[448,512]{1,0:T(8,128)(2,1)S(1)} collective-permute-done((bf16[448,512]{1,0:T(8,128)(2,1)S(1)}, bf16[448,512]{1,0:T(8,128)(2,1)S(1)}, u32[]{:S(2)}, u32[]{:S(2)}) %collective-permute-start.8) | collective-permute-done | bytes 458784 | tf_op jit(solution)/shard_map/ppermute | solution.py:161
  141.6 1.3 add_convert_fusion
  142.8 1.0 reshape.28
  143.8 7.4 %all-to-all-start.1 = ((bf16[64,7,512]{2,1,0:T(8,128)(2,1)}), bf16[64,7,512]{2,1,0:T(8,128)(2,1)S(1)}, u32[]{:S(2)}, u32[]{:S(2)}) async-start(bf16[64,7,512]{2,1,0:T(8,128)(2,1)} %reshape.28), calls=%async_computation.1 | async-start | bytes 1048576 | tf_op jit(solution)/shard_map/all_to_all | solution.py:234
  151.3 0.8 copy.13.probs_ref
  152.0 4.3 %shard_map.115 = (bf16[2048,128]{1,0:T(8,128)(2,1)}, bf16[2048,128]{1,0:T(8,128)(2,1)}, bf16[128,2048]{1,0:T(8,128)(2,1)}) custom-call(s32[1]{0:T(128)} %bitcast.2.me_ref, bf16[448,512]{1,0:T(8,128)(2,1)} %copy-done, bf16[448,512]{1,0:T(8,128)(2,1)} %copy-done.3, bf16[448,512]{1,0:T(8,128)(2,1)} %copy-done.2, bf16[448,512]{1,0:T(8,128)(2,1)} %copy-done.5, ...), custom_call_target="tpu_custom_call" | custom-call | flops 704643072 | bytes 5586948 | tf_op jit(solution)/shard_map/pallas_call | solution.py:22
  156.3 14.7 %all-to-all-done.1 = bf16[64,7,512]{2,1,0:T(8,128)(2,1)S(1)} async-done(((bf16[64,7,512]{2,1,0:T(8,128)(2,1)}), bf16[64,7,512]{2,1,0:T(8,128)(2,1)S(1)}, u32[]{:S(2)}, u32[]{:S(2)}) %all-to-all-start.1) | async-done | bytes 458784 | tf_op jit(solution)/shard_map/all_to_all | solution.py:234
  171.0 0.9 reshape.29.back_ref
  172.0 2.1 %shard_map.114 = (bf16[160,256]{1,0:T(8,128)(2,1)}, bf16[160,256]{1,0:T(8,128)(2,1)}) custom-call(s32[2,160]{1,0:T(2,128)} %get-tuple-element.18.pos_ref, f32[160,2]{1,0:T(8,128)} %copy.13.probs_ref, bf16[448,512]{1,0:T(8,128)(2,1)} %reshape.29.back_ref), custom_call_target="tpu_custom_call" | custom-call | flops 146800640 | bytes 625152 | tf_op jit(solution)/shard_map/pallas_call | solution.py:22
  (24 shorter events, 1.2 us)
Async XLA Ops:
  42.3 40.0 %copy-start = (bf16[448,512]{1,0:T(8,128)(2,1)}, bf16[448,512]{1,0:T(8,128)(2,1)S(1)}, u32[]{:S(2)}) copy-start(bf16[448,512]{1,0:T(8,128)(2,1)S(1)} %reshape.27.refs_0_) | copy-start | bytes 1376260
  42.3 13.1 %collective-permute-start = (bf16[448,512]{1,0:T(8,128)(2,1)S(1)}, bf16[448,512]{1,0:T(8,128)(2,1)S(1)}, u32[]{:S(2)}, u32[]{:S(2)}) collective-permute-start(bf16[448,512]{1,0:T(8,128)(2,1)S(1)} %reshape.27.refs_0_), channel_id=1, source_target_pairs={{0,384},{64,448},{128,256},{192,320},{256,128},{320,192},{384,0},{... | collective-permute-start | bytes 1376264 | tf_op jit(solution)/shard_map/ppermute | solution.py:161
  47.3 27.1 %collective-permute-start.4 = (bf16[448,512]{1,0:T(8,128)(2,1)S(1)}, bf16[448,512]{1,0:T(8,128)(2,1)S(1)}, u32[]{:S(2)}, u32[]{:S(2)}) collective-permute-start(bf16[448,512]{1,0:T(8,128)(2,1)S(1)} %reshape.27.refs_0_), channel_id=1, source_target_pairs={{0,128},{64,192},{128,0},{192,64},{256,384},{320,448},{384,256},{4... | collective-permute-start | bytes 1376264 | tf_op jit(solution)/shard_map/ppermute | solution.py:161
  55.5 26.9 %copy-start.1 = (bf16[448,512]{1,0:T(8,128)(2,1)}, bf16[448,512]{1,0:T(8,128)(2,1)S(1)}, u32[]{:S(2)}) copy-start(bf16[448,512]{1,0:T(8,128)(2,1)S(1)} %collective-permute-done.refs_4_.refs_6_) | copy-start | bytes 1376260
  55.5 23.0 %collective-permute-start.1 = (bf16[448,512]{1,0:T(8,128)(2,1)S(1)}, bf16[448,512]{1,0:T(8,128)(2,1)S(1)}, u32[]{:S(2)}, u32[]{:S(2)}) collective-permute-start(bf16[448,512]{1,0:T(8,128)(2,1)S(1)} %collective-permute-done.refs_4_.refs_6_), channel_id=1, source_target_pairs={{0,128},{64,192},{128,0},{192,64},{256,384},{320,448},{384,256},{4... | collective-permute-start | bytes 1376264 | tf_op jit(solution)/shard_map/ppermute | solution.py:161
  68.9 13.4 %collective-permute-start.3 = (bf16[448,512]{1,0:T(8,128)(2,1)S(1)}, bf16[448,512]{1,0:T(8,128)(2,1)S(1)}, u32[]{:S(2)}, u32[]{:S(2)}) collective-permute-start(bf16[448,512]{1,0:T(8,128)(2,1)S(1)} %reshape.27.refs_0_), channel_id=1, source_target_pairs={{0,64},{64,0},{128,192},{192,128},{256,320},{320,256},{384,448},{4... | collective-permute-start | bytes 1376264 | tf_op jit(solution)/shard_map/ppermute | solution.py:161
  72.4 9.9 %collective-permute-start.6 = (bf16[448,512]{1,0:T(8,128)(2,1)S(1)}, bf16[448,512]{1,0:T(8,128)(2,1)S(1)}, u32[]{:S(2)}, u32[]{:S(2)}) collective-permute-start(bf16[448,512]{1,0:T(8,128)(2,1)S(1)} %collective-permute-done.refs_4_.refs_6_), channel_id=1, source_target_pairs={{0,64},{64,0},{128,192},{192,128},{256,320},{320,256},{384,448},{4... | collective-permute-start | bytes 1376264 | tf_op jit(solution)/shard_map/ppermute | solution.py:161
  74.3 8.0 %copy-start.2 = (bf16[448,512]{1,0:T(8,128)(2,1)}, bf16[448,512]{1,0:T(8,128)(2,1)S(1)}, u32[]{:S(2)}) copy-start(bf16[448,512]{1,0:T(8,128)(2,1)S(1)} %collective-permute-done.4.refs_2_) | copy-start | bytes 1376260
  74.3 8.0 %collective-permute-start.5 = (bf16[448,512]{1,0:T(8,128)(2,1)S(1)}, bf16[448,512]{1,0:T(8,128)(2,1)S(1)}, u32[]{:S(2)}, u32[]{:S(2)}) collective-permute-start(bf16[448,512]{1,0:T(8,128)(2,1)S(1)} %collective-permute-done.4.refs_2_), channel_id=1, source_target_pairs={{0,64},{64,0},{128,192},{192,128},{256,320},{320,256},{384,448},{4... | collective-permute-start | bytes 1376264 | tf_op jit(solution)/shard_map/ppermute | solution.py:161
  78.5 8.8 %copy-start.6 = (bf16[448,512]{1,0:T(8,128)(2,1)}, bf16[448,512]{1,0:T(8,128)(2,1)S(1)}, u32[]{:S(2)}) copy-start(bf16[448,512]{1,0:T(8,128)(2,1)S(1)} %collective-permute-done.1.refs_0_.refs_4_) | copy-start | bytes 1376260
  78.5 8.8 %collective-permute-start.2 = (bf16[448,512]{1,0:T(8,128)(2,1)S(1)}, bf16[448,512]{1,0:T(8,128)(2,1)}, u32[]{:S(2)}, u32[]{:S(2)}) collective-permute-start(bf16[448,512]{1,0:T(8,128)(2,1)S(1)} %collective-permute-done.1.refs_0_.refs_4_), channel_id=1, source_target_pairs={{0,64},{64,0},{128,192},{192,128},{256,320},{320,256},{384,448},{4... | collective-permute-start | bytes 1376264 | tf_op jit(solution)/shard_map/ppermute | solution.py:161
  82.3 0.8 copy-start.3
  82.3 0.9 copy-start.4
  82.3 1.0 copy-start.5
  91.2 22.9 %collective-permute-start.7 = (bf16[1344,512]{1,0:T(8,128)(2,1)}, bf16[1344,512]{1,0:T(8,128)(2,1)S(1)}, u32[]{:S(2)}, u32[]{:S(2)}) collective-permute-start(bf16[1344,512]{1,0:T(8,128)(2,1)} %get-tuple-element.24), channel_id=1, source_target_pairs={{0,64},{64,0},{128,192},{192,128},{256,320},{320,256},{384,448},{4... | collective-permute-start | bytes 4128776 | tf_op jit(solution)/shard_map/ppermute | solution.py:161
  93.1 5.8 %collective-permute-start.9 = (bf16[448,512]{1,0:T(8,128)(2,1)}, bf16[448,512]{1,0:T(8,128)(2,1)S(1)}, u32[]{:S(2)}, u32[]{:S(2)}) collective-permute-start(bf16[448,512]{1,0:T(8,128)(2,1)} %get-tuple-element.25), channel_id=1, source_target_pairs={{0,64},{64,0},{128,192},{192,128},{256,320},{320,256},{384,448},{4... | collective-permute-start | bytes 1376264 | tf_op jit(solution)/shard_map/ppermute | solution.py:161
  100.1 14.0 %collective-permute-start.10 = (bf16[448,512]{1,0:T(8,128)(2,1)S(1)}, bf16[448,512]{1,0:T(8,128)(2,1)S(1)}, u32[]{:S(2)}, u32[]{:S(2)}) collective-permute-start(bf16[448,512]{1,0:T(8,128)(2,1)S(1)} %add_convert_fusion.2), channel_id=1, source_target_pairs={{0,128},{64,192},{128,0},{192,64},{256,384},{320,448},{384,256},{4... | collective-permute-start | bytes 1376264 | tf_op jit(solution)/shard_map/ppermute | solution.py:161
  115.5 15.0 %collective-permute-start.11 = (bf16[448,512]{1,0:T(8,128)(2,1)S(1)}, bf16[448,512]{1,0:T(8,128)(2,1)S(1)}, u32[]{:S(2)}, u32[]{:S(2)}) collective-permute-start(bf16[448,512]{1,0:T(8,128)(2,1)S(1)} %get-tuple-element.32), channel_id=1, source_target_pairs={{0,384},{64,448},{128,256},{192,320},{256,128},{320,192},{384,0},{... | collective-permute-start | bytes 1376264 | tf_op jit(solution)/shard_map/ppermute | solution.py:161
  118.8 32.5 %copy-start.7 = (f32[160,2]{0,1:T(2,128)S(1)}, f32[160,2]{0,1:T(2,128)}, u32[]{:S(2)}) copy-start(f32[160,2]{0,1:T(2,128)} %param.10) | copy-start | bytes 3844
  118.8 22.8 %collective-permute-start.8 = (bf16[448,512]{1,0:T(8,128)(2,1)S(1)}, bf16[448,512]{1,0:T(8,128)(2,1)S(1)}, u32[]{:S(2)}, u32[]{:S(2)}) collective-permute-start(bf16[448,512]{1,0:T(8,128)(2,1)S(1)} %get-tuple-element.31), channel_id=1, source_target_pairs={{0,128},{64,192},{128,0},{192,64},{256,384},{320,448},{384,256},{4... | collective-permute-start | bytes 1376264 | tf_op jit(solution)/shard_map/ppermute | solution.py:161
  143.8 27.2 %all-to-all-start.1 = ((bf16[64,7,512]{2,1,0:T(8,128)(2,1)}), bf16[64,7,512]{2,1,0:T(8,128)(2,1)S(1)}, u32[]{:S(2)}, u32[]{:S(2)}) async-start(bf16[64,7,512]{2,1,0:T(8,128)(2,1)} %reshape.28), calls=%async_computation.1 | async-start | bytes 1048576 | tf_op jit(solution)/shard_map/all_to_all | solution.py:234

commit v2 on v1

v2 whole, which is shorter than its diff:
```python
import functools

import jax
import jax.numpy as jnp
from jax import lax
from jax.experimental import pallas as pl
from jax.experimental.pallas import tpu as pltpu
from jax.sharding import Mesh
from jax.sharding import PartitionSpec as P

BF16, F32, I32 = jnp.bfloat16, jnp.float32, jnp.int32
PAD = 8
DP = ("za", "zb", "core")
FAR, CHIP, CORE = 4, 2, 1
FEATURES = (0, FAR)
QUAD = (0, CORE, CHIP, CORE + CHIP)


def dot(a, b, ca=1, cb=0):
    return lax.dot_general(a, b, (((ca,), (cb,)), ((), ())), preferred_element_type=F32)


def call(body, outs, args, flops, me=None):
    moved = sum(a.size * a.dtype.itemsize for a in args)
    moved += sum(o.size * o.dtype.itemsize for o in outs)
    vmem, smem = pl.BlockSpec(memory_space=pltpu.VMEM), pl.BlockSpec(memory_space=pltpu.SMEM)
    head = [] if me is None else [me]
    return pl.pallas_call(
        body,
        out_shape=outs,
        in_specs=[smem] * len(head) + [vmem] * len(args),
        out_specs=[vmem] * len(outs),
        cost_estimate=pl.CostEstimate(flops=flops, bytes_accessed=moved, transcendentals=0),
    )(*head, *args)


def iota(shape, dim):
    return lax.broadcasted_iota(I32, shape, dim)


def route_body(experts, capacity, ids_ref, probs_ref, tok_ref, grad_ref, out_ref, pos_ref):
    ids, probs = ids_ref[...], probs_ref[...]
    rows = ids.shape[1]
    width = tok_ref.shape[1]
    named = [iota((experts, rows), 0) == ids[k : k + 1, :] for k in range(2)]
    both = (named[0].astype(F32) + named[1].astype(F32)).astype(BF16)
    earlier = (iota((rows, rows), 0) < iota((rows, rows), 1)).astype(F32).astype(BF16)
    before = dot(both, earlier)
    place = iota((experts * PAD, rows), 0)
    here = []
    for k in range(2):
        slot = jnp.sum(jnp.where(named[k], before, 0.0), axis=0, keepdims=True).astype(I32)
        pos_ref[k : k + 1, :] = ids[k : k + 1, :] * capacity + slot
        here.append(place == ids[k : k + 1, :] * PAD + slot)
    picks = (here[0] | here[1]).astype(F32).astype(BF16)
    factor = jnp.sum(
        jnp.where(here[0], probs[0:1, :], jnp.where(here[1], probs[1:2, :], 0.0)),
        axis=1,
        keepdims=True,
    )
    routed = dot(picks, tok_ref[...]).astype(BF16)
    routed_grad = (dot(picks, grad_ref[...]) * factor).astype(BF16)
    for i in range(len(FEATURES)):
        at = pl.ds(i * experts * PAD, experts * PAD)
        out_ref[at, :width] = routed
        out_ref[at, width:] = routed_grad


def combine_body(pos_ref, probs_ref, back_ref, out_ref, grad_ref):
    pos, probs = pos_ref[...], probs_ref[...]
    rows = pos.shape[1]
    width = out_ref.shape[1]
    n = back_ref.shape[0] // len(FEATURES)
    place = iota((n, rows), 0)
    sums = []
    for k in range(2):
        pick = (place == pos[k : k + 1, :]).astype(F32).astype(BF16)
        sums.append(
            sum(dot(pick, back_ref[pl.ds(i * n, n), :], 0, 0) for i in range(len(FEATURES)))
        )
    out_ref[...] = (sums[0][:, :width] * probs[:, 0:1] + sums[1][:, :width] * probs[:, 1:2]).astype(
        BF16
    )
    grad_ref[...] = (sums[0][:, width:] + sums[1][:, width:]).astype(BF16)


def block_of(me_ref, mask, width):
    return pl.ds(pl.multiple_of((me_ref[0] ^ mask) * width, width), width)


def half_of(me_ref, i, n):
    far = jnp.where((me_ref[0] & FAR) == 0, i, 1 - i)
    return pl.ds(pl.multiple_of(far * n, n), n)


def pack_body(me_ref, gate_ref, up_ref, down_ref, *out_refs):
    width = out_refs[0].shape[0] // len(FEATURES)
    units = gate_ref.shape[1]
    for h, out_ref in zip(QUAD, out_refs):
        for i, f in enumerate(FEATURES):
            at, to = block_of(me_ref, h ^ f, width), pl.ds(i * width, width)
            out_ref[to, :units] = gate_ref[at, :]
            out_ref[to, units : 2 * units] = up_ref[at, :]
            out_ref[to, 2 * units :] = down_ref[:, at].T


def pre_body(me_ref, x_ref, first_ref, second_ref, *out_refs):
    n = x_ref.shape[0] // len(FEATURES)
    width = x_ref.shape[1] // 2
    units = first_ref.shape[1] // 3
    pres, hids = [0.0, 0.0], 0.0
    for i in range(len(FEATURES)):
        rows, w = half_of(me_ref, i, n), pl.ds(i * width, width)
        x, g = x_ref[rows, :width], x_ref[rows, width:]
        for j, ref in enumerate((first_ref, second_ref)):
            pres[j] = pres[j] + dot(x, ref[w, : 2 * units])
        downs = jnp.concatenate([first_ref[w, 2 * units :], second_ref[w, 2 * units :]], axis=1)
        hids = hids + dot(g, downs)
    for j, ref in enumerate(out_refs):
        ref[:, : 2 * units] = pres[j].astype(ref.dtype)
        ref[:, 2 * units :] = hids[:, j * units : (j + 1) * units].astype(ref.dtype)


def act_body(keep_ref, core_ref, chip_ref, out_ref):
    units = keep_ref.shape[1] // 3
    pre = keep_ref[...] + core_ref[...].astype(F32) + chip_ref[...].astype(F32)
    gate, up, hid = pre[:, :units], pre[:, units : 2 * units], pre[:, 2 * units :]
    sig = jax.nn.sigmoid(gate)
    silu = gate * sig
    out_ref[:, :units] = (silu * up).astype(BF16)
    out_ref[:, units : 2 * units] = (hid * up * sig * (1.0 + gate * (1.0 - sig))).astype(BF16)
    out_ref[:, 2 * units :] = (hid * silu).astype(BF16)


def result_body(first, me_ref, *refs):
    h_refs, w_refs = refs[:2], refs[2:4]
    acc_ref, out_ref = (None, refs[4]) if first else (refs[4], refs[5])
    n = h_refs[0].shape[0]
    units = h_refs[0].shape[1] // 3
    width = w_refs[0].shape[0] // len(FEATURES)
    hidden = jnp.concatenate([h[:, :units] for h in h_refs], axis=1)
    grads = jnp.concatenate([h[:, units:] for h in h_refs], axis=1)
    for i in range(len(FEATURES)):
        w = pl.ds(i * width, width)
        downs = jnp.concatenate([r[w, 2 * units :] for r in w_refs], axis=1)
        pairs = jnp.concatenate([r[w, : 2 * units] for r in w_refs], axis=1)
        out, back = dot(hidden, downs, 1, 1), dot(grads, pairs, 1, 1)
        if first:
            rows = pl.ds(i * n, n)
            out_ref[rows, :width] = out
            out_ref[rows, width:] = back
        else:
            rows, held = half_of(me_ref, i, n), pl.ds(i * n, n)
            out_ref[rows, :width] = (out + acc_ref[held, :width]).astype(BF16)
            out_ref[rows, width:] = (back + acc_ref[held, width:]).astype(BF16)


def weight_grads_body(me_ref, x_ref, *refs):
    h_refs, out_refs = refs[: len(QUAD)], refs[len(QUAD) :]
    n = x_ref.shape[0] // len(FEATURES)
    width = x_ref.shape[1] // 2
    units = h_refs[0].shape[1] // 3
    for i in range(len(FEATURES)):
        rows, to = half_of(me_ref, i, n), pl.ds(i * width, width)
        x, g = x_ref[rows, :width], x_ref[rows, width:]
        for h_ref, out_ref in zip(h_refs, out_refs):
            out_ref[to, : 2 * units] = dot(x, h_ref[:, units:], 0, 0).astype(BF16)
            out_ref[to, 2 * units :] = dot(g, h_ref[:, :units], 0, 0).astype(BF16)


def merge_body(me_ref, *refs):
    in_refs, (gate_ref, up_ref, down_ref) = refs[: len(QUAD)], refs[len(QUAD) :]
    width = in_refs[0].shape[0] // len(FEATURES)
    units = gate_ref.shape[1]
    for h, ref in zip(QUAD, in_refs):
        for i, f in enumerate(FEATURES):
            at, w = block_of(me_ref, h ^ f, width), pl.ds(i * width, width)
            gate_ref[at, :] = ref[w, :units]
            up_ref[at, :] = ref[w, units : 2 * units]
            down_ref[:, at] = ref[w, 2 * units :].T


def per_device(tokens, grad_out, expert_ids, gate_probs, gate_weight, up_weight, down_weight):
    experts = lax.axis_size("expert")
    rows, width = tokens.shape
    capacity = max(2, 3 * rows // experts)
    n, copies, quad = experts * capacity, len(FEATURES), len(QUAD)
    gate, up, down = gate_weight[0], up_weight[0], down_weight[0]
    units, model = down.shape
    me = lax.axis_index(DP).astype(I32).reshape(1)
    sds = jax.ShapeDtypeStruct
    per_pair = 6 * n * width * units

    def swap(x, mask):
        return lax.ppermute(x, DP, [(j, j ^ mask) for j in range(8)])

    send, pos = call(
        functools.partial(route_body, experts, capacity),
        [sds((copies * experts * PAD, 2 * width), BF16), sds((2, rows), I32)],
        [expert_ids.T, gate_probs.T, tokens, grad_out],
        4 * experts * PAD * rows * width,
    )
    filled = lax.all_to_all(
        send.reshape(copies * experts, PAD, 2 * width),
        ("za", "expert"),
        split_axis=0,
        concat_axis=0,
        tiled=True,
    )
    packs = call(
        pack_body,
        [sds((copies * width, 3 * units), BF16)] * quad,
        [gate, up, down],
        0,
        me,
    )
    w = [p if h == 0 else swap(p, h) for h, p in zip(QUAD, packs)]
    filled, *w = lax.optimization_barrier((filled, *w))
    x = filled[:, :capacity].reshape(copies * n, 2 * width)

    core_out = call(
        pre_body,
        [sds((n, 3 * units), BF16)] * 2,
        [x, w[1], w[3]],
        2 * copies * per_pair,
        me,
    )
    core_in = swap(jnp.concatenate(core_out, axis=0), CORE)
    keep = call(
        pre_body,
        [sds((n, 3 * units), F32)] * 2,
        [x, w[0], w[2]],
        2 * copies * per_pair,
        me,
    )
    chip_in = swap((keep[1] + core_in[n:].astype(F32)).astype(BF16), CHIP)
    (h0,) = call(
        act_body, [sds((n, 3 * units), BF16)], [keep[0], core_in[:n], chip_in], 0
    )
    h2 = swap(h0, CHIP)
    h1 = swap(h0, CORE)
    (acc,) = call(
        functools.partial(result_body, True),
        [sds((copies * n, 2 * width), F32)],
        [h0, h1, w[0], w[1]],
        2 * copies * per_pair,
        me,
    )
    h3 = swap(h2, CORE)
    (result,) = call(
        functools.partial(result_body, False),
        [sds((copies * n, 2 * width), BF16)],
        [h2, h3, w[2], w[3], acc],
        2 * copies * per_pair,
        me,
    )
    returned = lax.all_to_all(
        result.reshape(copies * experts, capacity, 2 * width),
        ("za", "expert"),
        split_axis=0,
        concat_axis=0,
        tiled=True,
    )
    shares = call(
        weight_grads_body,
        [sds((copies * width, 3 * units), BF16)] * quad,
        [x, h0, h1, h2, h3],
        quad * copies * per_pair,
        me,
    )
    got = [s if h == 0 else swap(s, h) for h, s in zip(QUAD, shares)]
    gate_grad, up_grad, down_grad = call(
        merge_body,
        [sds((model, units), BF16), sds((model, units), BF16), sds((units, model), BF16)],
        got,
        0,
        me,
    )
    layer_out, grad_tokens = call(
        combine_body,
        [sds((rows, width), BF16), sds((rows, width), BF16)],
        [pos, gate_probs, returned.reshape(copies * n, 2 * width)],
        8 * copies * n * rows * width,
    )
    return layer_out, grad_tokens, gate_grad[None], up_grad[None], down_grad[None]


def solution(mesh):
    experts = mesh.shape["expert"]
    fine = Mesh(mesh.devices.reshape(2, 2, 2, experts), (*DP, "expert"))
    return jax.shard_map(
        per_device,
        mesh=fine,
        in_specs=(
            P("expert", DP),
            P("expert", DP),
            P("expert", None),
            P("expert", None),
            P("expert", None, DP),
            P("expert", None, DP),
            P("expert", DP, None),
        ),
        out_specs=(
            P("expert", DP),
            P("expert", DP),
            P("expert", None, DP),
            P("expert", None, DP),
            P("expert", DP, None),
        ),
        check_vma=False,
    )
```

time: 175 us -> 180 us (1.029)
  blocking collectives: 39.3 us -> 0 us
  waiting for transfers between devices: 54 us -> 70.5 us
  starting transfers between devices: 52.3 us -> 67.4 us
  Pallas kernels: 19.9 us -> 28.4 us
  local copies, waits for them, and re-layouts: 3.85 us -> 9.2 us
    all_to_all x1 -> x0, blocking collectives: 39.3 us -> none  [per_device(): lax.all_to_all(send.reshape(experts, PAD, 2 * width), 'expert', split_axi...]
    ppermute x12 -> x11, waiting for transfers between devices: 39.3 us -> 70.4 us  [swap(): return lax.ppermute(x, DP, [(j, j ^ mask) for j in range(8)])]
    all_to_all x1 -> x2, starting transfers between devices: 7.45 us -> 35.9 us  [the longest x1 20.8 us: per_device(): lax.all_to_all(send.reshape(copies * experts, PAD, 2 * width), ('za', 'ex...]
    all_to_all x1 -> x2, waiting for transfers between devices: 14.7 us -> 0.01 us  [the longest x1 0.01 us: per_device(): lax.all_to_all(result.reshape(copies * experts, capacity, 2 * width), ('z...]
    ppermute x12 -> x11, starting transfers between devices: 44.9 us -> 31.5 us  [swap(): return lax.ppermute(x, DP, [(j, j ^ mask) for j in range(8)])]
    pallas_call x6 -> x10, Pallas kernels: 19.9 us -> 28.4 us  [call(): pl.pallas_call(body, out_shape=outs, in_specs=[smem] * len(head) + [vmem]...]
    convert_element_type x3 -> x1, other arithmetic: 3.86 us -> 1.17 us  [per_device(): chip_in = swap((keep[1] + core_in[n:].astype(F32)).astype(BF16), CHIP)]
    reshape x3, local copies, waits for them, and re-layouts: 2.06 us -> 4.67 us  [the longest x1 2.19 us: per_device(): result.reshape(copies * experts, capacity, 2 * width)]
  transfers between devices with their start and end apart: 13 -> 13, of which waited for: 6 -> 6; matrix products, arithmetic and copies ran while one was open for 1% -> 1% of each run, Pallas kernels for 7% -> 8%
where the time goes in v2:
time: 180 us; the launch traced here: 179 us
  waiting for transfers between devices  70.5 us (39%)
  starting transfers between devices  67.4 us (37%)
  Pallas kernels  28.4 us (16%)
  local copies, waits for them, and re-layouts  9.2 us (5%)
  other arithmetic  2.32 us (1%)
    ppermute x11, waiting for transfers between devices, swap(): return lax.ppermute(x, DP, [(j, j ^ mask) for j in range(8)])  70.4 us
    ppermute x11, starting transfers between devices, swap(): return lax.ppermute(x, DP, [(j, j ^ mask) for j in range(8)])  31.5 us
    pallas_call x10, Pallas kernels, call(): pl.pallas_call(body, out_shape=outs, in_specs=[smem] * len(head) + [vmem]...  28.4 us
    all_to_all x1, starting transfers between devices, per_device(): lax.all_to_all(send.reshape(copies * experts, PAD, 2 * width), ('za', 'ex...  20.8 us
    all_to_all x1, starting transfers between devices, per_device(): lax.all_to_all(result.reshape(copies * experts, capacity, 2 * width), ('z...  15.1 us
    unnamed x23, local copies, waits for them, and re-layouts  3.77 us
  transfers between devices with their start and end apart: 13, of which 6 were waited for; matrix products, arithmetic and copies ran while one was open for 1% of the time, Pallas kernels for 8%

profile of v2, /device:TPU:1, one launch (start us, length us, event | category | flops | bytes accessed | tf_op | source)
XLA Modules:
  0.0 178.6 jit_solution(3503634296244322732)
XLA Ops:
  0.6 2.5 %shard_map.110 = (bf16[1024,512]{1,0:T(8,128)(2,1)}, s32[2,160]{1,0:T(2,128)}) custom-call(s32[2,160]{1,0:T(2,128)} %bitcast.20, f32[2,160]{1,0:T(2,128)} %bitcast.16, bf16[160,256]{1,0:T(8,128)(2,1)} %tok_ref.1, bf16[160,256]{1,0:T(8,128)(2,1)} %grad_ref.1), custom_call_target="tpu_custom_call" | custom-call | flops 83886080 | bytes 1216256 | tf_op jit(solution)/shard_map/pallas_call | solution.py:28
  3.1 20.8 %all-to-all-start = ((bf16[128,8,512]{2,1,0:T(8,128)(2,1)}), bf16[128,8,512]{2,1,0:T(8,128)(2,1)S(1)}, u32[]{:S(2)}, u32[]{:S(2)}) async-start(bf16[128,8,512]{2,1,0:T(8,128)(2,1)} %bitcast.12), calls=%async_computation | async-start | bytes 2097152 | tf_op jit(solution)/shard_map/all_to_all | solution.py:203
  23.9 2.7 %shard_map.111 = (bf16[512,384]{1,0:T(8,128)(2,1)}, bf16[512,384]{1,0:T(8,128)(2,1)}, bf16[512,384]{1,0:T(8,128)(2,1)}, bf16[512,384]{1,0:T(8,128)(2,1)}) custom-call(s32[1]{0:T(128)} %bitcast.2.me_ref, bf16[2048,128]{1,0:T(8,128)(2,1)} %bitcast.13, bf16[2048,128]{1,0:T(8,128)(2,1)} %bitcast.14, bf16[128,2048]{1,0:T(8,128)(2,1)} %bitcast.15), custom_call_target="tpu_custom_call" | custom-call | bytes 3145728 | tf_op jit(solution)/shard_map/pallas_call | solution.py:28
  26.6 2.9 %collective-permute-start = (bf16[512,384]{1,0:T(8,128)(2,1)}, bf16[512,384]{1,0:T(8,128)(2,1)S(1)}, u32[]{:S(2)}, u32[]{:S(2)}) collective-permute-start(bf16[512,384]{1,0:T(8,128)(2,1)} %get-tuple-element.32), channel_id=1, source_target_pairs={{0,64},{64,0},{128,192},{192,128},{256,320},{320,256},{384,448},{4... | collective-permute-start | bytes 1179656 | tf_op jit(solution)/shard_map/ppermute | solution.py:195
  29.4 3.1 %collective-permute-start.1 = (bf16[512,384]{1,0:T(8,128)(2,1)}, bf16[512,384]{1,0:T(8,128)(2,1)S(1)}, u32[]{:S(2)}, u32[]{:S(2)}) collective-permute-start(bf16[512,384]{1,0:T(8,128)(2,1)} %get-tuple-element.33), channel_id=1, source_target_pairs={{0,128},{64,192},{128,0},{192,64},{256,384},{320,448},{384,256},{4... | collective-permute-start | bytes 1179656 | tf_op jit(solution)/shard_map/ppermute | solution.py:195
  32.5 2.4 %collective-permute-start.2 = (bf16[512,384]{1,0:T(8,128)(2,1)}, bf16[512,384]{1,0:T(8,128)(2,1)S(1)}, u32[]{:S(2)}, u32[]{:S(2)}) collective-permute-start(bf16[512,384]{1,0:T(8,128)(2,1)} %get-tuple-element.34), channel_id=1, source_target_pairs={{0,192},{64,128},{128,64},{192,0},{256,448},{320,384},{384,320},{4... | collective-permute-start | bytes 1179656 | tf_op jit(solution)/shard_map/ppermute | solution.py:195
  34.9 21.6 %collective-permute-done.1.second_ref.refs_2_ = bf16[512,384]{1,0:T(8,128)(2,1)S(1)} collective-permute-done((bf16[512,384]{1,0:T(8,128)(2,1)}, bf16[512,384]{1,0:T(8,128)(2,1)S(1)}, u32[]{:S(2)}, u32[]{:S(2)}) %collective-permute-start.1) | collective-permute-done | bytes 393248 | tf_op jit(solution)/shard_map/ppermute | solution.py:195
  56.5 8.4 %collective-permute-done.2.second_ref.refs_3_ = bf16[512,384]{1,0:T(8,128)(2,1)S(1)} collective-permute-done((bf16[512,384]{1,0:T(8,128)(2,1)}, bf16[512,384]{1,0:T(8,128)(2,1)S(1)}, u32[]{:S(2)}, u32[]{:S(2)}) %collective-permute-start.2) | collective-permute-done | bytes 393248 | tf_op jit(solution)/shard_map/ppermute | solution.py:195
  65.0 1.2 reshape.27.x_ref
  66.2 2.8 %shard_map.113 = (bf16[448,384]{1,0:T(8,128)(2,1)}, bf16[448,384]{1,0:T(8,128)(2,1)}) custom-call(s32[1]{0:T(128)} %bitcast.2.me_ref, bf16[896,512]{1,0:T(8,128)(2,1)} %reshape.27.x_ref, bf16[512,384]{1,0:T(8,128)(2,1)} %copy-done.2, bf16[512,384]{1,0:T(8,128)(2,1)} %copy-done.1), custom_call_target="tpu_custom_call" | custom-call | flops 352321536 | bytes 2392064 | tf_op jit(solution)/shard_map/pallas_call | solution.py:28
  70.1 2.3 %collective-permute-start.3 = (bf16[896,384]{1,0:T(8,128)(2,1)S(1)}, bf16[896,384]{1,0:T(8,128)(2,1)S(1)}, u32[]{:S(2)}, u32[]{:S(2)}) collective-permute-start(bf16[896,384]{1,0:T(8,128)(2,1)S(1)} %pad_maximum_fusion), channel_id=1, source_target_pairs={{0,64},{64,0},{128,192},{192,128},{256,320},{320,256},{384,448},{4... | collective-permute-start | bytes 2064392 | tf_op jit(solution)/shard_map/ppermute | solution.py:195
  72.4 3.0 %shard_map.112 = (f32[448,384]{1,0:T(8,128)}, f32[448,384]{1,0:T(8,128)}) custom-call(s32[1]{0:T(128)} %bitcast.2.me_ref, bf16[896,512]{1,0:T(8,128)(2,1)} %reshape.27.x_ref, bf16[512,384]{1,0:T(8,128)(2,1)} %get-tuple-element.36.first_ref.refs_2_, bf16[512,384]{1,0:T(8,128)(2,1)} %copy-done), custom_call_target="tpu_custom_call" | custom-call | flops 352321536 | bytes 3080192 | tf_op jit(solution)/shard_map/pallas_call | solution.py:28
  76.6 3.1 %collective-permute-start.4 = (bf16[448,384]{1,0:T(8,128)(2,1)S(1)}, bf16[448,384]{1,0:T(8,128)(2,1)S(1)}, u32[]{:S(2)}, u32[]{:S(2)}) collective-permute-start(bf16[448,384]{1,0:T(8,128)(2,1)S(1)} %add_convert_fusion), channel_id=1, source_target_pairs={{0,128},{64,192},{128,0},{192,64},{256,384},{320,448},{384,256},{4... | collective-permute-start | bytes 1032200 | tf_op jit(solution)/shard_map/ppermute | solution.py:195
  80.5 7.5 %collective-permute-done.4.chip_ref = bf16[448,384]{1,0:T(8,128)(2,1)S(1)} collective-permute-done((bf16[448,384]{1,0:T(8,128)(2,1)S(1)}, bf16[448,384]{1,0:T(8,128)(2,1)S(1)}, u32[]{:S(2)}, u32[]{:S(2)}) %collective-permute-start.4) | collective-permute-done | bytes 344096 | tf_op jit(solution)/shard_map/ppermute | solution.py:195
  88.8 2.2 %shard_map.114.refs_0_ = bf16[448,384]{1,0:T(8,128)(2,1)} custom-call(f32[448,384]{1,0:T(8,128)} %get-tuple-element.38.keep_ref, bf16[448,384]{1,0:T(8,128)(2,1)} %slice.12.core_ref, bf16[448,384]{1,0:T(8,128)(2,1)} %copy-done.6), custom_call_target="tpu_custom_call" | custom-call | bytes 1720320 | tf_op jit(solution)/shard_map/pallas_call | solution.py:28
  91.0 3.1 %collective-permute-start.5 = (bf16[448,384]{1,0:T(8,128)(2,1)}, bf16[448,384]{1,0:T(8,128)(2,1)S(1)}, u32[]{:S(2)}, u32[]{:S(2)}) collective-permute-start(bf16[448,384]{1,0:T(8,128)(2,1)} %shard_map.114.refs_0_), channel_id=1, source_target_pairs={{0,128},{64,192},{128,0},{192,64},{256,384},{320,448},{384,256},{4... | collective-permute-start | bytes 1032200 | tf_op jit(solution)/shard_map/ppermute | solution.py:195
  94.1 3.2 %collective-permute-start.7 = (bf16[448,384]{1,0:T(8,128)(2,1)}, bf16[448,384]{1,0:T(8,128)(2,1)S(1)}, u32[]{:S(2)}, u32[]{:S(2)}) collective-permute-start(bf16[448,384]{1,0:T(8,128)(2,1)} %shard_map.114.refs_0_), channel_id=1, source_target_pairs={{0,64},{64,0},{128,192},{192,128},{256,320},{320,256},{384,448},{4... | collective-permute-start | bytes 1032200 | tf_op jit(solution)/shard_map/ppermute | solution.py:195
  97.3 4.5 %collective-permute-done.5.refs_0_.refs_2_ = bf16[448,384]{1,0:T(8,128)(2,1)S(1)} collective-permute-done((bf16[448,384]{1,0:T(8,128)(2,1)}, bf16[448,384]{1,0:T(8,128)(2,1)S(1)}, u32[]{:S(2)}, u32[]{:S(2)}) %collective-permute-start.5) | collective-permute-done | bytes 344096 | tf_op jit(solution)/shard_map/ppermute | solution.py:195
  101.7 3.7 %collective-permute-start.6 = (bf16[448,384]{1,0:T(8,128)(2,1)S(1)}, bf16[448,384]{1,0:T(8,128)(2,1)S(1)}, u32[]{:S(2)}, u32[]{:S(2)}) collective-permute-start(bf16[448,384]{1,0:T(8,128)(2,1)S(1)} %collective-permute-done.5.refs_0_.refs_2_), channel_id=1, source_target_pairs={{0,64},{64,0},{128,192},{192,128},{256,320},{320,256},{384,448},{4... | collective-permute-start | bytes 1032200 | tf_op jit(solution)/shard_map/ppermute | solution.py:195
  106.2 3.1 %shard_map.115.refs_4_ = f32[896,512]{1,0:T(8,128)} custom-call(s32[1]{0:T(128)} %bitcast.2.me_ref, bf16[448,384]{1,0:T(8,128)(2,1)} %shard_map.114.refs_0_, bf16[448,384]{1,0:T(8,128)(2,1)} %copy-done.8, bf16[512,384]{1,0:T(8,128)(2,1)} %get-tuple-element.36.first_ref.refs_2_, bf16[512,384]{1,0:T(8,128)(2,1)} %copy-done.2), custom_call_target="tpu_custom_call" | custom-call | flops 352321536 | bytes 3309568 | tf_op jit(solution)/shard_map/pallas_call | solution.py:28
  110.1 3.5 %shard_map.116 = bf16[896,512]{1,0:T(8,128)(2,1)} custom-call(s32[1]{0:T(128)} %bitcast.2.me_ref, bf16[448,384]{1,0:T(8,128)(2,1)} %copy-done.7, bf16[448,384]{1,0:T(8,128)(2,1)} %copy-done.9, bf16[512,384]{1,0:T(8,128)(2,1)} %copy-done, bf16[512,384]{1,0:T(8,128)(2,1)} %copy-done.1, f32[896,512]{1,0:T(8,128)} %shard_map.115.refs_4_), custom_call_target="tpu_custom_call" | custom-call | flops 352321536 | bytes 4227072 | tf_op jit(solution)/shard_map/pallas_call | solution.py:28
  113.6 2.2 %reshape.28 = bf16[128,7,512]{2,1,0:T(8,128)(2,1)} reshape(bf16[896,512]{1,0:T(8,128)(2,1)} %shard_map.116) | data formatting | bytes 1835008 | tf_op jit(solution)/shard_map/reshape | solution.py:258
  115.8 15.1 %all-to-all-start.1 = ((bf16[128,7,512]{2,1,0:T(8,128)(2,1)}), bf16[128,7,512]{2,1,0:T(8,128)(2,1)S(1)}, u32[]{:S(2)}, u32[]{:S(2)}) async-start(bf16[128,7,512]{2,1,0:T(8,128)(2,1)} %reshape.28), calls=%async_computation.1 | async-start | bytes 2097152 | tf_op jit(solution)/shard_map/all_to_all | solution.py:257
  130.9 3.6 %shard_map.118 = (bf16[512,384]{1,0:T(8,128)(2,1)}, bf16[512,384]{1,0:T(8,128)(2,1)}, bf16[512,384]{1,0:T(8,128)(2,1)}, bf16[512,384]{1,0:T(8,128)(2,1)}) custom-call(s32[1]{0:T(128)} %bitcast.2.me_ref, bf16[896,512]{1,0:T(8,128)(2,1)} %reshape.27.x_ref, bf16[448,384]{1,0:T(8,128)(2,1)} %shard_map.114.refs_0_, bf16[448,384]{1,0:T(8,128)(2,1)} %copy-done.8, ...), custom_call_target="tpu_custom_call" | custom-call | flops 704643072 | bytes 3866624 | tf_op jit(solution)/shard_map/pallas_call | solution.py:28
  134.5 2.2 %collective-permute-start.8 = (bf16[512,384]{1,0:T(8,128)(2,1)}, bf16[512,384]{1,0:T(8,128)(2,1)S(1)}, u32[]{:S(2)}, u32[]{:S(2)}) collective-permute-start(bf16[512,384]{1,0:T(8,128)(2,1)} %get-tuple-element.47), channel_id=1, source_target_pairs={{0,64},{64,0},{128,192},{192,128},{256,320},{320,256},{384,448},{4... | collective-permute-start | bytes 1179656 | tf_op jit(solution)/shard_map/ppermute | solution.py:195
  136.7 2.4 %collective-permute-start.9 = (bf16[512,384]{1,0:T(8,128)(2,1)}, bf16[512,384]{1,0:T(8,128)(2,1)S(1)}, u32[]{:S(2)}, u32[]{:S(2)}) collective-permute-start(bf16[512,384]{1,0:T(8,128)(2,1)} %get-tuple-element.48), channel_id=1, source_target_pairs={{0,128},{64,192},{128,0},{192,64},{256,384},{320,448},{384,256},{4... | collective-permute-start | bytes 1179656 | tf_op jit(solution)/shard_map/ppermute | solution.py:195
  139.0 3.3 %collective-permute-start.10 = (bf16[512,384]{1,0:T(8,128)(2,1)}, bf16[512,384]{1,0:T(8,128)(2,1)S(1)}, u32[]{:S(2)}, u32[]{:S(2)}) collective-permute-start(bf16[512,384]{1,0:T(8,128)(2,1)} %get-tuple-element.49), channel_id=1, source_target_pairs={{0,192},{64,128},{128,64},{192,0},{256,448},{320,384},{384,320},{4... | collective-permute-start | bytes 1179656 | tf_op jit(solution)/shard_map/ppermute | solution.py:195
  143.1 20.0 %collective-permute-done.9.refs_2_ = bf16[512,384]{1,0:T(8,128)(2,1)S(1)} collective-permute-done((bf16[512,384]{1,0:T(8,128)(2,1)}, bf16[512,384]{1,0:T(8,128)(2,1)S(1)}, u32[]{:S(2)}, u32[]{:S(2)}) %collective-permute-start.9) | collective-permute-done | bytes 393248 | tf_op jit(solution)/shard_map/ppermute | solution.py:195
  163.1 8.4 %collective-permute-done.10.refs_3_ = bf16[512,384]{1,0:T(8,128)(2,1)S(1)} collective-permute-done((bf16[512,384]{1,0:T(8,128)(2,1)}, bf16[512,384]{1,0:T(8,128)(2,1)S(1)}, u32[]{:S(2)}, u32[]{:S(2)}) %collective-permute-start.10) | collective-permute-done | bytes 393248 | tf_op jit(solution)/shard_map/ppermute | solution.py:195
  172.3 2.7 %shard_map.119 = (bf16[2048,128]{1,0:T(8,128)(2,1)}, bf16[2048,128]{1,0:T(8,128)(2,1)}, bf16[128,2048]{1,0:T(8,128)(2,1)}) custom-call(s32[1]{0:T(128)} %bitcast.2.me_ref, bf16[512,384]{1,0:T(8,128)(2,1)} %get-tuple-element.46.refs_0_, bf16[512,384]{1,0:T(8,128)(2,1)} %copy-done.3, bf16[512,384]{1,0:T(8,128)(2,1)} %copy-done.4, bf16[512,384]{1,0:T(8,128)(2,1)} %copy-done.5), custom_call_target="tpu_custom_call" | custom-call | bytes 3145728 | tf_op jit(solution)/shard_map/pallas_call | solution.py:28
  175.0 1.2 reshape.29.back_ref
  176.2 2.4 %shard_map.117 = (bf16[160,256]{1,0:T(8,128)(2,1)}, bf16[160,256]{1,0:T(8,128)(2,1)}) custom-call(s32[2,160]{1,0:T(2,128)} %get-tuple-element.29.pos_ref, f32[160,2]{1,0:T(8,128)} %copy.13.probs_ref, bf16[896,512]{1,0:T(8,128)(2,1)} %reshape.29.back_ref), custom_call_target="tpu_custom_call" | custom-call | flops 293601280 | bytes 1083904 | tf_op jit(solution)/shard_map/pallas_call | solution.py:28
  (33 shorter events, 6.9 us)
Async XLA Ops:
  3.1 61.9 %all-to-all-start = ((bf16[128,8,512]{2,1,0:T(8,128)(2,1)}), bf16[128,8,512]{2,1,0:T(8,128)(2,1)S(1)}, u32[]{:S(2)}, u32[]{:S(2)}) async-start(bf16[128,8,512]{2,1,0:T(8,128)(2,1)} %bitcast.12), calls=%async_computation | async-start | bytes 2097152 | tf_op jit(solution)/shard_map/all_to_all | solution.py:203
  26.6 8.3 %collective-permute-start = (bf16[512,384]{1,0:T(8,128)(2,1)}, bf16[512,384]{1,0:T(8,128)(2,1)S(1)}, u32[]{:S(2)}, u32[]{:S(2)}) collective-permute-start(bf16[512,384]{1,0:T(8,128)(2,1)} %get-tuple-element.32), channel_id=1, source_target_pairs={{0,64},{64,0},{128,192},{192,128},{256,320},{320,256},{384,448},{4... | collective-permute-start | bytes 1179656 | tf_op jit(solution)/shard_map/ppermute | solution.py:195
  29.4 27.1 %collective-permute-start.1 = (bf16[512,384]{1,0:T(8,128)(2,1)}, bf16[512,384]{1,0:T(8,128)(2,1)S(1)}, u32[]{:S(2)}, u32[]{:S(2)}) collective-permute-start(bf16[512,384]{1,0:T(8,128)(2,1)} %get-tuple-element.33), channel_id=1, source_target_pairs={{0,128},{64,192},{128,0},{192,64},{256,384},{320,448},{384,256},{4... | collective-permute-start | bytes 1179656 | tf_op jit(solution)/shard_map/ppermute | solution.py:195
  32.5 32.4 %collective-permute-start.2 = (bf16[512,384]{1,0:T(8,128)(2,1)}, bf16[512,384]{1,0:T(8,128)(2,1)S(1)}, u32[]{:S(2)}, u32[]{:S(2)}) collective-permute-start(bf16[512,384]{1,0:T(8,128)(2,1)} %get-tuple-element.34), channel_id=1, source_target_pairs={{0,192},{64,128},{128,64},{192,0},{256,448},{320,384},{384,320},{4... | collective-permute-start | bytes 1179656 | tf_op jit(solution)/shard_map/ppermute | solution.py:195
  34.9 31.3 %copy-start.2 = (bf16[512,384]{1,0:T(8,128)(2,1)}, bf16[512,384]{1,0:T(8,128)(2,1)S(1)}, u32[]{:S(2)}) copy-start(bf16[512,384]{1,0:T(8,128)(2,1)S(1)} %collective-permute-done.first_ref.refs_3_) | copy-start | bytes 1179652
  56.5 12.4 %copy-start = (bf16[512,384]{1,0:T(8,128)(2,1)}, bf16[512,384]{1,0:T(8,128)(2,1)S(1)}, u32[]{:S(2)}) copy-start(bf16[512,384]{1,0:T(8,128)(2,1)S(1)} %collective-permute-done.1.second_ref.refs_2_) | copy-start | bytes 1179652
  65.0 1.2 copy-start.1
  70.1 5.3 %collective-permute-start.3 = (bf16[896,384]{1,0:T(8,128)(2,1)S(1)}, bf16[896,384]{1,0:T(8,128)(2,1)S(1)}, u32[]{:S(2)}, u32[]{:S(2)}) collective-permute-start(bf16[896,384]{1,0:T(8,128)(2,1)S(1)} %pad_maximum_fusion), channel_id=1, source_target_pairs={{0,64},{64,0},{128,192},{192,128},{256,320},{320,256},{384,448},{4... | collective-permute-start | bytes 2064392 | tf_op jit(solution)/shard_map/ppermute | solution.py:195
  76.6 11.4 %collective-permute-start.4 = (bf16[448,384]{1,0:T(8,128)(2,1)S(1)}, bf16[448,384]{1,0:T(8,128)(2,1)S(1)}, u32[]{:S(2)}, u32[]{:S(2)}) collective-permute-start(bf16[448,384]{1,0:T(8,128)(2,1)S(1)} %add_convert_fusion), channel_id=1, source_target_pairs={{0,128},{64,192},{128,0},{192,64},{256,384},{320,448},{384,256},{4... | collective-permute-start | bytes 1032200 | tf_op jit(solution)/shard_map/ppermute | solution.py:195
  88.0 0.8 copy-start.6
  91.0 10.7 %collective-permute-start.5 = (bf16[448,384]{1,0:T(8,128)(2,1)}, bf16[448,384]{1,0:T(8,128)(2,1)S(1)}, u32[]{:S(2)}, u32[]{:S(2)}) collective-permute-start(bf16[448,384]{1,0:T(8,128)(2,1)} %shard_map.114.refs_0_), channel_id=1, source_target_pairs={{0,128},{64,192},{128,0},{192,64},{256,384},{320,448},{384,256},{4... | collective-permute-start | bytes 1032200 | tf_op jit(solution)/shard_map/ppermute | solution.py:195
  94.1 11.4 %collective-permute-start.7 = (bf16[448,384]{1,0:T(8,128)(2,1)}, bf16[448,384]{1,0:T(8,128)(2,1)S(1)}, u32[]{:S(2)}, u32[]{:S(2)}) collective-permute-start(bf16[448,384]{1,0:T(8,128)(2,1)} %shard_map.114.refs_0_), channel_id=1, source_target_pairs={{0,64},{64,0},{128,192},{192,128},{256,320},{320,256},{384,448},{4... | collective-permute-start | bytes 1032200 | tf_op jit(solution)/shard_map/ppermute | solution.py:195
  101.7 7.6 %copy-start.7 = (bf16[448,384]{1,0:T(8,128)(2,1)}, bf16[448,384]{1,0:T(8,128)(2,1)S(1)}, u32[]{:S(2)}) copy-start(bf16[448,384]{1,0:T(8,128)(2,1)S(1)} %collective-permute-done.5.refs_0_.refs_2_) | copy-start | bytes 1032196
  101.7 7.6 %collective-permute-start.6 = (bf16[448,384]{1,0:T(8,128)(2,1)S(1)}, bf16[448,384]{1,0:T(8,128)(2,1)S(1)}, u32[]{:S(2)}, u32[]{:S(2)}) collective-permute-start(bf16[448,384]{1,0:T(8,128)(2,1)S(1)} %collective-permute-done.5.refs_0_.refs_2_), channel_id=1, source_target_pairs={{0,64},{64,0},{128,192},{192,128},{256,320},{320,256},{384,448},{4... | collective-permute-start | bytes 1032200 | tf_op jit(solution)/shard_map/ppermute | solution.py:195
  105.5 0.8 copy-start.8
  109.4 0.7 copy-start.9
  115.8 59.2 %all-to-all-start.1 = ((bf16[128,7,512]{2,1,0:T(8,128)(2,1)}), bf16[128,7,512]{2,1,0:T(8,128)(2,1)S(1)}, u32[]{:S(2)}, u32[]{:S(2)}) async-start(bf16[128,7,512]{2,1,0:T(8,128)(2,1)} %reshape.28), calls=%async_computation.1 | async-start | bytes 2097152 | tf_op jit(solution)/shard_map/all_to_all | solution.py:257
  130.8 11.5 %copy-start.10 = (f32[160,2]{0,1:T(2,128)S(1)}, f32[160,2]{0,1:T(2,128)}, u32[]{:S(2)}) copy-start(f32[160,2]{0,1:T(2,128)} %param.10) | copy-start | bytes 3844
  134.5 8.6 %collective-permute-start.8 = (bf16[512,384]{1,0:T(8,128)(2,1)}, bf16[512,384]{1,0:T(8,128)(2,1)S(1)}, u32[]{:S(2)}, u32[]{:S(2)}) collective-permute-start(bf16[512,384]{1,0:T(8,128)(2,1)} %get-tuple-element.47), channel_id=1, source_target_pairs={{0,64},{64,0},{128,192},{192,128},{256,320},{320,256},{384,448},{4... | collective-permute-start | bytes 1179656 | tf_op jit(solution)/shard_map/ppermute | solution.py:195
  136.7 26.4 %collective-permute-start.9 = (bf16[512,384]{1,0:T(8,128)(2,1)}, bf16[512,384]{1,0:T(8,128)(2,1)S(1)}, u32[]{:S(2)}, u32[]{:S(2)}) collective-permute-start(bf16[512,384]{1,0:T(8,128)(2,1)} %get-tuple-element.48), channel_id=1, source_target_pairs={{0,128},{64,192},{128,0},{192,64},{256,384},{320,448},{384,256},{4... | collective-permute-start | bytes 1179656 | tf_op jit(solution)/shard_map/ppermute | solution.py:195
  139.0 32.5 %collective-permute-start.10 = (bf16[512,384]{1,0:T(8,128)(2,1)}, bf16[512,384]{1,0:T(8,128)(2,1)S(1)}, u32[]{:S(2)}, u32[]{:S(2)}) collective-permute-start(bf16[512,384]{1,0:T(8,128)(2,1)} %get-tuple-element.49), channel_id=1, source_target_pairs={{0,192},{64,128},{128,64},{192,0},{256,448},{320,384},{384,320},{4... | collective-permute-start | bytes 1179656 | tf_op jit(solution)/shard_map/ppermute | solution.py:195
  143.1 28.4 %copy-start.3 = (bf16[512,384]{1,0:T(8,128)(2,1)}, bf16[512,384]{1,0:T(8,128)(2,1)S(1)}, u32[]{:S(2)}) copy-start(bf16[512,384]{1,0:T(8,128)(2,1)S(1)} %collective-permute-done.8.refs_1_) | copy-start | bytes 1179652
  163.1 8.4 %copy-start.4 = (bf16[512,384]{1,0:T(8,128)(2,1)}, bf16[512,384]{1,0:T(8,128)(2,1)S(1)}, u32[]{:S(2)}) copy-start(bf16[512,384]{1,0:T(8,128)(2,1)S(1)} %collective-permute-done.9.refs_2_) | copy-start | bytes 1179652
  171.5 0.8 copy-start.5

commit v3 on v2

--- a/solution.py
+++ b/solution.py
@@ -8,12 +8,12 @@
 from jax.sharding import Mesh
 from jax.sharding import PartitionSpec as P
 
+
 BF16, F32, I32 = jnp.bfloat16, jnp.float32, jnp.int32
 PAD = 8
 DP = ("za", "zb", "core")
 FAR, CHIP, CORE = 4, 2, 1
 FEATURES = (0, FAR)
-QUAD = (0, CORE, CHIP, CORE + CHIP)
 
 
 def dot(a, b, ca=1, cb=0):
@@ -93,15 +93,14 @@
     return pl.ds(pl.multiple_of(far * n, n), n)
 
 
-def pack_body(me_ref, gate_ref, up_ref, down_ref, *out_refs):
-    width = out_refs[0].shape[0] // len(FEATURES)
+def pack_body(masks, me_ref, gate_ref, up_ref, down_ref, out_ref):
+    width = out_ref.shape[0] // len(masks)
     units = gate_ref.shape[1]
-    for h, out_ref in zip(QUAD, out_refs):
-        for i, f in enumerate(FEATURES):
-            at, to = block_of(me_ref, h ^ f, width), pl.ds(i * width, width)
-            out_ref[to, :units] = gate_ref[at, :]
-            out_ref[to, units : 2 * units] = up_ref[at, :]
-            out_ref[to, 2 * units :] = down_ref[:, at].T
+    for i, mask in enumerate(masks):
+        at, to = block_of(me_ref, mask, width), pl.ds(i * width, width)
+        out_ref[to, :units] = gate_ref[at, :]
+        out_ref[to, units : 2 * units] = up_ref[at, :]
+        out_ref[to, 2 * units :] = down_ref[:, at].T
 
 
 def pre_body(me_ref, x_ref, first_ref, second_ref, *out_refs):
@@ -155,26 +154,34 @@
             out_ref[rows, width:] = (back + acc_ref[held, width:]).astype(BF16)
 
 
-def weight_grads_body(me_ref, x_ref, *refs):
-    h_refs, out_refs = refs[: len(QUAD)], refs[len(QUAD) :]
-    n = x_ref.shape[0] // len(FEATURES)
-    width = x_ref.shape[1] // 2
-    units = h_refs[0].shape[1] // 3
+def weight_grads_body(me_ref, own_ref, near_ref, far_ref, h0_ref, h1_ref, keep_ref, send_ref):
+    n = near_ref.shape[0]
+    width = own_ref.shape[1] // 2
+    units = h0_ref.shape[1] // 3
+    grads = jnp.concatenate([h0_ref[:, units:], h1_ref[:, units:]], axis=1)
+    hidden = jnp.concatenate([h0_ref[:, :units], h1_ref[:, :units]], axis=1)
+
+    def work(x, g, to):
+        both, down = dot(x, grads, 0, 0).astype(BF16), dot(g, hidden, 0, 0).astype(BF16)
+        keep_ref[to, : 2 * units], send_ref[to, : 2 * units] = both[:, : 2 * units], both[:, 2 * units :]
+        keep_ref[to, 2 * units :], send_ref[to, 2 * units :] = down[:, :units], down[:, units:]
+
     for i in range(len(FEATURES)):
-        rows, to = half_of(me_ref, i, n), pl.ds(i * width, width)
-        x, g = x_ref[rows, :width], x_ref[rows, width:]
-        for h_ref, out_ref in zip(h_refs, out_refs):
-            out_ref[to, : 2 * units] = dot(x, h_ref[:, units:], 0, 0).astype(BF16)
-            out_ref[to, 2 * units :] = dot(g, h_ref[:, :units], 0, 0).astype(BF16)
-
-
-def merge_body(me_ref, *refs):
-    in_refs, (gate_ref, up_ref, down_ref) = refs[: len(QUAD)], refs[len(QUAD) :]
-    width = in_refs[0].shape[0] // len(FEATURES)
+        rows = pl.ds(i * n, n)
+        work(own_ref[rows, :width], own_ref[rows, width:], pl.ds(i * width, width))
+    for i, ref in enumerate((near_ref, far_ref)):
+        at = pl.ds((len(FEATURES) + i) * width, width)
+        work(ref[:, :width], ref[:, width:], at)
+
+
+def merge_body(me_ref, keep_ref, got_ref, gate_ref, up_ref, down_ref):
     units = gate_ref.shape[1]
-    for h, ref in zip(QUAD, in_refs):
-        for i, f in enumerate(FEATURES):
-            at, w = block_of(me_ref, h ^ f, width), pl.ds(i * width, width)
+    width = keep_ref.shape[0] // 4
+    for core, ref in ((0, keep_ref), (CORE, got_ref)):
+        for i in range(4):
+            block = ((me_ref[0] ^ core ^ (CHIP if i >= 2 else 0)) & (FAR - 1)) + FAR * (i % 2)
+            at = pl.ds(pl.multiple_of(block * width, width), width)
+            w = pl.ds(i * width, width)
             gate_ref[at, :] = ref[w, :units]
             up_ref[at, :] = ref[w, units : 2 * units]
             down_ref[:, at] = ref[w, 2 * units :].T
@@ -184,7 +191,7 @@
     experts = lax.axis_size("expert")
     rows, width = tokens.shape
     capacity = max(2, 3 * rows // experts)
-    n, copies, quad = experts * capacity, len(FEATURES), len(QUAD)
+    n, copies = experts * capacity, len(FEATURES)
     gate, up, down = gate_weight[0], up_weight[0], down_weight[0]
     units, model = down.shape
     me = lax.axis_index(DP).astype(I32).reshape(1)
@@ -194,45 +201,45 @@
     def swap(x, mask):
         return lax.ppermute(x, DP, [(j, j ^ mask) for j in range(8)])
 
+    def pack(*masks):
+        return call(
+            functools.partial(pack_body, masks),
+            [sds((len(masks) * width, 3 * units), BF16)],
+            [gate, up, down],
+            0,
+            me,
+        )[0]
+
+    def pre(weights, dtype):
+        return call(
+            pre_body, [sds((n, 3 * units), dtype)] * 2, [x, *weights], 2 * copies * per_pair, me
+        )
+
+    def there_and_back(a):
+        return lax.all_to_all(a, ("za", "expert"), split_axis=0, concat_axis=0, tiled=True)
+
+    cut = copies * width
+    chip_w = swap(pack(CHIP, CHIP ^ FAR, CHIP ^ CORE, CHIP ^ CORE ^ FAR), CHIP)
     send, pos = call(
         functools.partial(route_body, experts, capacity),
         [sds((copies * experts * PAD, 2 * width), BF16), sds((2, rows), I32)],
         [expert_ids.T, gate_probs.T, tokens, grad_out],
         4 * experts * PAD * rows * width,
     )
-    filled = lax.all_to_all(
-        send.reshape(copies * experts, PAD, 2 * width),
-        ("za", "expert"),
-        split_axis=0,
-        concat_axis=0,
-        tiled=True,
-    )
-    packs = call(
-        pack_body,
-        [sds((copies * width, 3 * units), BF16)] * quad,
-        [gate, up, down],
-        0,
-        me,
-    )
-    w = [p if h == 0 else swap(p, h) for h, p in zip(QUAD, packs)]
-    filled, *w = lax.optimization_barrier((filled, *w))
+    filled = there_and_back(send.reshape(copies * experts, PAD, 2 * width))
+    near = pack(0, FAR, CORE, CORE ^ FAR)
+    core_w = swap(near[cut:], CORE)
+    relay_w = swap(chip_w[cut:], CORE)
+    filled, near, core_w, chip_w, relay_w = lax.optimization_barrier(
+        (filled, near, core_w, chip_w, relay_w)
+    )
+    w = {0: near[:cut], CORE: core_w, CHIP: chip_w[:cut], CHIP ^ CORE: relay_w}
     x = filled[:, :capacity].reshape(copies * n, 2 * width)
-
-    core_out = call(
-        pre_body,
-        [sds((n, 3 * units), BF16)] * 2,
-        [x, w[1], w[3]],
-        2 * copies * per_pair,
-        me,
-    )
+    x_near = swap(x[:n], CHIP)
+
+    core_out = pre((w[1], w[3]), BF16)
     core_in = swap(jnp.concatenate(core_out, axis=0), CORE)
-    keep = call(
-        pre_body,
-        [sds((n, 3 * units), F32)] * 2,
-        [x, w[0], w[2]],
-        2 * copies * per_pair,
-        me,
-    )
+    keep = pre((w[0], w[2]), F32)
     chip_in = swap((keep[1] + core_in[n:].astype(F32)).astype(BF16), CHIP)
     (h0,) = call(
         act_body, [sds((n, 3 * units), BF16)], [keep[0], core_in[:n], chip_in], 0
@@ -246,7 +253,9 @@
         2 * copies * per_pair,
         me,
     )
+    h2, acc, last = lax.optimization_barrier((h2, acc, x[n:]))
     h3 = swap(h2, CORE)
+    x_far = swap(last, CHIP)
     (result,) = call(
         functools.partial(result_body, False),
         [sds((copies * n, 2 * width), BF16)],
@@ -254,25 +263,19 @@
         2 * copies * per_pair,
         me,
     )
-    returned = lax.all_to_all(
-        result.reshape(copies * experts, capacity, 2 * width),
-        ("za", "expert"),
-        split_axis=0,
-        concat_axis=0,
-        tiled=True,
-    )
-    shares = call(
+    returned = there_and_back(result.reshape(copies * experts, capacity, 2 * width))
+    kept, share = call(
         weight_grads_body,
-        [sds((copies * width, 3 * units), BF16)] * quad,
-        [x, h0, h1, h2, h3],
-        quad * copies * per_pair,
+        [sds((4 * width, 3 * units), BF16)] * 2,
+        [x, x_near, x_far, h0, h1],
+        8 * per_pair,
         me,
     )
-    got = [s if h == 0 else swap(s, h) for h, s in zip(QUAD, shares)]
+    got = swap(share, CORE)
     gate_grad, up_grad, down_grad = call(
         merge_body,
         [sds((model, units), BF16), sds((model, units), BF16), sds((units, model), BF16)],
-        got,
+        [kept, got],
         0,
         me,
     )

time: 180 us -> 198 us (1.10)
  waiting for transfers between devices: 70.5 us -> 82.6 us
  local copies, waits for them, and re-layouts: 9.2 us -> 13.1 us
  Pallas kernels: 28.4 us -> 30.9 us
    ppermute x11, waiting for transfers between devices: 70.4 us -> 82.6 us  [swap(): return lax.ppermute(x, DP, [(j, j ^ mask) for j in range(8)])]
    slice x0 -> x7, local copies, waits for them, and re-layouts: none -> 3.03 us  [the longest x2 1.57 us: per_device(): w = {0: near[:cut], CORE: core_w, CHIP: chip_w[:cut], CHIP ^ CORE: relay_w}]
    pallas_call x10 -> x11, Pallas kernels: 28.4 us -> 30.9 us  [call(): pl.pallas_call(body, out_shape=outs, in_specs=[smem] * len(head) + [vmem]...]
  transfers between devices with their start and end apart: 13 -> 13, of which waited for: 6 -> 8; matrix products, arithmetic and copies ran while one was open for 1% -> 2% of each run, Pallas kernels for 8% -> 9%
where the time goes in v3:
time: 198 us; the launch traced here: 197 us
  waiting for transfers between devices  82.6 us (42%)
  starting transfers between devices  66.3 us (33%)
  Pallas kernels  30.9 us (16%)
  local copies, waits for them, and re-layouts  13.1 us (7%)
  other arithmetic  3.16 us (2%)
    ppermute x11, waiting for transfers between devices, swap(): return lax.ppermute(x, DP, [(j, j ^ mask) for j in range(8)])  82.6 us
    all_to_all x2, starting transfers between devices, there_and_back(): lax.all_to_all(a, ('za', 'expert'), split_axis=0, concat_axis=0, tiled=True)  35.8 us
    pallas_call x11, Pallas kernels, call(): pl.pallas_call(body, out_shape=outs, in_specs=[smem] * len(head) + [vmem]...  30.9 us
    ppermute x11, starting transfers between devices, swap(): return lax.ppermute(x, DP, [(j, j ^ mask) for j in range(8)])  30.5 us
    unnamed x23, local copies, waits for them, and re-layouts  4.63 us
  transfers between devices with their start and end apart: 13, of which 8 were waited for; matrix products, arithmetic and copies ran while one was open for 2% of the time, Pallas kernels for 9%

profile of v3, /device:TPU:1, one launch (start us, length us, event | category | flops | bytes accessed | tf_op | source)
XLA Modules:
  0.0 196.9 jit_solution(715571594296508136)
XLA Ops:
  0.6 2.5 %shard_map.110 = (bf16[1024,512]{1,0:T(8,128)(2,1)}, s32[2,160]{1,0:T(2,128)}) custom-call(s32[2,160]{1,0:T(2,128)} %bitcast.23, f32[2,160]{1,0:T(2,128)} %bitcast.19, bf16[160,256]{1,0:T(8,128)(2,1)} %tok_ref.1, bf16[160,256]{1,0:T(8,128)(2,1)} %grad_ref.1), custom_call_target="tpu_custom_call" | custom-call | flops 83886080 | bytes 1216256 | tf_op jit(solution)/shard_map/pallas_call | solution.py:28
  3.1 20.8 %all-to-all-start = ((bf16[128,8,512]{2,1,0:T(8,128)(2,1)}), bf16[128,8,512]{2,1,0:T(8,128)(2,1)S(1)}, u32[]{:S(2)}, u32[]{:S(2)}) async-start(bf16[128,8,512]{2,1,0:T(8,128)(2,1)} %bitcast.18), calls=%async_computation | async-start | bytes 2097152 | tf_op jit(solution)/shard_map/all_to_all | solution.py:219
  23.9 2.4 %shard_map.112 = bf16[1024,384]{1,0:T(8,128)(2,1)} custom-call(s32[1]{0:T(128)} %bitcast.2.me_ref, bf16[2048,128]{1,0:T(8,128)(2,1)} %bitcast.12, bf16[2048,128]{1,0:T(8,128)(2,1)} %bitcast.14, bf16[128,2048]{1,0:T(8,128)(2,1)} %bitcast.16), custom_call_target="tpu_custom_call" | custom-call | bytes 2359296 | tf_op jit(solution)/shard_map/pallas_call | solution.py:28
  26.3 3.1 %collective-permute-start.1 = (bf16[1024,384]{1,0:T(8,128)(2,1)}, bf16[1024,384]{1,0:T(8,128)(2,1)S(1)}, u32[]{:S(2)}, u32[]{:S(2)}) collective-permute-start(bf16[1024,384]{1,0:T(8,128)(2,1)} %shard_map.112), channel_id=1, source_target_pairs={{0,128},{64,192},{128,0},{192,64},{256,384},{320,448},{384,256},{4... | collective-permute-start | bytes 2359304 | tf_op jit(solution)/shard_map/ppermute | solution.py:202
  29.4 2.4 %shard_map.111 = bf16[1024,384]{1,0:T(8,128)(2,1)} custom-call(s32[1]{0:T(128)} %bitcast.2.me_ref, bf16[2048,128]{1,0:T(8,128)(2,1)} %bitcast.13, bf16[2048,128]{1,0:T(8,128)(2,1)} %bitcast.15, bf16[128,2048]{1,0:T(8,128)(2,1)} %bitcast.17), custom_call_target="tpu_custom_call" | custom-call | bytes 2359296 | tf_op jit(solution)/shard_map/pallas_call | solution.py:28
  32.8 3.1 %collective-permute-start = (bf16[512,384]{1,0:T(8,128)(2,1)S(1)}, bf16[512,384]{1,0:T(8,128)(2,1)S(1)}, u32[]{:S(2)}, u32[]{:S(2)}) collective-permute-start(bf16[512,384]{1,0:T(8,128)(2,1)S(1)} %slice.46), channel_id=1, source_target_pairs={{0,64},{64,0},{128,192},{192,128},{256,320},{320,256},{384,448},{4... | collective-permute-start | bytes 1179656 | tf_op jit(solution)/shard_map/ppermute | solution.py:202
  36.0 28.7 %collective-permute-done.1 = bf16[1024,384]{1,0:T(8,128)(2,1)S(1)} collective-permute-done((bf16[1024,384]{1,0:T(8,128)(2,1)}, bf16[1024,384]{1,0:T(8,128)(2,1)S(1)}, u32[]{:S(2)}, u32[]{:S(2)}) %collective-permute-start.1) | collective-permute-done | bytes 786464 | tf_op jit(solution)/shard_map/ppermute | solution.py:202
  64.8 2.7 %collective-permute-start.2 = (bf16[512,384]{1,0:T(8,128)(2,1)S(1)}, bf16[512,384]{1,0:T(8,128)(2,1)S(1)}, u32[]{:S(2)}, u32[]{:S(2)}) collective-permute-start(bf16[512,384]{1,0:T(8,128)(2,1)S(1)} %slice.47), channel_id=1, source_target_pairs={{0,64},{64,0},{128,192},{192,128},{256,320},{320,256},{384,448},{4... | collective-permute-start | bytes 1179656 | tf_op jit(solution)/shard_map/ppermute | solution.py:202
  70.0 2.8 %shard_map.114 = (bf16[448,384]{1,0:T(8,128)(2,1)}, bf16[448,384]{1,0:T(8,128)(2,1)}) custom-call(s32[1]{0:T(128)} %bitcast.2.me_ref, bf16[896,512]{1,0:T(8,128)(2,1)} %reshape.29.x_ref.own_ref, bf16[512,384]{1,0:T(8,128)(2,1)} %copy-done.2, bf16[512,384]{1,0:T(8,128)(2,1)} %copy-done.1), custom_call_target="tpu_custom_call" | custom-call | flops 352321536 | bytes 2392064 | tf_op jit(solution)/shard_map/pallas_call | solution.py:28
  72.9 2.0 %pad_maximum_fusion = bf16[896,384]{1,0:T(8,128)(2,1)} fusion(bf16[448,384]{1,0:T(8,128)(2,1)} %get-tuple-element.35, bf16[448,384]{1,0:T(8,128)(2,1)} %get-tuple-element.34), kind=kLoop, calls=%fused_computation | loop fusion | flops 1376256 | bytes 1376256 | tf_op jit(solution)/shard_map/concatenate | solution.py:241
  74.9 2.3 %collective-permute-start.3 = (bf16[896,384]{1,0:T(8,128)(2,1)}, bf16[896,384]{1,0:T(8,128)(2,1)S(1)}, u32[]{:S(2)}, u32[]{:S(2)}) collective-permute-start(bf16[896,384]{1,0:T(8,128)(2,1)} %pad_maximum_fusion), channel_id=1, source_target_pairs={{0,64},{64,0},{128,192},{192,128},{256,320},{320,256},{384,448},{4... | collective-permute-start | bytes 2064392 | tf_op jit(solution)/shard_map/ppermute | solution.py:202
  78.7 3.0 %shard_map.113 = (f32[448,384]{1,0:T(8,128)}, f32[448,384]{1,0:T(8,128)}) custom-call(s32[1]{0:T(128)} %bitcast.2.me_ref, bf16[896,512]{1,0:T(8,128)(2,1)} %reshape.29.x_ref.own_ref, bf16[512,384]{1,0:T(8,128)(2,1)} %slice.38.first_ref.refs_2_, bf16[512,384]{1,0:T(8,128)(2,1)} %slice.39.second_ref.refs_2_), custom_call_target="tpu_custom_call" | custom-call | flops 352321536 | bytes 3080192 | tf_op jit(solution)/shard_map/pallas_call | solution.py:28
  82.9 3.0 %collective-permute-start.4 = (bf16[448,384]{1,0:T(8,128)(2,1)S(1)}, bf16[448,384]{1,0:T(8,128)(2,1)S(1)}, u32[]{:S(2)}, u32[]{:S(2)}) collective-permute-start(bf16[448,384]{1,0:T(8,128)(2,1)S(1)} %add_convert_fusion), channel_id=1, source_target_pairs={{0,128},{64,192},{128,0},{192,64},{256,384},{320,448},{384,256},{4... | collective-permute-start | bytes 1032200 | tf_op jit(solution)/shard_map/ppermute | solution.py:202
  86.7 7.6 %collective-permute-done.4.chip_ref = bf16[448,384]{1,0:T(8,128)(2,1)S(1)} collective-permute-done((bf16[448,384]{1,0:T(8,128)(2,1)S(1)}, bf16[448,384]{1,0:T(8,128)(2,1)S(1)}, u32[]{:S(2)}, u32[]{:S(2)}) %collective-permute-start.4) | collective-permute-done | bytes 344096 | tf_op jit(solution)/shard_map/ppermute | solution.py:202
  95.0 2.2 %shard_map.115.refs_0_.h0_ref = bf16[448,384]{1,0:T(8,128)(2,1)} custom-call(f32[448,384]{1,0:T(8,128)} %get-tuple-element.31.keep_ref, bf16[448,384]{1,0:T(8,128)(2,1)} %slice.48.core_ref, bf16[448,384]{1,0:T(8,128)(2,1)} %copy-done.4), custom_call_target="tpu_custom_call" | custom-call | bytes 1720320 | tf_op jit(solution)/shard_map/pallas_call | solution.py:28
  97.2 2.9 %collective-permute-start.6 = (bf16[448,384]{1,0:T(8,128)(2,1)}, bf16[448,384]{1,0:T(8,128)(2,1)S(1)}, u32[]{:S(2)}, u32[]{:S(2)}) collective-permute-start(bf16[448,384]{1,0:T(8,128)(2,1)} %shard_map.115.refs_0_.h0_ref), channel_id=1, source_target_pairs={{0,64},{64,0},{128,192},{192,128},{256,320},{320,256},{384,448},{4... | collective-permute-start | bytes 1032200 | tf_op jit(solution)/shard_map/ppermute | solution.py:202
  100.1 3.0 %collective-permute-start.5 = (bf16[448,384]{1,0:T(8,128)(2,1)}, bf16[448,384]{1,0:T(8,128)(2,1)S(1)}, u32[]{:S(2)}, u32[]{:S(2)}) collective-permute-start(bf16[448,384]{1,0:T(8,128)(2,1)} %shard_map.115.refs_0_.h0_ref), channel_id=1, source_target_pairs={{0,128},{64,192},{128,0},{192,64},{256,384},{320,448},{384,256},{4... | collective-permute-start | bytes 1032200 | tf_op jit(solution)/shard_map/ppermute | solution.py:202
  104.1 3.1 %shard_map.116.refs_4_ = f32[896,512]{1,0:T(8,128)} custom-call(s32[1]{0:T(128)} %bitcast.2.me_ref, bf16[448,384]{1,0:T(8,128)(2,1)} %shard_map.115.refs_0_.h0_ref, bf16[448,384]{1,0:T(8,128)(2,1)} %copy-done.5, bf16[512,384]{1,0:T(8,128)(2,1)} %slice.38.first_ref.refs_2_, bf16[512,384]{1,0:T(8,128)(2,1)} %copy-done.2), custom_call_target="tpu_custom_call" | custom-call | flops 352321536 | bytes 3309568 | tf_op jit(solution)/shard_map/pallas_call | solution.py:28
  107.2 4.6 %collective-permute-done.5.refs_0_ = bf16[448,384]{1,0:T(8,128)(2,1)S(1)} collective-permute-done((bf16[448,384]{1,0:T(8,128)(2,1)}, bf16[448,384]{1,0:T(8,128)(2,1)S(1)}, u32[]{:S(2)}, u32[]{:S(2)}) %collective-permute-start.5) | collective-permute-done | bytes 344096 | tf_op jit(solution)/shard_map/ppermute | solution.py:202
  111.9 2.8 %collective-permute-start.7 = (bf16[448,384]{1,0:T(8,128)(2,1)S(1)}, bf16[448,384]{1,0:T(8,128)(2,1)S(1)}, u32[]{:S(2)}, u32[]{:S(2)}) collective-permute-start(bf16[448,384]{1,0:T(8,128)(2,1)S(1)} %collective-permute-done.5.refs_0_), channel_id=1, source_target_pairs={{0,64},{64,0},{128,192},{192,128},{256,320},{320,256},{384,448},{4... | collective-permute-start | bytes 1032200 | tf_op jit(solution)/shard_map/ppermute | solution.py:202
  116.6 3.5 %shard_map.117 = bf16[896,512]{1,0:T(8,128)(2,1)} custom-call(s32[1]{0:T(128)} %bitcast.2.me_ref, bf16[448,384]{1,0:T(8,128)(2,1)} %copy-done.6, bf16[448,384]{1,0:T(8,128)(2,1)} %copy-done.7, bf16[512,384]{1,0:T(8,128)(2,1)} %slice.39.second_ref.refs_2_, bf16[512,384]{1,0:T(8,128)(2,1)} %copy-done.1, f32[896,512]{1,0:T(8,128)} %shard_map.116.refs_4_), custom_call_target="tpu_custom_call" | custom-call | flops 352321536 | bytes 4227072 | tf_op jit(solution)/shard_map/pallas_call | solution.py:28
  120.1 2.2 %reshape.30 = bf16[128,7,512]{2,1,0:T(8,128)(2,1)} reshape(bf16[896,512]{1,0:T(8,128)(2,1)} %shard_map.117) | data formatting | bytes 1835008 | tf_op jit(solution)/shard_map/reshape | solution.py:266
  122.3 15.0 %all-to-all-start.1 = ((bf16[128,7,512]{2,1,0:T(8,128)(2,1)}), bf16[128,7,512]{2,1,0:T(8,128)(2,1)S(1)}, u32[]{:S(2)}, u32[]{:S(2)}) async-start(bf16[128,7,512]{2,1,0:T(8,128)(2,1)} %reshape.30), calls=%async_computation.1 | async-start | bytes 2097152 | tf_op jit(solution)/shard_map/all_to_all | solution.py:219
  137.5 2.4 %collective-permute-start.8 = (bf16[448,512]{1,0:T(8,128)(2,1)S(1)}, bf16[448,512]{1,0:T(8,128)(2,1)S(1)}, u32[]{:S(2)}, u32[]{:S(2)}) collective-permute-start(bf16[448,512]{1,0:T(8,128)(2,1)S(1)} %slice.45), channel_id=1, source_target_pairs={{0,128},{64,192},{128,0},{192,64},{256,384},{320,448},{384,256},{4... | collective-permute-start | bytes 1376264 | tf_op jit(solution)/shard_map/ppermute | solution.py:202
  139.9 2.9 %collective-permute-start.9 = (bf16[448,512]{1,0:T(8,128)(2,1)S(1)}, bf16[448,512]{1,0:T(8,128)(2,1)S(1)}, u32[]{:S(2)}, u32[]{:S(2)}) collective-permute-start(bf16[448,512]{1,0:T(8,128)(2,1)S(1)} %slice.43), channel_id=1, source_target_pairs={{0,128},{64,192},{128,0},{192,64},{256,384},{320,448},{384,256},{4... | collective-permute-start | bytes 1376264 | tf_op jit(solution)/shard_map/ppermute | solution.py:202
  142.8 27.9 %collective-permute-done.8.near_ref = bf16[448,512]{1,0:T(8,128)(2,1)S(1)} collective-permute-done((bf16[448,512]{1,0:T(8,128)(2,1)S(1)}, bf16[448,512]{1,0:T(8,128)(2,1)S(1)}, u32[]{:S(2)}, u32[]{:S(2)}) %collective-permute-start.8) | collective-permute-done | bytes 458784 | tf_op jit(solution)/shard_map/ppermute | solution.py:202
  170.6 9.8 %collective-permute-done.9.far_ref = bf16[448,512]{1,0:T(8,128)(2,1)S(1)} collective-permute-done((bf16[448,512]{1,0:T(8,128)(2,1)S(1)}, bf16[448,512]{1,0:T(8,128)(2,1)S(1)}, u32[]{:S(2)}, u32[]{:S(2)}) %collective-permute-start.9) | collective-permute-done | bytes 458784 | tf_op jit(solution)/shard_map/ppermute | solution.py:202
  181.2 3.8 %shard_map.119 = (bf16[1024,384]{1,0:T(8,128)(2,1)}, bf16[1024,384]{1,0:T(8,128)(2,1)}) custom-call(s32[1]{0:T(128)} %bitcast.2.me_ref, bf16[896,512]{1,0:T(8,128)(2,1)} %reshape.29.x_ref.own_ref, bf16[448,512]{1,0:T(8,128)(2,1)} %copy-done.9, bf16[448,512]{1,0:T(8,128)(2,1)} %copy-done.10, bf16[448,384]{1,0:T(8,128)(2,1)} %shard_map.115.refs_0_.h0_ref, ...), custom_call_target="tpu_custom_call" | custom-call | flops 704643072 | bytes 4096000 | tf_op jit(solution)/shard_map/pallas_call | solution.py:28
  185.0 2.4 %collective-permute-start.10 = (bf16[1024,384]{1,0:T(8,128)(2,1)}, bf16[1024,384]{1,0:T(8,128)(2,1)S(1)}, u32[]{:S(2)}, u32[]{:S(2)}) collective-permute-start(bf16[1024,384]{1,0:T(8,128)(2,1)} %get-tuple-element.43), channel_id=1, source_target_pairs={{0,64},{64,0},{128,192},{192,128},{256,320},{320,256},{384,448},{4... | collective-permute-start | bytes 2359304 | tf_op jit(solution)/shard_map/ppermute | solution.py:202
  188.3 1.3 collective-permute-done.10.got_ref
  190.5 2.7 %shard_map.120 = (bf16[2048,128]{1,0:T(8,128)(2,1)}, bf16[2048,128]{1,0:T(8,128)(2,1)}, bf16[128,2048]{1,0:T(8,128)(2,1)}) custom-call(s32[1]{0:T(128)} %bitcast.2.me_ref, bf16[1024,384]{1,0:T(8,128)(2,1)} %get-tuple-element.42.keep_ref, bf16[1024,384]{1,0:T(8,128)(2,1)} %copy-done.3), custom_call_target="tpu_custom_call" | custom-call | bytes 3145728 | tf_op jit(solution)/shard_map/pallas_call | solution.py:28
  194.4 2.4 %shard_map.118 = (bf16[160,256]{1,0:T(8,128)(2,1)}, bf16[160,256]{1,0:T(8,128)(2,1)}) custom-call(s32[2,160]{1,0:T(2,128)} %get-tuple-element.26.pos_ref, f32[160,2]{1,0:T(8,128)} %copy.13.probs_ref, bf16[896,512]{1,0:T(8,128)(2,1)} %reshape.31.back_ref), custom_call_target="tpu_custom_call" | custom-call | flops 293601280 | bytes 1083904 | tf_op jit(solution)/shard_map/pallas_call | solution.py:28
  (41 shorter events, 14.6 us)
Async XLA Ops:
  3.1 65.7 %all-to-all-start = ((bf16[128,8,512]{2,1,0:T(8,128)(2,1)}), bf16[128,8,512]{2,1,0:T(8,128)(2,1)S(1)}, u32[]{:S(2)}, u32[]{:S(2)}) async-start(bf16[128,8,512]{2,1,0:T(8,128)(2,1)} %bitcast.18), calls=%async_computation | async-start | bytes 2097152 | tf_op jit(solution)/shard_map/all_to_all | solution.py:219
  26.3 38.4 %collective-permute-start.1 = (bf16[1024,384]{1,0:T(8,128)(2,1)}, bf16[1024,384]{1,0:T(8,128)(2,1)S(1)}, u32[]{:S(2)}, u32[]{:S(2)}) collective-permute-start(bf16[1024,384]{1,0:T(8,128)(2,1)} %shard_map.112), channel_id=1, source_target_pairs={{0,128},{64,192},{128,0},{192,64},{256,384},{320,448},{384,256},{4... | collective-permute-start | bytes 2359304 | tf_op jit(solution)/shard_map/ppermute | solution.py:202
  32.8 34.6 %collective-permute-start = (bf16[512,384]{1,0:T(8,128)(2,1)S(1)}, bf16[512,384]{1,0:T(8,128)(2,1)S(1)}, u32[]{:S(2)}, u32[]{:S(2)}) collective-permute-start(bf16[512,384]{1,0:T(8,128)(2,1)S(1)} %slice.46), channel_id=1, source_target_pairs={{0,64},{64,0},{128,192},{192,128},{256,320},{320,256},{384,448},{4... | collective-permute-start | bytes 1179656 | tf_op jit(solution)/shard_map/ppermute | solution.py:202
  64.8 4.0 %collective-permute-start.2 = (bf16[512,384]{1,0:T(8,128)(2,1)S(1)}, bf16[512,384]{1,0:T(8,128)(2,1)S(1)}, u32[]{:S(2)}, u32[]{:S(2)}) collective-permute-start(bf16[512,384]{1,0:T(8,128)(2,1)S(1)} %slice.47), channel_id=1, source_target_pairs={{0,64},{64,0},{128,192},{192,128},{256,320},{320,256},{384,448},{4... | collective-permute-start | bytes 1179656 | tf_op jit(solution)/shard_map/ppermute | solution.py:202
  67.5 2.6 %copy-start.2 = (bf16[512,384]{1,0:T(8,128)(2,1)}, bf16[512,384]{1,0:T(8,128)(2,1)S(1)}, u32[]{:S(2)}) copy-start(bf16[512,384]{1,0:T(8,128)(2,1)S(1)} %collective-permute-done.first_ref.refs_3_) | copy-start | bytes 1179652
  68.8 1.2 copy-start.1
  70.0 7.1 %copy-start = (bf16[1024,384]{1,0:T(8,128)(2,1)S(1)}, bf16[1024,384]{1,0:T(8,128)(2,1)}, u32[]{:S(2)}) copy-start(bf16[1024,384]{1,0:T(8,128)(2,1)} %shard_map.111) | copy-start | bytes 2359300
  74.9 6.9 %collective-permute-start.3 = (bf16[896,384]{1,0:T(8,128)(2,1)}, bf16[896,384]{1,0:T(8,128)(2,1)S(1)}, u32[]{:S(2)}, u32[]{:S(2)}) collective-permute-start(bf16[896,384]{1,0:T(8,128)(2,1)} %pad_maximum_fusion), channel_id=1, source_target_pairs={{0,64},{64,0},{128,192},{192,128},{256,320},{320,256},{384,448},{4... | collective-permute-start | bytes 2064392 | tf_op jit(solution)/shard_map/ppermute | solution.py:202
  82.9 11.4 %collective-permute-start.4 = (bf16[448,384]{1,0:T(8,128)(2,1)S(1)}, bf16[448,384]{1,0:T(8,128)(2,1)S(1)}, u32[]{:S(2)}, u32[]{:S(2)}) collective-permute-start(bf16[448,384]{1,0:T(8,128)(2,1)S(1)} %add_convert_fusion), channel_id=1, source_target_pairs={{0,128},{64,192},{128,0},{192,64},{256,384},{320,448},{384,256},{4... | collective-permute-start | bytes 1032200 | tf_op jit(solution)/shard_map/ppermute | solution.py:202
  94.3 0.7 copy-start.4
  97.2 6.1 %collective-permute-start.6 = (bf16[448,384]{1,0:T(8,128)(2,1)}, bf16[448,384]{1,0:T(8,128)(2,1)S(1)}, u32[]{:S(2)}, u32[]{:S(2)}) collective-permute-start(bf16[448,384]{1,0:T(8,128)(2,1)} %shard_map.115.refs_0_.h0_ref), channel_id=1, source_target_pairs={{0,64},{64,0},{128,192},{192,128},{256,320},{320,256},{384,448},{4... | collective-permute-start | bytes 1032200 | tf_op jit(solution)/shard_map/ppermute | solution.py:202
  100.1 11.7 %collective-permute-start.5 = (bf16[448,384]{1,0:T(8,128)(2,1)}, bf16[448,384]{1,0:T(8,128)(2,1)S(1)}, u32[]{:S(2)}, u32[]{:S(2)}) collective-permute-start(bf16[448,384]{1,0:T(8,128)(2,1)} %shard_map.115.refs_0_.h0_ref), channel_id=1, source_target_pairs={{0,128},{64,192},{128,0},{192,64},{256,384},{320,448},{384,256},{4... | collective-permute-start | bytes 1032200 | tf_op jit(solution)/shard_map/ppermute | solution.py:202
  103.4 0.7 copy-start.5
  111.9 4.0 %copy-start.6 = (bf16[448,384]{1,0:T(8,128)(2,1)}, bf16[448,384]{1,0:T(8,128)(2,1)S(1)}, u32[]{:S(2)}) copy-start(bf16[448,384]{1,0:T(8,128)(2,1)S(1)} %collective-permute-done.5.refs_0_) | copy-start | bytes 1032196
  111.9 4.0 %collective-permute-start.7 = (bf16[448,384]{1,0:T(8,128)(2,1)S(1)}, bf16[448,384]{1,0:T(8,128)(2,1)S(1)}, u32[]{:S(2)}, u32[]{:S(2)}) collective-permute-start(bf16[448,384]{1,0:T(8,128)(2,1)S(1)} %collective-permute-done.5.refs_0_), channel_id=1, source_target_pairs={{0,64},{64,0},{128,192},{192,128},{256,320},{320,256},{384,448},{4... | collective-permute-start | bytes 1032200 | tf_op jit(solution)/shard_map/ppermute | solution.py:202
  115.9 0.7 copy-start.7
  122.3 70.9 %all-to-all-start.1 = ((bf16[128,7,512]{2,1,0:T(8,128)(2,1)}), bf16[128,7,512]{2,1,0:T(8,128)(2,1)S(1)}, u32[]{:S(2)}, u32[]{:S(2)}) async-start(bf16[128,7,512]{2,1,0:T(8,128)(2,1)} %reshape.30), calls=%async_computation.1 | async-start | bytes 2097152 | tf_op jit(solution)/shard_map/all_to_all | solution.py:219
  137.5 50.0 %copy-start.8 = (f32[160,2]{0,1:T(2,128)S(1)}, f32[160,2]{0,1:T(2,128)}, u32[]{:S(2)}) copy-start(f32[160,2]{0,1:T(2,128)} %param.10) | copy-start | bytes 3844
  137.5 33.2 %collective-permute-start.8 = (bf16[448,512]{1,0:T(8,128)(2,1)S(1)}, bf16[448,512]{1,0:T(8,128)(2,1)S(1)}, u32[]{:S(2)}, u32[]{:S(2)}) collective-permute-start(bf16[448,512]{1,0:T(8,128)(2,1)S(1)} %slice.45), channel_id=1, source_target_pairs={{0,128},{64,192},{128,0},{192,64},{256,384},{320,448},{384,256},{4... | collective-permute-start | bytes 1376264 | tf_op jit(solution)/shard_map/ppermute | solution.py:202
  139.9 40.6 %collective-permute-start.9 = (bf16[448,512]{1,0:T(8,128)(2,1)S(1)}, bf16[448,512]{1,0:T(8,128)(2,1)S(1)}, u32[]{:S(2)}, u32[]{:S(2)}) collective-permute-start(bf16[448,512]{1,0:T(8,128)(2,1)S(1)} %slice.43), channel_id=1, source_target_pairs={{0,128},{64,192},{128,0},{192,64},{256,384},{320,448},{384,256},{4... | collective-permute-start | bytes 1376264 | tf_op jit(solution)/shard_map/ppermute | solution.py:202
  170.6 9.8 %copy-start.9 = (bf16[448,512]{1,0:T(8,128)(2,1)}, bf16[448,512]{1,0:T(8,128)(2,1)S(1)}, u32[]{:S(2)}) copy-start(bf16[448,512]{1,0:T(8,128)(2,1)S(1)} %collective-permute-done.8.near_ref) | copy-start | bytes 1376260
  180.5 0.8 copy-start.10
  185.0 4.5 %collective-permute-start.10 = (bf16[1024,384]{1,0:T(8,128)(2,1)}, bf16[1024,384]{1,0:T(8,128)(2,1)S(1)}, u32[]{:S(2)}, u32[]{:S(2)}) collective-permute-start(bf16[1024,384]{1,0:T(8,128)(2,1)} %get-tuple-element.43), channel_id=1, source_target_pairs={{0,64},{64,0},{128,192},{192,128},{256,320},{320,256},{384,448},{4... | collective-permute-start | bytes 2359304 | tf_op jit(solution)/shard_map/ppermute | solution.py:202
  189.6 0.9 copy-start.3

commit v4 on v3

--- a/solution.py
+++ b/solution.py
@@ -31,6 +31,7 @@
         in_specs=[smem] * len(head) + [vmem] * len(args),
         out_specs=[vmem] * len(outs),
         cost_estimate=pl.CostEstimate(flops=flops, bytes_accessed=moved, transcendentals=0),
+        compiler_params=pltpu.CompilerParams(vmem_limit_bytes=16 << 20),
     )(*head, *args)
 
 
@@ -115,14 +116,16 @@
             pres[j] = pres[j] + dot(x, ref[w, : 2 * units])
         downs = jnp.concatenate([first_ref[w, 2 * units :], second_ref[w, 2 * units :]], axis=1)
         hids = hids + dot(g, downs)
-    for j, ref in enumerate(out_refs):
-        ref[:, : 2 * units] = pres[j].astype(ref.dtype)
-        ref[:, 2 * units :] = hids[:, j * units : (j + 1) * units].astype(ref.dtype)
+    for j in range(2):
+        ref, at = (out_refs[0], pl.ds(j * n, n)) if len(out_refs) == 1 else (out_refs[j], pl.ds(0, n))
+        ref[at, : 2 * units] = pres[j].astype(ref.dtype)
+        ref[at, 2 * units :] = hids[:, j * units : (j + 1) * units].astype(ref.dtype)
 
 
 def act_body(keep_ref, core_ref, chip_ref, out_ref):
     units = keep_ref.shape[1] // 3
-    pre = keep_ref[...] + core_ref[...].astype(F32) + chip_ref[...].astype(F32)
+    n = keep_ref.shape[0]
+    pre = keep_ref[...] + core_ref[pl.ds(0, n), :].astype(F32) + chip_ref[...].astype(F32)
     gate, up, hid = pre[:, :units], pre[:, units : 2 * units], pre[:, 2 * units :]
     sig = jax.nn.sigmoid(gate)
     silu = gate * sig
@@ -136,7 +139,7 @@
     acc_ref, out_ref = (None, refs[4]) if first else (refs[4], refs[5])
     n = h_refs[0].shape[0]
     units = h_refs[0].shape[1] // 3
-    width = w_refs[0].shape[0] // len(FEATURES)
+    width = out_ref.shape[1] // 2
     hidden = jnp.concatenate([h[:, :units] for h in h_refs], axis=1)
     grads = jnp.concatenate([h[:, units:] for h in h_refs], axis=1)
     for i in range(len(FEATURES)):
@@ -210,10 +213,8 @@
             me,
         )[0]
 
-    def pre(weights, dtype):
-        return call(
-            pre_body, [sds((n, 3 * units), dtype)] * 2, [x, *weights], 2 * copies * per_pair, me
-        )
+    def pre(weights, outs):
+        return call(pre_body, outs, [x, *weights], 2 * copies * per_pair, me)
 
     def there_and_back(a):
         return lax.all_to_all(a, ("za", "expert"), split_axis=0, concat_axis=0, tiled=True)
@@ -233,17 +234,15 @@
     filled, near, core_w, chip_w, relay_w = lax.optimization_barrier(
         (filled, near, core_w, chip_w, relay_w)
     )
-    w = {0: near[:cut], CORE: core_w, CHIP: chip_w[:cut], CHIP ^ CORE: relay_w}
+    w = {0: near, CORE: core_w, CHIP: chip_w, CHIP ^ CORE: relay_w}
     x = filled[:, :capacity].reshape(copies * n, 2 * width)
     x_near = swap(x[:n], CHIP)
 
-    core_out = pre((w[1], w[3]), BF16)
-    core_in = swap(jnp.concatenate(core_out, axis=0), CORE)
-    keep = pre((w[0], w[2]), F32)
+    (core_out,) = pre((w[1], w[3]), [sds((2 * n, 3 * units), BF16)])
+    core_in = swap(core_out, CORE)
+    keep = pre((w[0], w[2]), [sds((n, 3 * units), F32)] * 2)
     chip_in = swap((keep[1] + core_in[n:].astype(F32)).astype(BF16), CHIP)
-    (h0,) = call(
-        act_body, [sds((n, 3 * units), BF16)], [keep[0], core_in[:n], chip_in], 0
-    )
+    (h0,) = call(act_body, [sds((n, 3 * units), BF16)], [keep[0], core_in, chip_in], 0)
     h2 = swap(h0, CHIP)
     h1 = swap(h0, CORE)
     (acc,) = call(

time: 198 us -> 180 us (0.909)
  Pallas kernels: 30.9 us -> 10.8 us
  waiting for transfers between devices: 82.6 us -> 88.2 us
  other arithmetic: 3.16 us -> 0.07 us
    pallas_call x11, Pallas kernels: 30.9 us -> 10.8 us  [call(): pl.pallas_call(body, out_shape=outs, in_specs=[smem] * len(head) + [vmem]...]
    ppermute x11, waiting for transfers between devices: 82.6 us -> 88.2 us  [swap(): return lax.ppermute(x, DP, [(j, j ^ mask) for j in range(8)])]
    slice x3 -> x0, local copies, waits for them, and re-layouts: 2.33 us -> none  [the longest x2 1.57 us: per_device(): w = {0: near[:cut], CORE: core_w, CHIP: chip_w[:cut], CHIP ^ CORE: relay_w}]
    slice x2, local copies, waits for them, and re-layouts: 0.23 us -> 2.39 us  [per_device(): x_near = swap(x[:n], CHIP)]
    concatenate x1 -> x0, other arithmetic: 2 us -> none  [per_device(): core_in = swap(jnp.concatenate(core_out, axis=0), CORE)]
    unnamed x23 -> x29, local copies, waits for them, and re-layouts: 4.63 us -> 3.4 us
  transfers between devices with their start and end apart: 13 -> 13, of which waited for: 8 -> 9; matrix products, arithmetic and copies ran while one was open for 2% -> 3% of each run, Pallas kernels for 9% -> 3%
where the time goes in v4:
time: 180 us
  waiting for transfers between devices  88.2 us (49%)
  starting transfers between devices  67.4 us (37%)
  local copies, waits for them, and re-layouts  12.1 us (7%)
  Pallas kernels  10.8 us (6%)
    ppermute x11, waiting for transfers between devices, swap(): return lax.ppermute(x, DP, [(j, j ^ mask) for j in range(8)])  88.2 us
    all_to_all x2, starting transfers between devices, there_and_back(): lax.all_to_all(a, ('za', 'expert'), split_axis=0, concat_axis=0, tiled=True)  36.9 us
    ppermute x11, starting transfers between devices, swap(): return lax.ppermute(x, DP, [(j, j ^ mask) for j in range(8)])  30.5 us
    pallas_call x11, Pallas kernels, call(): pl.pallas_call(body, out_shape=outs, in_specs=[smem] * len(head) + [vmem]...  10.8 us
  transfers between devices with their start and end apart: 13, of which 9 were waited for; matrix products, arithmetic and copies ran while one was open for 3% of the time, Pallas kernels for 3%

profile of v4, /device:TPU:1, one launch (start us, length us, event | category | flops | bytes accessed | tf_op | source)
XLA Modules:
  0.0 179.6 jit_solution(13832324780736479761)
XLA Ops:
  3.9 1.5 shard_map.110
  5.4 21.3 %all-to-all-start = ((bf16[128,8,512]{2,1,0:T(8,128)(2,1)}), bf16[128,8,512]{2,1,0:T(8,128)(2,1)}, u32[]{:S(2)}, u32[]{:S(2)}) async-start(bf16[128,8,512]{2,1,0:T(8,128)(2,1)} %bitcast.3), calls=%async_computation | async-start | bytes 2097152 | tf_op jit(solution)/shard_map/all_to_all | solution.py:220
  27.0 3.1 %collective-permute-start.1 = (bf16[1024,384]{1,0:T(8,128)(2,1)S(1)}, bf16[1024,384]{1,0:T(8,128)(2,1)S(1)}, u32[]{:S(2)}, u32[]{:S(2)}) collective-permute-start(bf16[1024,384]{1,0:T(8,128)(2,1)S(1)} %shard_map.112), channel_id=1, source_target_pairs={{0,128},{64,192},{128,0},{192,64},{256,384},{320,448},{384,256},{4... | collective-permute-start | bytes 2359304 | tf_op jit(solution)/shard_map/ppermute | solution.py:205
  30.3 3.1 %collective-permute-start = (bf16[512,384]{1,0:T(8,128)(2,1)S(1)}, bf16[512,384]{1,0:T(8,128)(2,1)S(1)}, u32[]{:S(2)}, u32[]{:S(2)}) collective-permute-start(bf16[512,384]{1,0:T(8,128)(2,1)S(1)} %slice.34), channel_id=1, source_target_pairs={{0,64},{64,0},{128,192},{192,128},{256,320},{320,256},{384,448},{4... | collective-permute-start | bytes 1179656 | tf_op jit(solution)/shard_map/ppermute | solution.py:205
  33.5 33.7 %collective-permute-done.1.second_ref.refs_2_ = bf16[1024,384]{1,0:T(8,128)(2,1)S(1)} collective-permute-done((bf16[1024,384]{1,0:T(8,128)(2,1)S(1)}, bf16[1024,384]{1,0:T(8,128)(2,1)S(1)}, u32[]{:S(2)}, u32[]{:S(2)}) %collective-permute-start.1) | collective-permute-done | bytes 786464 | tf_op jit(solution)/shard_map/ppermute | solution.py:205
  67.2 2.8 %collective-permute-start.2 = (bf16[512,384]{1,0:T(8,128)(2,1)S(1)}, bf16[512,384]{1,0:T(8,128)(2,1)S(1)}, u32[]{:S(2)}, u32[]{:S(2)}) collective-permute-start(bf16[512,384]{1,0:T(8,128)(2,1)S(1)} %slice.35), channel_id=1, source_target_pairs={{0,64},{64,0},{128,192},{192,128},{256,320},{320,256},{384,448},{4... | collective-permute-start | bytes 1179656 | tf_op jit(solution)/shard_map/ppermute | solution.py:205
  70.0 1.3 collective-permute-done.2.second_ref.refs_3_
  71.3 1.6 reshape.29.x_ref.own_ref
  73.5 2.3 %collective-permute-start.3 = (bf16[896,384]{1,0:T(8,128)(2,1)S(1)}, bf16[896,384]{1,0:T(8,128)(2,1)S(1)}, u32[]{:S(2)}, u32[]{:S(2)}) collective-permute-start(bf16[896,384]{1,0:T(8,128)(2,1)S(1)} %shard_map.114), channel_id=1, source_target_pairs={{0,64},{64,0},{128,192},{192,128},{256,320},{320,256},{384,448},{4... | collective-permute-start | bytes 2064392 | tf_op jit(solution)/shard_map/ppermute | solution.py:205
  76.3 1.2 collective-permute-done.3.core_ref
  77.6 2.7 %collective-permute-start.4 = (bf16[448,384]{1,0:T(8,128)(2,1)S(1)}, bf16[448,384]{1,0:T(8,128)(2,1)S(1)}, u32[]{:S(2)}, u32[]{:S(2)}) collective-permute-start(bf16[448,384]{1,0:T(8,128)(2,1)S(1)} %add_convert_fusion), channel_id=1, source_target_pairs={{0,128},{64,192},{128,0},{192,64},{256,384},{320,448},{384,256},{4... | collective-permute-start | bytes 1032200 | tf_op jit(solution)/shard_map/ppermute | solution.py:205
  80.3 8.4 %collective-permute-done.4.chip_ref = bf16[448,384]{1,0:T(8,128)(2,1)S(1)} collective-permute-done((bf16[448,384]{1,0:T(8,128)(2,1)S(1)}, bf16[448,384]{1,0:T(8,128)(2,1)S(1)}, u32[]{:S(2)}, u32[]{:S(2)}) %collective-permute-start.4) | collective-permute-done | bytes 344096 | tf_op jit(solution)/shard_map/ppermute | solution.py:205
  89.0 3.1 %collective-permute-start.6 = (bf16[448,384]{1,0:T(8,128)(2,1)S(1)}, bf16[448,384]{1,0:T(8,128)(2,1)}, u32[]{:S(2)}, u32[]{:S(2)}) collective-permute-start(bf16[448,384]{1,0:T(8,128)(2,1)S(1)} %shard_map.115.refs_0_.h0_ref), channel_id=1, source_target_pairs={{0,64},{64,0},{128,192},{192,128},{256,320},{320,256},{384,448},{4... | collective-permute-start | bytes 1032200 | tf_op jit(solution)/shard_map/ppermute | solution.py:205
  92.1 2.7 %collective-permute-start.5 = (bf16[448,384]{1,0:T(8,128)(2,1)S(1)}, bf16[448,384]{1,0:T(8,128)(2,1)}, u32[]{:S(2)}, u32[]{:S(2)}) collective-permute-start(bf16[448,384]{1,0:T(8,128)(2,1)S(1)} %shard_map.115.refs_0_.h0_ref), channel_id=1, source_target_pairs={{0,128},{64,192},{128,0},{192,64},{256,384},{320,448},{384,256},{4... | collective-permute-start | bytes 1032200 | tf_op jit(solution)/shard_map/ppermute | solution.py:205
  94.8 2.2 %fusion = (bf16[64,7,512]{2,1,0:T(8,128)(2,1)}, bf16[64,7,512]{2,1,0:T(8,128)(2,1)}) fusion(bf16[128,8,512]{2,1,0:T(8,128)(2,1)} %all-to-all-done), kind=kLoop, calls=%fused_computation.1 | loop fusion | bytes 1835008 | tf_op jit(solution)/shard_map/slice | solution.py:239
  97.0 2.0 %slice.31 = bf16[448,512]{1,0:T(8,128)(2,1)} reshape(bf16[64,7,512]{2,1,0:T(8,128)(2,1)} %get-tuple-element.44) | data formatting | bytes 917504 | tf_op jit(solution)/shard_map/slice | solution.py:255
  99.0 1.6 shard_map.116.refs_4_
  100.6 3.1 %collective-permute-done.5.refs_0_ = bf16[448,384]{1,0:T(8,128)(2,1)} collective-permute-done((bf16[448,384]{1,0:T(8,128)(2,1)S(1)}, bf16[448,384]{1,0:T(8,128)(2,1)}, u32[]{:S(2)}, u32[]{:S(2)}) %collective-permute-start.5) | collective-permute-done | bytes 344096 | tf_op jit(solution)/shard_map/ppermute | solution.py:205
  103.7 2.8 %collective-permute-start.7 = (bf16[448,384]{1,0:T(8,128)(2,1)}, bf16[448,384]{1,0:T(8,128)(2,1)S(1)}, u32[]{:S(2)}, u32[]{:S(2)}) collective-permute-start(bf16[448,384]{1,0:T(8,128)(2,1)} %collective-permute-done.5.refs_0_), channel_id=1, source_target_pairs={{0,64},{64,0},{128,192},{192,128},{256,320},{320,256},{384,448},{4... | collective-permute-start | bytes 1032200 | tf_op jit(solution)/shard_map/ppermute | solution.py:205
  106.5 1.5 collective-permute-done.7.refs_1_
  108.0 1.5 shard_map.117
  109.5 1.3 reshape.30
  110.8 15.5 %all-to-all-start.1 = ((bf16[128,7,512]{2,1,0:T(8,128)(2,1)}), bf16[128,7,512]{2,1,0:T(8,128)(2,1)}, u32[]{:S(2)}, u32[]{:S(2)}) async-start(bf16[128,7,512]{2,1,0:T(8,128)(2,1)} %reshape.30), calls=%async_computation.1 | async-start | bytes 2097152 | tf_op jit(solution)/shard_map/all_to_all | solution.py:220
  126.5 2.3 %collective-permute-start.8 = (bf16[448,512]{1,0:T(8,128)(2,1)S(1)}, bf16[448,512]{1,0:T(8,128)(2,1)S(1)}, u32[]{:S(2)}, u32[]{:S(2)}) collective-permute-start(bf16[448,512]{1,0:T(8,128)(2,1)S(1)} %slice.33), channel_id=1, source_target_pairs={{0,128},{64,192},{128,0},{192,64},{256,384},{320,448},{384,256},{4... | collective-permute-start | bytes 1376264 | tf_op jit(solution)/shard_map/ppermute | solution.py:205
  128.9 2.9 %collective-permute-start.9 = (bf16[448,512]{1,0:T(8,128)(2,1)S(1)}, bf16[448,512]{1,0:T(8,128)(2,1)S(1)}, u32[]{:S(2)}, u32[]{:S(2)}) collective-permute-start(bf16[448,512]{1,0:T(8,128)(2,1)S(1)} %copy-done.13), channel_id=1, source_target_pairs={{0,128},{64,192},{128,0},{192,64},{256,384},{320,448},{384,256},{4... | collective-permute-start | bytes 1376264 | tf_op jit(solution)/shard_map/ppermute | solution.py:205
  131.8 27.4 %collective-permute-done.8.near_ref = bf16[448,512]{1,0:T(8,128)(2,1)S(1)} collective-permute-done((bf16[448,512]{1,0:T(8,128)(2,1)S(1)}, bf16[448,512]{1,0:T(8,128)(2,1)S(1)}, u32[]{:S(2)}, u32[]{:S(2)}) %collective-permute-start.8) | collective-permute-done | bytes 458784 | tf_op jit(solution)/shard_map/ppermute | solution.py:205
  159.2 9.8 %collective-permute-done.9.far_ref = bf16[448,512]{1,0:T(8,128)(2,1)S(1)} collective-permute-done((bf16[448,512]{1,0:T(8,128)(2,1)S(1)}, bf16[448,512]{1,0:T(8,128)(2,1)S(1)}, u32[]{:S(2)}, u32[]{:S(2)}) %collective-permute-start.9) | collective-permute-done | bytes 458784 | tf_op jit(solution)/shard_map/ppermute | solution.py:205
  169.0 2.0 %shard_map.119 = (bf16[1024,384]{1,0:T(8,128)(2,1)S(1)}, bf16[1024,384]{1,0:T(8,128)(2,1)S(1)}) custom-call(s32[1]{0:T(128)} %bitcast.2.me_ref, bf16[896,512]{1,0:T(8,128)(2,1)S(1)} %reshape.29.x_ref.own_ref, bf16[448,512]{1,0:T(8,128)(2,1)S(1)} %collective-permute-done.8.near_ref, bf16[448,512]{1,0:T(8,128)(2,1)S(1)} %collective-permute-done.9.far_ref, ...), custom_call_target="tpu_custom_call" | custom-call | flops 704643072 | bytes 4096000 | tf_op jit(solution)/shard_map/pallas_call | solution.py:28
  171.1 2.6 %collective-permute-start.10 = (bf16[1024,384]{1,0:T(8,128)(2,1)S(1)}, bf16[1024,384]{1,0:T(8,128)(2,1)S(1)}, u32[]{:S(2)}, u32[]{:S(2)}) collective-permute-start(bf16[1024,384]{1,0:T(8,128)(2,1)S(1)} %get-tuple-element.39), channel_id=1, source_target_pairs={{0,64},{64,0},{128,192},{192,128},{256,320},{320,256},{384,448},{4... | collective-permute-start | bytes 2359304 | tf_op jit(solution)/shard_map/ppermute | solution.py:205
  173.8 1.8 collective-permute-done.10.got_ref
  175.6 1.3 shard_map.120
  176.9 1.4 reshape.31.back_ref
  (43 shorter events, 6.6 us)
Async XLA Ops:
  0.6 26.1 %copy-start.2 = (bf16[1,128,2048]{2,1,0:T(8,128)(2,1)S(1)}, bf16[1,128,2048]{2,1,0:T(8,128)(2,1)}, u32[]{:S(2)}) copy-start(bf16[1,128,2048]{2,1,0:T(8,128)(2,1)} %param.13) | copy-start | bytes 1572868
  0.6 26.1 %copy-start.1 = (bf16[1,2048,128]{2,1,0:T(8,128)(2,1)S(1)}, bf16[1,2048,128]{2,1,0:T(8,128)(2,1)}, u32[]{:S(2)}) copy-start(bf16[1,2048,128]{2,1,0:T(8,128)(2,1)} %param.12) | copy-start | bytes 1572868
  0.7 26.1 %copy-start = (bf16[1,2048,128]{2,1,0:T(8,128)(2,1)S(1)}, bf16[1,2048,128]{2,1,0:T(8,128)(2,1)}, u32[]{:S(2)}) copy-start(bf16[1,2048,128]{2,1,0:T(8,128)(2,1)} %param.11) | copy-start | bytes 1572868
  0.7 0.8 copy-start.7
  1.5 0.9 copy-start.9
  2.3 0.9 copy-start.10
  3.2 0.7 copy-start.11
  5.4 65.9 %all-to-all-start = ((bf16[128,8,512]{2,1,0:T(8,128)(2,1)}), bf16[128,8,512]{2,1,0:T(8,128)(2,1)}, u32[]{:S(2)}, u32[]{:S(2)}) async-start(bf16[128,8,512]{2,1,0:T(8,128)(2,1)} %bitcast.3), calls=%async_computation | async-start | bytes 2097152 | tf_op jit(solution)/shard_map/all_to_all | solution.py:220
  27.0 40.2 %collective-permute-start.1 = (bf16[1024,384]{1,0:T(8,128)(2,1)S(1)}, bf16[1024,384]{1,0:T(8,128)(2,1)S(1)}, u32[]{:S(2)}, u32[]{:S(2)}) collective-permute-start(bf16[1024,384]{1,0:T(8,128)(2,1)S(1)} %shard_map.112), channel_id=1, source_target_pairs={{0,128},{64,192},{128,0},{192,64},{256,384},{320,448},{384,256},{4... | collective-permute-start | bytes 2359304 | tf_op jit(solution)/shard_map/ppermute | solution.py:205
  30.3 39.7 %collective-permute-start = (bf16[512,384]{1,0:T(8,128)(2,1)S(1)}, bf16[512,384]{1,0:T(8,128)(2,1)S(1)}, u32[]{:S(2)}, u32[]{:S(2)}) collective-permute-start(bf16[512,384]{1,0:T(8,128)(2,1)S(1)} %slice.34), channel_id=1, source_target_pairs={{0,64},{64,0},{128,192},{192,128},{256,320},{320,256},{384,448},{4... | collective-permute-start | bytes 1179656 | tf_op jit(solution)/shard_map/ppermute | solution.py:205
  67.2 4.2 %collective-permute-start.2 = (bf16[512,384]{1,0:T(8,128)(2,1)S(1)}, bf16[512,384]{1,0:T(8,128)(2,1)S(1)}, u32[]{:S(2)}, u32[]{:S(2)}) collective-permute-start(bf16[512,384]{1,0:T(8,128)(2,1)S(1)} %slice.35), channel_id=1, source_target_pairs={{0,64},{64,0},{128,192},{192,128},{256,320},{320,256},{384,448},{4... | collective-permute-start | bytes 1179656 | tf_op jit(solution)/shard_map/ppermute | solution.py:205
  71.3 2.1 %copy-start.3 = (bf16[512,384]{1,0:T(8,128)(2,1)}, bf16[512,384]{1,0:T(8,128)(2,1)S(1)}, u32[]{:S(2)}) copy-start(bf16[512,384]{1,0:T(8,128)(2,1)S(1)} %collective-permute-done.2.second_ref.refs_3_) | copy-start | bytes 1179652
  73.5 4.0 %collective-permute-start.3 = (bf16[896,384]{1,0:T(8,128)(2,1)S(1)}, bf16[896,384]{1,0:T(8,128)(2,1)S(1)}, u32[]{:S(2)}, u32[]{:S(2)}) collective-permute-start(bf16[896,384]{1,0:T(8,128)(2,1)S(1)} %shard_map.114), channel_id=1, source_target_pairs={{0,64},{64,0},{128,192},{192,128},{256,320},{320,256},{384,448},{4... | collective-permute-start | bytes 2064392 | tf_op jit(solution)/shard_map/ppermute | solution.py:205
  77.6 11.1 %collective-permute-start.4 = (bf16[448,384]{1,0:T(8,128)(2,1)S(1)}, bf16[448,384]{1,0:T(8,128)(2,1)S(1)}, u32[]{:S(2)}, u32[]{:S(2)}) collective-permute-start(bf16[448,384]{1,0:T(8,128)(2,1)S(1)} %add_convert_fusion), channel_id=1, source_target_pairs={{0,128},{64,192},{128,0},{192,64},{256,384},{320,448},{384,256},{4... | collective-permute-start | bytes 1032200 | tf_op jit(solution)/shard_map/ppermute | solution.py:205
  88.9 11.7 %copy-start.5 = (bf16[448,384]{1,0:T(8,128)(2,1)}, bf16[448,384]{1,0:T(8,128)(2,1)S(1)}, u32[]{:S(2)}) copy-start(bf16[448,384]{1,0:T(8,128)(2,1)S(1)} %shard_map.115.refs_0_.h0_ref) | copy-start | bytes 1032196
  89.0 10.1 %collective-permute-start.6 = (bf16[448,384]{1,0:T(8,128)(2,1)S(1)}, bf16[448,384]{1,0:T(8,128)(2,1)}, u32[]{:S(2)}, u32[]{:S(2)}) collective-permute-start(bf16[448,384]{1,0:T(8,128)(2,1)S(1)} %shard_map.115.refs_0_.h0_ref), channel_id=1, source_target_pairs={{0,64},{64,0},{128,192},{192,128},{256,320},{320,256},{384,448},{4... | collective-permute-start | bytes 1032200 | tf_op jit(solution)/shard_map/ppermute | solution.py:205
  92.1 11.6 %collective-permute-start.5 = (bf16[448,384]{1,0:T(8,128)(2,1)S(1)}, bf16[448,384]{1,0:T(8,128)(2,1)}, u32[]{:S(2)}, u32[]{:S(2)}) collective-permute-start(bf16[448,384]{1,0:T(8,128)(2,1)S(1)} %shard_map.115.refs_0_.h0_ref), channel_id=1, source_target_pairs={{0,128},{64,192},{128,0},{192,64},{256,384},{320,448},{384,256},{4... | collective-permute-start | bytes 1032200 | tf_op jit(solution)/shard_map/ppermute | solution.py:205
  99.0 8.9 %copy-start.4 = (bf16[512,384]{1,0:T(8,128)(2,1)S(1)}, bf16[512,384]{1,0:T(8,128)(2,1)}, u32[]{:S(2)}) copy-start(bf16[512,384]{1,0:T(8,128)(2,1)} %copy-done.3) | copy-start | bytes 1179652
  103.7 4.2 %collective-permute-start.7 = (bf16[448,384]{1,0:T(8,128)(2,1)}, bf16[448,384]{1,0:T(8,128)(2,1)S(1)}, u32[]{:S(2)}, u32[]{:S(2)}) collective-permute-start(bf16[448,384]{1,0:T(8,128)(2,1)} %collective-permute-done.5.refs_0_), channel_id=1, source_target_pairs={{0,64},{64,0},{128,192},{192,128},{256,320},{320,256},{384,448},{4... | collective-permute-start | bytes 1032200 | tf_op jit(solution)/shard_map/ppermute | solution.py:205
  109.5 16.8 %copy-start.12 = (bf16[64,7,512]{2,1,0:T(8,128)(2,1)S(1)}, bf16[64,7,512]{2,1,0:T(8,128)(2,1)}, u32[]{:S(2)}) copy-start(bf16[64,7,512]{2,1,0:T(8,128)(2,1)} %get-tuple-element.43) | copy-start | bytes 1376260
  110.8 18.1 %copy-start.13 = (bf16[448,512]{1,0:T(8,128)(2,1)S(1)}, bf16[448,512]{1,0:T(8,128)(2,1)}, u32[]{:S(2)}) copy-start(bf16[448,512]{1,0:T(8,128)(2,1)} %slice.31) | copy-start | bytes 1376260
  110.8 58.3 %copy-start.6 = (bf16[448,384]{1,0:T(8,128)(2,1)S(1)}, bf16[448,384]{1,0:T(8,128)(2,1)}, u32[]{:S(2)}) copy-start(bf16[448,384]{1,0:T(8,128)(2,1)} %copy-done.5) | copy-start | bytes 1032196
  110.8 66.2 %all-to-all-start.1 = ((bf16[128,7,512]{2,1,0:T(8,128)(2,1)}), bf16[128,7,512]{2,1,0:T(8,128)(2,1)}, u32[]{:S(2)}, u32[]{:S(2)}) async-start(bf16[128,7,512]{2,1,0:T(8,128)(2,1)} %reshape.30), calls=%async_computation.1 | async-start | bytes 2097152 | tf_op jit(solution)/shard_map/all_to_all | solution.py:220
  126.3 47.4 %copy-start.8 = (f32[160,2]{0,1:T(2,128)S(1)}, f32[160,2]{0,1:T(2,128)}, u32[]{:S(2)}) copy-start(f32[160,2]{0,1:T(2,128)} %param.10) | copy-start | bytes 3844
  126.5 32.7 %collective-permute-start.8 = (bf16[448,512]{1,0:T(8,128)(2,1)S(1)}, bf16[448,512]{1,0:T(8,128)(2,1)S(1)}, u32[]{:S(2)}, u32[]{:S(2)}) collective-permute-start(bf16[448,512]{1,0:T(8,128)(2,1)S(1)} %slice.33), channel_id=1, source_target_pairs={{0,128},{64,192},{128,0},{192,64},{256,384},{320,448},{384,256},{4... | collective-permute-start | bytes 1376264 | tf_op jit(solution)/shard_map/ppermute | solution.py:205
  128.9 40.2 %collective-permute-start.9 = (bf16[448,512]{1,0:T(8,128)(2,1)S(1)}, bf16[448,512]{1,0:T(8,128)(2,1)S(1)}, u32[]{:S(2)}, u32[]{:S(2)}) collective-permute-start(bf16[448,512]{1,0:T(8,128)(2,1)S(1)} %copy-done.13), channel_id=1, source_target_pairs={{0,128},{64,192},{128,0},{192,64},{256,384},{320,448},{384,256},{4... | collective-permute-start | bytes 1376264 | tf_op jit(solution)/shard_map/ppermute | solution.py:205
  171.1 4.5 %collective-permute-start.10 = (bf16[1024,384]{1,0:T(8,128)(2,1)S(1)}, bf16[1024,384]{1,0:T(8,128)(2,1)S(1)}, u32[]{:S(2)}, u32[]{:S(2)}) collective-permute-start(bf16[1024,384]{1,0:T(8,128)(2,1)S(1)} %get-tuple-element.39), channel_id=1, source_target_pairs={{0,64},{64,0},{128,192},{192,128},{256,320},{320,256},{384,448},{4... | collective-permute-start | bytes 2359304 | tf_op jit(solution)/shard_map/ppermute | solution.py:205

commit v5 on v4

--- a/solution.py
+++ b/solution.py
@@ -10,8 +10,8 @@
 
 
 BF16, F32, I32 = jnp.bfloat16, jnp.float32, jnp.int32
-PAD = 8
 DP = ("za", "zb", "core")
+SMALL = pltpu.CompilerParams(vmem_limit_bytes=16 << 20)
 FAR, CHIP, CORE = 4, 2, 1
 FEATURES = (0, FAR)
 
@@ -31,7 +31,7 @@
         in_specs=[smem] * len(head) + [vmem] * len(args),
         out_specs=[vmem] * len(outs),
         cost_estimate=pl.CostEstimate(flops=flops, bytes_accessed=moved, transcendentals=0),
-        compiler_params=pltpu.CompilerParams(vmem_limit_bytes=16 << 20),
+        compiler_params=SMALL,
     )(*head, *args)
 
 
@@ -39,7 +39,7 @@
     return lax.broadcasted_iota(I32, shape, dim)
 
 
-def route_body(experts, capacity, ids_ref, probs_ref, tok_ref, grad_ref, out_ref, pos_ref):
+def route_body(experts, piece, ids_ref, probs_ref, tok_ref, grad_ref, out_ref, pos_ref):
     ids, probs = ids_ref[...], probs_ref[...]
     rows = ids.shape[1]
     width = tok_ref.shape[1]
@@ -47,12 +47,13 @@
     both = (named[0].astype(F32) + named[1].astype(F32)).astype(BF16)
     earlier = (iota((rows, rows), 0) < iota((rows, rows), 1)).astype(F32).astype(BF16)
     before = dot(both, earlier)
-    place = iota((experts * PAD, rows), 0)
+    place = iota((experts * piece, rows), 0)
     here = []
     for k in range(2):
         slot = jnp.sum(jnp.where(named[k], before, 0.0), axis=0, keepdims=True).astype(I32)
-        pos_ref[k : k + 1, :] = ids[k : k + 1, :] * capacity + slot
-        here.append(place == ids[k : k + 1, :] * PAD + slot)
+        pos = ids[k : k + 1, :] * piece + slot
+        pos_ref[k : k + 1, :] = pos
+        here.append(place == pos)
     picks = (here[0] | here[1]).astype(F32).astype(BF16)
     factor = jnp.sum(
         jnp.where(here[0], probs[0:1, :], jnp.where(here[1], probs[1:2, :], 0.0)),
@@ -62,7 +63,7 @@
     routed = dot(picks, tok_ref[...]).astype(BF16)
     routed_grad = (dot(picks, grad_ref[...]) * factor).astype(BF16)
     for i in range(len(FEATURES)):
-        at = pl.ds(i * experts * PAD, experts * PAD)
+        at = pl.ds(i * experts * piece, experts * piece)
         out_ref[at, :width] = routed
         out_ref[at, width:] = routed_grad
 
@@ -94,14 +95,26 @@
     return pl.ds(pl.multiple_of(far * n, n), n)
 
 
-def pack_body(masks, me_ref, gate_ref, up_ref, down_ref, out_ref):
+def pack_body(masks, me_ref, gate_ref, up_ref, down_ref, out_ref, downs, sems):
     width = out_ref.shape[0] // len(masks)
     units = gate_ref.shape[1]
+    fetches = []
     for i, mask in enumerate(masks):
         at, to = block_of(me_ref, mask, width), pl.ds(i * width, width)
-        out_ref[to, :units] = gate_ref[at, :]
-        out_ref[to, units : 2 * units] = up_ref[at, :]
-        out_ref[to, 2 * units :] = down_ref[:, at].T
+        pairs = (
+            (down_ref.at[:, at], downs.at[i]),
+            (gate_ref.at[at, :], out_ref.at[to, :units]),
+            (up_ref.at[at, :], out_ref.at[to, units : 2 * units]),
+        )
+        for k, (source, target) in enumerate(pairs):
+            fetches.append(pltpu.make_async_copy(source, target, sems.at[3 * i + k]))
+            fetches[-1].start()
+    for i in range(len(masks)):
+        fetches[3 * i].wait()
+        out_ref[pl.ds(i * width, width), 2 * units :] = downs[i].T
+    for i in range(len(masks)):
+        fetches[3 * i + 1].wait()
+        fetches[3 * i + 2].wait()
 
 
 def pre_body(me_ref, x_ref, first_ref, second_ref, *out_refs):
@@ -157,24 +170,20 @@
             out_ref[rows, width:] = (back + acc_ref[held, width:]).astype(BF16)
 
 
-def weight_grads_body(me_ref, own_ref, near_ref, far_ref, h0_ref, h1_ref, keep_ref, send_ref):
-    n = near_ref.shape[0]
+def weight_grads_body(own_ref, first_ref, last_ref, h0_ref, h1_ref, keep_ref, send_ref):
+    n = h0_ref.shape[0]
+    parts = [(own_ref, pl.ds(i * n, n)) for i in range(len(FEATURES))]
+    parts += [(first_ref, pl.ds(0, n)), (last_ref, pl.ds(0, n))]
     width = own_ref.shape[1] // 2
     units = h0_ref.shape[1] // 3
     grads = jnp.concatenate([h0_ref[:, units:], h1_ref[:, units:]], axis=1)
     hidden = jnp.concatenate([h0_ref[:, :units], h1_ref[:, :units]], axis=1)
-
-    def work(x, g, to):
-        both, down = dot(x, grads, 0, 0).astype(BF16), dot(g, hidden, 0, 0).astype(BF16)
+    for i, (ref, rows) in enumerate(parts):
+        to = pl.ds(i * width, width)
+        both = dot(ref[rows, :width], grads, 0, 0).astype(BF16)
+        down = dot(ref[rows, width:], hidden, 0, 0).astype(BF16)
         keep_ref[to, : 2 * units], send_ref[to, : 2 * units] = both[:, : 2 * units], both[:, 2 * units :]
         keep_ref[to, 2 * units :], send_ref[to, 2 * units :] = down[:, :units], down[:, units:]
-
-    for i in range(len(FEATURES)):
-        rows = pl.ds(i * n, n)
-        work(own_ref[rows, :width], own_ref[rows, width:], pl.ds(i * width, width))
-    for i, ref in enumerate((near_ref, far_ref)):
-        at = pl.ds((len(FEATURES) + i) * width, width)
-        work(ref[:, :width], ref[:, width:], at)
 
 
 def merge_body(me_ref, keep_ref, got_ref, gate_ref, up_ref, down_ref):
@@ -194,7 +203,8 @@
     experts = lax.axis_size("expert")
     rows, width = tokens.shape
     capacity = max(2, 3 * rows // experts)
-    n, copies = experts * capacity, len(FEATURES)
+    piece = -(-capacity // 8) * 8
+    n, copies = experts * piece, len(FEATURES)
     gate, up, down = gate_weight[0], up_weight[0], down_weight[0]
     units, model = down.shape
     me = lax.axis_index(DP).astype(I32).reshape(1)
@@ -204,14 +214,22 @@
     def swap(x, mask):
         return lax.ppermute(x, DP, [(j, j ^ mask) for j in range(8)])
 
-    def pack(*masks):
-        return call(
+    def pack(*masks, params=None):
+        space = pl.BlockSpec(memory_space=pl.ANY)
+        return pl.pallas_call(
             functools.partial(pack_body, masks),
-            [sds((len(masks) * width, 3 * units), BF16)],
-            [gate, up, down],
-            0,
-            me,
-        )[0]
+            out_shape=sds((len(masks) * width, 3 * units), BF16),
+            in_specs=[pl.BlockSpec(memory_space=pltpu.SMEM), space, space, space],
+            out_specs=pl.BlockSpec(memory_space=pltpu.VMEM),
+            scratch_shapes=[
+                pltpu.VMEM((len(masks), units, width), BF16),
+                pltpu.SemaphoreType.DMA((3 * len(masks),)),
+            ],
+            cost_estimate=pl.CostEstimate(
+                flops=0, bytes_accessed=12 * len(masks) * width * units, transcendentals=0
+            ),
+            compiler_params=params,
+        )(me, gate, up, down)
 
     def pre(weights, outs):
         return call(pre_body, outs, [x, *weights], 2 * copies * per_pair, me)
@@ -222,21 +240,21 @@
     cut = copies * width
     chip_w = swap(pack(CHIP, CHIP ^ FAR, CHIP ^ CORE, CHIP ^ CORE ^ FAR), CHIP)
     send, pos = call(
-        functools.partial(route_body, experts, capacity),
-        [sds((copies * experts * PAD, 2 * width), BF16), sds((2, rows), I32)],
+        functools.partial(route_body, experts, piece),
+        [sds((copies * n, 2 * width), BF16), sds((2, rows), I32)],
         [expert_ids.T, gate_probs.T, tokens, grad_out],
-        4 * experts * PAD * rows * width,
-    )
-    filled = there_and_back(send.reshape(copies * experts, PAD, 2 * width))
-    near = pack(0, FAR, CORE, CORE ^ FAR)
+        4 * n * rows * width,
+    )
+    filled = there_and_back(send.reshape(copies * experts, piece, 2 * width))
+    near = pack(0, FAR, CORE, CORE ^ FAR, params=SMALL)
     core_w = swap(near[cut:], CORE)
     relay_w = swap(chip_w[cut:], CORE)
     filled, near, core_w, chip_w, relay_w = lax.optimization_barrier(
         (filled, near, core_w, chip_w, relay_w)
     )
     w = {0: near, CORE: core_w, CHIP: chip_w, CHIP ^ CORE: relay_w}
-    x = filled[:, :capacity].reshape(copies * n, 2 * width)
-    x_near = swap(x[:n], CHIP)
+    x = filled.reshape(copies * n, 2 * width)
+    x_first = swap(x[:n], CHIP)
 
     (core_out,) = pre((w[1], w[3]), [sds((2 * n, 3 * units), BF16)])
     core_in = swap(core_out, CORE)
@@ -254,7 +272,7 @@
     )
     h2, acc, last = lax.optimization_barrier((h2, acc, x[n:]))
     h3 = swap(h2, CORE)
-    x_far = swap(last, CHIP)
+    x_last = swap(last, CHIP)
     (result,) = call(
         functools.partial(result_body, False),
         [sds((copies * n, 2 * width), BF16)],
@@ -262,13 +280,12 @@
         2 * copies * per_pair,
         me,
     )
-    returned = there_and_back(result.reshape(copies * experts, capacity, 2 * width))
+    returned = there_and_back(result.reshape(copies * experts, piece, 2 * width))
     kept, share = call(
         weight_grads_body,
         [sds((4 * width, 3 * units), BF16)] * 2,
-        [x, x_near, x_far, h0, h1],
+        [x, x_first, x_last, h0, h1],
         8 * per_pair,
-        me,
     )
     got = swap(share, CORE)
     gate_grad, up_grad, down_grad = call(

time: 180 us -> 183 us (1.017)
  waiting for transfers between devices: 88.2 us -> 93.4 us
  local copies, waits for them, and re-layouts: 12.1 us -> 8.48 us
    ppermute x11, waiting for transfers between devices: 88.2 us -> 93.4 us  [swap(): return lax.ppermute(x, DP, [(j, j ^ mask) for j in range(8)])]
    reshape x3 -> x0, local copies, waits for them, and re-layouts: 4.25 us -> none  [the longest x1 1.57 us: per_device(): x = filled[:, :capacity].reshape(copies * n, 2 * width)]
    unnamed x29, local copies, waits for them, and re-layouts: 3.4 us -> 7.36 us
    slice x3 -> x1, local copies, waits for them, and re-layouts: 4.36 us -> 1.03 us  [per_device(): x_first = swap(x[:n], CHIP)]
    pallas_call x0 -> x2, Pallas kernels: none -> 2.76 us  [pack(): pl.pallas_call(functools.partial(pack_body, masks), out_shape=sds((len(ma...]
    pallas_call x11 -> x9, Pallas kernels: 10.8 us -> 9.61 us  [call(): pl.pallas_call(body, out_shape=outs, in_specs=[smem] * len(head) + [vmem]...]
  transfers between devices with their start and end apart: 13 -> 13, of which waited for: 9 -> 9; matrix products, arithmetic and copies ran while one was open for 3% -> 1% of each run, Pallas kernels for 3% -> 4%
where the time goes in v5:
time: 183 us; the launch traced here: 182 us
  waiting for transfers between devices  93.4 us (51%)
  starting transfers between devices  66.8 us (37%)
  Pallas kernels  12.4 us (7%)
  local copies, waits for them, and re-layouts  8.48 us (5%)
    ppermute x11, waiting for transfers between devices, swap(): return lax.ppermute(x, DP, [(j, j ^ mask) for j in range(8)])  93.4 us
    all_to_all x2, starting transfers between devices, there_and_back(): lax.all_to_all(a, ('za', 'expert'), split_axis=0, concat_axis=0, tiled=True)  36.1 us
    ppermute x11, starting transfers between devices, swap(): return lax.ppermute(x, DP, [(j, j ^ mask) for j in range(8)])  30.8 us
    pallas_call x9, Pallas kernels, call(): pl.pallas_call(body, out_shape=outs, in_specs=[smem] * len(head) + [vmem]...  9.61 us
    unnamed x29, local copies, waits for them, and re-layouts  7.36 us
  transfers between devices with their start and end apart: 13, of which 9 were waited for; matrix products, arithmetic and copies ran while one was open for 1% of the time, Pallas kernels for 4%

profile of v5, /device:TPU:1, one launch (start us, length us, event | category | flops | bytes accessed | tf_op | source)
XLA Modules:
  0.0 182.1 jit_solution(17364818829899973261)
XLA Ops:
  3.8 1.5 shard_map.110
  5.3 20.9 %all-to-all-start = ((bf16[128,8,512]{2,1,0:T(8,128)(2,1)}), bf16[128,8,512]{2,1,0:T(8,128)(2,1)S(1)}, u32[]{:S(2)}, u32[]{:S(2)}) async-start(bf16[128,8,512]{2,1,0:T(8,128)(2,1)} %bitcast.3), calls=%async_computation | async-start | bytes 2097152 | tf_op jit(solution)/shard_map/all_to_all | solution.py:238
  26.2 2.2 %shard_map.112 = bf16[1024,384]{1,0:T(8,128)(2,1)} custom-call(s32[1]{0:T(128)} %bitcast.2.me_ref, bf16[2048,128]{1,0:T(8,128)(2,1)} %bitcast.20, bf16[2048,128]{1,0:T(8,128)(2,1)} %bitcast.22, bf16[128,2048]{1,0:T(8,128)(2,1)} %bitcast.24), custom_call_target="tpu_custom_call" | custom-call | bytes 1572864 | tf_op jit(solution)/shard_map/pallas_call | solution.py:219
  28.4 3.1 %collective-permute-start.1 = (bf16[1024,384]{1,0:T(8,128)(2,1)}, bf16[1024,384]{1,0:T(8,128)(2,1)S(1)}, u32[]{:S(2)}, u32[]{:S(2)}) collective-permute-start(bf16[1024,384]{1,0:T(8,128)(2,1)} %shard_map.112), channel_id=1, source_target_pairs={{0,128},{64,192},{128,0},{192,64},{256,384},{320,448},{384,256},{4... | collective-permute-start | bytes 2359304 | tf_op jit(solution)/shard_map/ppermute | solution.py:215
  31.6 1.0 copy-done.1
  32.6 1.0 copy-done.2
  34.3 3.1 %collective-permute-start = (bf16[512,384]{1,0:T(8,128)(2,1)S(1)}, bf16[512,384]{1,0:T(8,128)(2,1)S(1)}, u32[]{:S(2)}, u32[]{:S(2)}) collective-permute-start(bf16[512,384]{1,0:T(8,128)(2,1)S(1)} %slice.28), channel_id=1, source_target_pairs={{0,64},{64,0},{128,192},{192,128},{256,320},{320,256},{384,448},{4... | collective-permute-start | bytes 1179656 | tf_op jit(solution)/shard_map/ppermute | solution.py:215
  37.4 29.7 %collective-permute-done.1.second_ref.refs_2_ = bf16[1024,384]{1,0:T(8,128)(2,1)S(1)} collective-permute-done((bf16[1024,384]{1,0:T(8,128)(2,1)}, bf16[1024,384]{1,0:T(8,128)(2,1)S(1)}, u32[]{:S(2)}, u32[]{:S(2)}) %collective-permute-start.1) | collective-permute-done | bytes 786464 | tf_op jit(solution)/shard_map/ppermute | solution.py:215
  67.1 2.7 %collective-permute-start.2 = (bf16[512,384]{1,0:T(8,128)(2,1)S(1)}, bf16[512,384]{1,0:T(8,128)(2,1)S(1)}, u32[]{:S(2)}, u32[]{:S(2)}) collective-permute-start(bf16[512,384]{1,0:T(8,128)(2,1)S(1)} %slice.29), channel_id=1, source_target_pairs={{0,64},{64,0},{128,192},{192,128},{256,320},{320,256},{384,448},{4... | collective-permute-start | bytes 1179656 | tf_op jit(solution)/shard_map/ppermute | solution.py:215
  69.8 1.3 collective-permute-done.2.second_ref.refs_3_
  71.7 2.3 %collective-permute-start.3 = (bf16[1024,384]{1,0:T(8,128)(2,1)S(1)}, bf16[1024,384]{1,0:T(8,128)(2,1)S(1)}, u32[]{:S(2)}, u32[]{:S(2)}) collective-permute-start(bf16[1024,384]{1,0:T(8,128)(2,1)S(1)} %shard_map.114), channel_id=1, source_target_pairs={{0,64},{64,0},{128,192},{192,128},{256,320},{320,256},{384,448},{4... | collective-permute-start | bytes 2359304 | tf_op jit(solution)/shard_map/ppermute | solution.py:215
  74.6 1.3 collective-permute-done.3.core_ref
  76.0 3.0 %collective-permute-start.4 = (bf16[512,384]{1,0:T(8,128)(2,1)S(1)}, bf16[512,384]{1,0:T(8,128)(2,1)S(1)}, u32[]{:S(2)}, u32[]{:S(2)}) collective-permute-start(bf16[512,384]{1,0:T(8,128)(2,1)S(1)} %add_convert_fusion), channel_id=1, source_target_pairs={{0,128},{64,192},{128,0},{192,64},{256,384},{320,448},{384,256},{4... | collective-permute-start | bytes 1179656 | tf_op jit(solution)/shard_map/ppermute | solution.py:215
  78.9 9.2 %collective-permute-done.4.chip_ref = bf16[512,384]{1,0:T(8,128)(2,1)S(1)} collective-permute-done((bf16[512,384]{1,0:T(8,128)(2,1)S(1)}, bf16[512,384]{1,0:T(8,128)(2,1)S(1)}, u32[]{:S(2)}, u32[]{:S(2)}) %collective-permute-start.4) | collective-permute-done | bytes 393248 | tf_op jit(solution)/shard_map/ppermute | solution.py:215
  88.4 3.1 %collective-permute-start.6 = (bf16[512,384]{1,0:T(8,128)(2,1)S(1)}, bf16[512,384]{1,0:T(8,128)(2,1)S(1)}, u32[]{:S(2)}, u32[]{:S(2)}) collective-permute-start(bf16[512,384]{1,0:T(8,128)(2,1)S(1)} %shard_map.115.refs_0_.h0_ref), channel_id=1, source_target_pairs={{0,64},{64,0},{128,192},{192,128},{256,320},{320,256},{384,448},{4... | collective-permute-start | bytes 1179656 | tf_op jit(solution)/shard_map/ppermute | solution.py:215
  91.6 3.0 %collective-permute-start.5 = (bf16[512,384]{1,0:T(8,128)(2,1)S(1)}, bf16[512,384]{1,0:T(8,128)(2,1)S(1)}, u32[]{:S(2)}, u32[]{:S(2)}) collective-permute-start(bf16[512,384]{1,0:T(8,128)(2,1)S(1)} %shard_map.115.refs_0_.h0_ref), channel_id=1, source_target_pairs={{0,128},{64,192},{128,0},{192,64},{256,384},{320,448},{384,256},{4... | collective-permute-start | bytes 1179656 | tf_op jit(solution)/shard_map/ppermute | solution.py:215
  94.5 1.0 slice_bitcast_fusion
  96.2 7.9 %collective-permute-done.5.refs_0_ = bf16[512,384]{1,0:T(8,128)(2,1)S(1)} collective-permute-done((bf16[512,384]{1,0:T(8,128)(2,1)S(1)}, bf16[512,384]{1,0:T(8,128)(2,1)S(1)}, u32[]{:S(2)}, u32[]{:S(2)}) %collective-permute-start.5) | collective-permute-done | bytes 393248 | tf_op jit(solution)/shard_map/ppermute | solution.py:215
  104.1 2.8 %collective-permute-start.7 = (bf16[512,384]{1,0:T(8,128)(2,1)S(1)}, bf16[512,384]{1,0:T(8,128)(2,1)S(1)}, u32[]{:S(2)}, u32[]{:S(2)}) collective-permute-start(bf16[512,384]{1,0:T(8,128)(2,1)S(1)} %collective-permute-done.5.refs_0_), channel_id=1, source_target_pairs={{0,64},{64,0},{128,192},{192,128},{256,320},{320,256},{384,448},{4... | collective-permute-start | bytes 1179656 | tf_op jit(solution)/shard_map/ppermute | solution.py:215
  106.9 1.3 collective-permute-done.7.refs_1_
  108.2 1.6 shard_map.117
  109.8 15.2 %all-to-all-start.1 = ((bf16[128,8,512]{2,1,0:T(8,128)(2,1)}), bf16[128,8,512]{2,1,0:T(8,128)(2,1)S(1)}, u32[]{:S(2)}, u32[]{:S(2)}) async-start(bf16[128,8,512]{2,1,0:T(8,128)(2,1)} %bitcast.9), calls=%async_computation.1 | async-start | bytes 2097152 | tf_op jit(solution)/shard_map/all_to_all | solution.py:238
  125.0 2.4 %collective-permute-start.8 = (bf16[512,512]{1,0:T(8,128)(2,1)}, bf16[512,512]{1,0:T(8,128)(2,1)S(1)}, u32[]{:S(2)}, u32[]{:S(2)}) collective-permute-start(bf16[512,512]{1,0:T(8,128)(2,1)} %get-tuple-element.43), channel_id=1, source_target_pairs={{0,128},{64,192},{128,0},{192,64},{256,384},{320,448},{384,256},{4... | collective-permute-start | bytes 1572872 | tf_op jit(solution)/shard_map/ppermute | solution.py:215
  127.4 2.9 %collective-permute-start.9 = (bf16[512,512]{1,0:T(8,128)(2,1)}, bf16[512,512]{1,0:T(8,128)(2,1)S(1)}, u32[]{:S(2)}, u32[]{:S(2)}) collective-permute-start(bf16[512,512]{1,0:T(8,128)(2,1)} %get-tuple-element.37), channel_id=1, source_target_pairs={{0,128},{64,192},{128,0},{192,64},{256,384},{320,448},{384,256},{4... | collective-permute-start | bytes 1572872 | tf_op jit(solution)/shard_map/ppermute | solution.py:215
  130.3 29.4 %collective-permute-done.8.first_ref = bf16[512,512]{1,0:T(8,128)(2,1)S(1)} collective-permute-done((bf16[512,512]{1,0:T(8,128)(2,1)}, bf16[512,512]{1,0:T(8,128)(2,1)S(1)}, u32[]{:S(2)}, u32[]{:S(2)}) %collective-permute-start.8) | collective-permute-done | bytes 524320 | tf_op jit(solution)/shard_map/ppermute | solution.py:215
  159.7 11.2 %collective-permute-done.9.last_ref = bf16[512,512]{1,0:T(8,128)(2,1)S(1)} collective-permute-done((bf16[512,512]{1,0:T(8,128)(2,1)}, bf16[512,512]{1,0:T(8,128)(2,1)S(1)}, u32[]{:S(2)}, u32[]{:S(2)}) %collective-permute-start.9) | collective-permute-done | bytes 524320 | tf_op jit(solution)/shard_map/ppermute | solution.py:215
  171.0 2.0 %shard_map.119 = (bf16[1024,384]{1,0:T(8,128)(2,1)S(1)}, bf16[1024,384]{1,0:T(8,128)(2,1)}) custom-call(bf16[1024,512]{1,0:T(8,128)(2,1)S(1)} %bitcast.19, bf16[512,512]{1,0:T(8,128)(2,1)S(1)} %collective-permute-done.8.first_ref, bf16[512,512]{1,0:T(8,128)(2,1)S(1)} %collective-permute-done.9.last_ref, bf16[512,384]{1,0:T(8,128)(2,1)S(1)} %shard_map.115.refs_0_.h0_ref, ...), custom_call_target="tpu_custom_call" | custom-call | flops 805306368 | bytes 4456448 | tf_op jit(solution)/shard_map/pallas_call | solution.py:28
  173.8 2.4 %collective-permute-start.10 = (bf16[1024,384]{1,0:T(8,128)(2,1)}, bf16[1024,384]{1,0:T(8,128)(2,1)S(1)}, u32[]{:S(2)}, u32[]{:S(2)}) collective-permute-start(bf16[1024,384]{1,0:T(8,128)(2,1)} %get-tuple-element.39), channel_id=1, source_target_pairs={{0,64},{64,0},{128,192},{192,128},{256,320},{320,256},{384,448},{4... | collective-permute-start | bytes 2359304 | tf_op jit(solution)/shard_map/ppermute | solution.py:215
  176.4 2.0 %collective-permute-done.10.got_ref = bf16[1024,384]{1,0:T(8,128)(2,1)S(1)} collective-permute-done((bf16[1024,384]{1,0:T(8,128)(2,1)}, bf16[1024,384]{1,0:T(8,128)(2,1)S(1)}, u32[]{:S(2)}, u32[]{:S(2)}) %collective-permute-start.10) | collective-permute-done | bytes 786464 | tf_op jit(solution)/shard_map/ppermute | solution.py:215
  178.4 1.1 copy-done.6
  179.5 1.3 shard_map.120
  180.9 1.2 shard_map.118
  (38 shorter events, 6.9 us)
Async XLA Ops:
  0.6 0.7 copy-start.9
  1.3 0.9 copy-start.11
  2.2 0.9 copy-start.12
  3.1 0.7 copy-start.13
  5.3 26.3 %copy-start = (bf16[1,2048,128]{2,1,0:T(8,128)(2,1)S(1)}, bf16[1,2048,128]{2,1,0:T(8,128)(2,1)}, u32[]{:S(2)}) copy-start(bf16[1,2048,128]{2,1,0:T(8,128)(2,1)} %param.11) | copy-start | bytes 1572868
  5.3 65.8 %all-to-all-start = ((bf16[128,8,512]{2,1,0:T(8,128)(2,1)}), bf16[128,8,512]{2,1,0:T(8,128)(2,1)S(1)}, u32[]{:S(2)}, u32[]{:S(2)}) async-start(bf16[128,8,512]{2,1,0:T(8,128)(2,1)} %bitcast.3), calls=%async_computation | async-start | bytes 2097152 | tf_op jit(solution)/shard_map/all_to_all | solution.py:238
  28.4 38.6 %collective-permute-start.1 = (bf16[1024,384]{1,0:T(8,128)(2,1)}, bf16[1024,384]{1,0:T(8,128)(2,1)S(1)}, u32[]{:S(2)}, u32[]{:S(2)}) collective-permute-start(bf16[1024,384]{1,0:T(8,128)(2,1)} %shard_map.112), channel_id=1, source_target_pairs={{0,128},{64,192},{128,0},{192,64},{256,384},{320,448},{384,256},{4... | collective-permute-start | bytes 2359304 | tf_op jit(solution)/shard_map/ppermute | solution.py:215
  31.6 1.0 copy-start.1
  32.6 1.0 copy-start.2
  34.3 35.5 %collective-permute-start = (bf16[512,384]{1,0:T(8,128)(2,1)S(1)}, bf16[512,384]{1,0:T(8,128)(2,1)S(1)}, u32[]{:S(2)}, u32[]{:S(2)}) collective-permute-start(bf16[512,384]{1,0:T(8,128)(2,1)S(1)} %slice.28), channel_id=1, source_target_pairs={{0,64},{64,0},{128,192},{192,128},{256,320},{320,256},{384,448},{4... | collective-permute-start | bytes 1179656 | tf_op jit(solution)/shard_map/ppermute | solution.py:215
  67.1 4.0 %collective-permute-start.2 = (bf16[512,384]{1,0:T(8,128)(2,1)S(1)}, bf16[512,384]{1,0:T(8,128)(2,1)S(1)}, u32[]{:S(2)}, u32[]{:S(2)}) collective-permute-start(bf16[512,384]{1,0:T(8,128)(2,1)S(1)} %slice.29), channel_id=1, source_target_pairs={{0,64},{64,0},{128,192},{192,128},{256,320},{320,256},{384,448},{4... | collective-permute-start | bytes 1179656 | tf_op jit(solution)/shard_map/ppermute | solution.py:215
  71.1 3.5 %copy-start.3 = (bf16[512,384]{1,0:T(8,128)(2,1)}, bf16[512,384]{1,0:T(8,128)(2,1)S(1)}, u32[]{:S(2)}) copy-start(bf16[512,384]{1,0:T(8,128)(2,1)S(1)} %collective-permute-done.2.second_ref.refs_3_) | copy-start | bytes 1179652
  71.7 4.2 %collective-permute-start.3 = (bf16[1024,384]{1,0:T(8,128)(2,1)S(1)}, bf16[1024,384]{1,0:T(8,128)(2,1)S(1)}, u32[]{:S(2)}, u32[]{:S(2)}) collective-permute-start(bf16[1024,384]{1,0:T(8,128)(2,1)S(1)} %shard_map.114), channel_id=1, source_target_pairs={{0,64},{64,0},{128,192},{192,128},{256,320},{320,256},{384,448},{4... | collective-permute-start | bytes 2359304 | tf_op jit(solution)/shard_map/ppermute | solution.py:215
  76.0 12.2 %collective-permute-start.4 = (bf16[512,384]{1,0:T(8,128)(2,1)S(1)}, bf16[512,384]{1,0:T(8,128)(2,1)S(1)}, u32[]{:S(2)}, u32[]{:S(2)}) collective-permute-start(bf16[512,384]{1,0:T(8,128)(2,1)S(1)} %add_convert_fusion), channel_id=1, source_target_pairs={{0,128},{64,192},{128,0},{192,64},{256,384},{320,448},{384,256},{4... | collective-permute-start | bytes 1179656 | tf_op jit(solution)/shard_map/ppermute | solution.py:215
  88.4 7.2 %collective-permute-start.6 = (bf16[512,384]{1,0:T(8,128)(2,1)S(1)}, bf16[512,384]{1,0:T(8,128)(2,1)S(1)}, u32[]{:S(2)}, u32[]{:S(2)}) collective-permute-start(bf16[512,384]{1,0:T(8,128)(2,1)S(1)} %shard_map.115.refs_0_.h0_ref), channel_id=1, source_target_pairs={{0,64},{64,0},{128,192},{192,128},{256,320},{320,256},{384,448},{4... | collective-permute-start | bytes 1179656 | tf_op jit(solution)/shard_map/ppermute | solution.py:215
  91.6 12.6 %collective-permute-start.5 = (bf16[512,384]{1,0:T(8,128)(2,1)S(1)}, bf16[512,384]{1,0:T(8,128)(2,1)S(1)}, u32[]{:S(2)}, u32[]{:S(2)}) collective-permute-start(bf16[512,384]{1,0:T(8,128)(2,1)S(1)} %shard_map.115.refs_0_.h0_ref), channel_id=1, source_target_pairs={{0,128},{64,192},{128,0},{192,64},{256,384},{320,448},{384,256},{4... | collective-permute-start | bytes 1179656 | tf_op jit(solution)/shard_map/ppermute | solution.py:215
  95.6 12.6 %copy-start.4 = (bf16[512,384]{1,0:T(8,128)(2,1)S(1)}, bf16[512,384]{1,0:T(8,128)(2,1)}, u32[]{:S(2)}) copy-start(bf16[512,384]{1,0:T(8,128)(2,1)} %copy-done.3) | copy-start | bytes 1179652
  95.6 8.5 %copy-start.7 = (bf16[512,384]{1,0:T(8,128)(2,1)}, bf16[512,384]{1,0:T(8,128)(2,1)S(1)}, u32[]{:S(2)}) copy-start(bf16[512,384]{1,0:T(8,128)(2,1)S(1)} %collective-permute-done.6.refs_1_.h1_ref) | copy-start | bytes 1179652
  104.1 4.1 %collective-permute-start.7 = (bf16[512,384]{1,0:T(8,128)(2,1)S(1)}, bf16[512,384]{1,0:T(8,128)(2,1)S(1)}, u32[]{:S(2)}, u32[]{:S(2)}) collective-permute-start(bf16[512,384]{1,0:T(8,128)(2,1)S(1)} %collective-permute-done.5.refs_0_), channel_id=1, source_target_pairs={{0,64},{64,0},{128,192},{192,128},{256,320},{320,256},{384,448},{4... | collective-permute-start | bytes 1179656 | tf_op jit(solution)/shard_map/ppermute | solution.py:215
  109.8 61.1 %copy-start.8 = (bf16[512,384]{1,0:T(8,128)(2,1)S(1)}, bf16[512,384]{1,0:T(8,128)(2,1)}, u32[]{:S(2)}) copy-start(bf16[512,384]{1,0:T(8,128)(2,1)} %copy-done.7) | copy-start | bytes 1179652
  109.8 66.4 %copy-start.10 = (f32[160,2]{0,1:T(2,128)S(1)}, f32[160,2]{0,1:T(2,128)}, u32[]{:S(2)}) copy-start(f32[160,2]{0,1:T(2,128)} %param.10) | copy-start | bytes 3844
  109.8 71.0 %all-to-all-start.1 = ((bf16[128,8,512]{2,1,0:T(8,128)(2,1)}), bf16[128,8,512]{2,1,0:T(8,128)(2,1)S(1)}, u32[]{:S(2)}, u32[]{:S(2)}) async-start(bf16[128,8,512]{2,1,0:T(8,128)(2,1)} %bitcast.9), calls=%async_computation.1 | async-start | bytes 2097152 | tf_op jit(solution)/shard_map/all_to_all | solution.py:238
  125.0 34.7 %collective-permute-start.8 = (bf16[512,512]{1,0:T(8,128)(2,1)}, bf16[512,512]{1,0:T(8,128)(2,1)S(1)}, u32[]{:S(2)}, u32[]{:S(2)}) collective-permute-start(bf16[512,512]{1,0:T(8,128)(2,1)} %get-tuple-element.43), channel_id=1, source_target_pairs={{0,128},{64,192},{128,0},{192,64},{256,384},{320,448},{384,256},{4... | collective-permute-start | bytes 1572872 | tf_op jit(solution)/shard_map/ppermute | solution.py:215
  127.4 43.5 %collective-permute-start.9 = (bf16[512,512]{1,0:T(8,128)(2,1)}, bf16[512,512]{1,0:T(8,128)(2,1)S(1)}, u32[]{:S(2)}, u32[]{:S(2)}) collective-permute-start(bf16[512,512]{1,0:T(8,128)(2,1)} %get-tuple-element.37), channel_id=1, source_target_pairs={{0,128},{64,192},{128,0},{192,64},{256,384},{320,448},{384,256},{4... | collective-permute-start | bytes 1572872 | tf_op jit(solution)/shard_map/ppermute | solution.py:215
  172.9 0.9 copy-start.5
  173.8 4.5 %collective-permute-start.10 = (bf16[1024,384]{1,0:T(8,128)(2,1)}, bf16[1024,384]{1,0:T(8,128)(2,1)S(1)}, u32[]{:S(2)}, u32[]{:S(2)}) collective-permute-start(bf16[1024,384]{1,0:T(8,128)(2,1)} %get-tuple-element.39), channel_id=1, source_target_pairs={{0,64},{64,0},{128,192},{192,128},{256,320},{320,256},{384,448},{4... | collective-permute-start | bytes 2359304 | tf_op jit(solution)/shard_map/ppermute | solution.py:215
  178.4 1.1 copy-start.6

commit v6 on v5

--- a/solution.py
+++ b/solution.py
@@ -170,10 +170,9 @@
             out_ref[rows, width:] = (back + acc_ref[held, width:]).astype(BF16)
 
 
-def weight_grads_body(own_ref, first_ref, last_ref, h0_ref, h1_ref, keep_ref, send_ref):
+def weight_grads_body(own_ref, near_ref, h0_ref, h1_ref, keep_ref, send_ref):
     n = h0_ref.shape[0]
-    parts = [(own_ref, pl.ds(i * n, n)) for i in range(len(FEATURES))]
-    parts += [(first_ref, pl.ds(0, n)), (last_ref, pl.ds(0, n))]
+    parts = [(ref, pl.ds(i * n, n)) for ref in (own_ref, near_ref) for i in range(len(FEATURES))]
     width = own_ref.shape[1] // 2
     units = h0_ref.shape[1] // 3
     grads = jnp.concatenate([h0_ref[:, units:], h1_ref[:, units:]], axis=1)
@@ -254,7 +253,6 @@
     )
     w = {0: near, CORE: core_w, CHIP: chip_w, CHIP ^ CORE: relay_w}
     x = filled.reshape(copies * n, 2 * width)
-    x_first = swap(x[:n], CHIP)
 
     (core_out,) = pre((w[1], w[3]), [sds((2 * n, 3 * units), BF16)])
     core_in = swap(core_out, CORE)
@@ -270,9 +268,9 @@
         2 * copies * per_pair,
         me,
     )
-    h2, acc, last = lax.optimization_barrier((h2, acc, x[n:]))
+    x_near = swap(x, CHIP)
+    h2, acc = lax.optimization_barrier((h2, acc))
     h3 = swap(h2, CORE)
-    x_last = swap(last, CHIP)
     (result,) = call(
         functools.partial(result_body, False),
         [sds((copies * n, 2 * width), BF16)],
@@ -284,7 +282,7 @@
     kept, share = call(
         weight_grads_body,
         [sds((4 * width, 3 * units), BF16)] * 2,
-        [x, x_first, x_last, h0, h1],
+        [x, x_near, h0, h1],
         8 * per_pair,
     )
     got = swap(share, CORE)

time: 183 us -> 183 us (level)
  waiting for transfers between devices: 93.4 us -> 97.3 us
  starting transfers between devices: 66.8 us -> 64.1 us
    ppermute x11 -> x10, waiting for transfers between devices: 93.4 us -> 97.3 us  [swap(): return lax.ppermute(x, DP, [(j, j ^ mask) for j in range(8)])]
    ppermute x11 -> x10, starting transfers between devices: 30.8 us -> 28 us  [swap(): return lax.ppermute(x, DP, [(j, j ^ mask) for j in range(8)])]
  transfers between devices with their start and end apart: 13 -> 12, of which waited for: 9 -> 8; matrix products, arithmetic and copies ran while one was open for 1% -> 0% of each run, Pallas kernels for 4% -> 4%
where the time goes in v6:
time: 183 us; the launch traced here: 182 us
  waiting for transfers between devices  97.3 us (53%)
  starting transfers between devices  64.1 us (35%)
  Pallas kernels  12.4 us (7%)
  local copies, waits for them, and re-layouts  7.45 us (4%)
    ppermute x10, waiting for transfers between devices, swap(): return lax.ppermute(x, DP, [(j, j ^ mask) for j in range(8)])  97.3 us
    all_to_all x2, starting transfers between devices, there_and_back(): lax.all_to_all(a, ('za', 'expert'), split_axis=0, concat_axis=0, tiled=True)  36.1 us
    ppermute x10, starting transfers between devices, swap(): return lax.ppermute(x, DP, [(j, j ^ mask) for j in range(8)])  28 us
    pallas_call x9, Pallas kernels, call(): pl.pallas_call(body, out_shape=outs, in_specs=[smem] * len(head) + [vmem]...  9.61 us
    unnamed x29, local copies, waits for them, and re-layouts  7.37 us
  transfers between devices with their start and end apart: 12, of which 8 were waited for; matrix products, arithmetic and copies ran while one was open for 0% of the time, Pallas kernels for 4%

profile of v6, /device:TPU:1, one launch (start us, length us, event | category | flops | bytes accessed | tf_op | source)
XLA Modules:
  0.0 182.2 jit_solution(10272022767718138519)
XLA Ops:
  1.3 0.9 copy-done.11
  2.2 0.9 copy-done.12
  3.8 1.5 shard_map.110
  5.3 20.9 %all-to-all-start = ((bf16[128,8,512]{2,1,0:T(8,128)(2,1)}), bf16[128,8,512]{2,1,0:T(8,128)(2,1)S(1)}, u32[]{:S(2)}, u32[]{:S(2)}) async-start(bf16[128,8,512]{2,1,0:T(8,128)(2,1)} %bitcast.3), calls=%async_computation | async-start | bytes 2097152 | tf_op jit(solution)/shard_map/all_to_all | solution.py:237
  26.2 2.2 %shard_map.112 = bf16[1024,384]{1,0:T(8,128)(2,1)} custom-call(s32[1]{0:T(128)} %bitcast.2.me_ref, bf16[2048,128]{1,0:T(8,128)(2,1)} %bitcast.17, bf16[2048,128]{1,0:T(8,128)(2,1)} %bitcast.19, bf16[128,2048]{1,0:T(8,128)(2,1)} %bitcast.21), custom_call_target="tpu_custom_call" | custom-call | bytes 1572864 | tf_op jit(solution)/shard_map/pallas_call | solution.py:218
  28.4 3.1 %collective-permute-start.1 = (bf16[1024,384]{1,0:T(8,128)(2,1)}, bf16[1024,384]{1,0:T(8,128)(2,1)S(1)}, u32[]{:S(2)}, u32[]{:S(2)}) collective-permute-start(bf16[1024,384]{1,0:T(8,128)(2,1)} %shard_map.112), channel_id=1, source_target_pairs={{0,128},{64,192},{128,0},{192,64},{256,384},{320,448},{384,256},{4... | collective-permute-start | bytes 2359304 | tf_op jit(solution)/shard_map/ppermute | solution.py:214
  31.6 1.0 copy-done.1
  32.6 1.0 copy-done.2
  34.3 3.1 %collective-permute-start = (bf16[512,384]{1,0:T(8,128)(2,1)S(1)}, bf16[512,384]{1,0:T(8,128)(2,1)S(1)}, u32[]{:S(2)}, u32[]{:S(2)}) collective-permute-start(bf16[512,384]{1,0:T(8,128)(2,1)S(1)} %slice.12), channel_id=1, source_target_pairs={{0,64},{64,0},{128,192},{192,128},{256,320},{320,256},{384,448},{4... | collective-permute-start | bytes 1179656 | tf_op jit(solution)/shard_map/ppermute | solution.py:214
  37.4 29.6 %collective-permute-done.1.second_ref.refs_2_ = bf16[1024,384]{1,0:T(8,128)(2,1)S(1)} collective-permute-done((bf16[1024,384]{1,0:T(8,128)(2,1)}, bf16[1024,384]{1,0:T(8,128)(2,1)S(1)}, u32[]{:S(2)}, u32[]{:S(2)}) %collective-permute-start.1) | collective-permute-done | bytes 786464 | tf_op jit(solution)/shard_map/ppermute | solution.py:214
  67.1 2.7 %collective-permute-start.2 = (bf16[512,384]{1,0:T(8,128)(2,1)S(1)}, bf16[512,384]{1,0:T(8,128)(2,1)S(1)}, u32[]{:S(2)}, u32[]{:S(2)}) collective-permute-start(bf16[512,384]{1,0:T(8,128)(2,1)S(1)} %slice.13), channel_id=1, source_target_pairs={{0,64},{64,0},{128,192},{192,128},{256,320},{320,256},{384,448},{4... | collective-permute-start | bytes 1179656 | tf_op jit(solution)/shard_map/ppermute | solution.py:214
  69.8 1.3 collective-permute-done.2.second_ref.refs_3_
  71.7 2.3 %collective-permute-start.3 = (bf16[1024,384]{1,0:T(8,128)(2,1)S(1)}, bf16[1024,384]{1,0:T(8,128)(2,1)S(1)}, u32[]{:S(2)}, u32[]{:S(2)}) collective-permute-start(bf16[1024,384]{1,0:T(8,128)(2,1)S(1)} %shard_map.114), channel_id=1, source_target_pairs={{0,64},{64,0},{128,192},{192,128},{256,320},{320,256},{384,448},{4... | collective-permute-start | bytes 2359304 | tf_op jit(solution)/shard_map/ppermute | solution.py:214
  74.6 1.3 collective-permute-done.3.core_ref
  76.0 3.0 %collective-permute-start.4 = (bf16[512,384]{1,0:T(8,128)(2,1)S(1)}, bf16[512,384]{1,0:T(8,128)(2,1)S(1)}, u32[]{:S(2)}, u32[]{:S(2)}) collective-permute-start(bf16[512,384]{1,0:T(8,128)(2,1)S(1)} %add_convert_fusion), channel_id=1, source_target_pairs={{0,128},{64,192},{128,0},{192,64},{256,384},{320,448},{384,256},{4... | collective-permute-start | bytes 1179656 | tf_op jit(solution)/shard_map/ppermute | solution.py:214
  78.9 9.2 %collective-permute-done.4.chip_ref = bf16[512,384]{1,0:T(8,128)(2,1)S(1)} collective-permute-done((bf16[512,384]{1,0:T(8,128)(2,1)S(1)}, bf16[512,384]{1,0:T(8,128)(2,1)S(1)}, u32[]{:S(2)}, u32[]{:S(2)}) %collective-permute-start.4) | collective-permute-done | bytes 393248 | tf_op jit(solution)/shard_map/ppermute | solution.py:214
  88.4 3.3 %collective-permute-start.6 = (bf16[512,384]{1,0:T(8,128)(2,1)S(1)}, bf16[512,384]{1,0:T(8,128)(2,1)S(1)}, u32[]{:S(2)}, u32[]{:S(2)}) collective-permute-start(bf16[512,384]{1,0:T(8,128)(2,1)S(1)} %shard_map.115.refs_0_.h0_ref), channel_id=1, source_target_pairs={{0,64},{64,0},{128,192},{192,128},{256,320},{320,256},{384,448},{4... | collective-permute-start | bytes 1179656 | tf_op jit(solution)/shard_map/ppermute | solution.py:214
  91.7 3.0 %collective-permute-start.5 = (bf16[512,384]{1,0:T(8,128)(2,1)S(1)}, bf16[512,384]{1,0:T(8,128)(2,1)S(1)}, u32[]{:S(2)}, u32[]{:S(2)}) collective-permute-start(bf16[512,384]{1,0:T(8,128)(2,1)S(1)} %shard_map.115.refs_0_.h0_ref), channel_id=1, source_target_pairs={{0,128},{64,192},{128,0},{192,64},{256,384},{320,448},{384,256},{4... | collective-permute-start | bytes 1179656 | tf_op jit(solution)/shard_map/ppermute | solution.py:214
  95.3 8.9 %collective-permute-done.5.refs_0_ = bf16[512,384]{1,0:T(8,128)(2,1)S(1)} collective-permute-done((bf16[512,384]{1,0:T(8,128)(2,1)S(1)}, bf16[512,384]{1,0:T(8,128)(2,1)S(1)}, u32[]{:S(2)}, u32[]{:S(2)}) %collective-permute-start.5) | collective-permute-done | bytes 393248 | tf_op jit(solution)/shard_map/ppermute | solution.py:214
  104.3 2.8 %collective-permute-start.7 = (bf16[512,384]{1,0:T(8,128)(2,1)S(1)}, bf16[512,384]{1,0:T(8,128)(2,1)S(1)}, u32[]{:S(2)}, u32[]{:S(2)}) collective-permute-start(bf16[512,384]{1,0:T(8,128)(2,1)S(1)} %collective-permute-done.5.refs_0_), channel_id=1, source_target_pairs={{0,64},{64,0},{128,192},{192,128},{256,320},{320,256},{384,448},{4... | collective-permute-start | bytes 1179656 | tf_op jit(solution)/shard_map/ppermute | solution.py:214
  107.0 1.3 collective-permute-done.7.refs_1_
  108.4 1.6 shard_map.117
  110.0 15.1 %all-to-all-start.1 = ((bf16[128,8,512]{2,1,0:T(8,128)(2,1)}), bf16[128,8,512]{2,1,0:T(8,128)(2,1)S(1)}, u32[]{:S(2)}, u32[]{:S(2)}) async-start(bf16[128,8,512]{2,1,0:T(8,128)(2,1)} %bitcast.8), calls=%async_computation.1 | async-start | bytes 2097152 | tf_op jit(solution)/shard_map/all_to_all | solution.py:237
  125.1 2.4 %collective-permute-start.8 = (bf16[1024,512]{1,0:T(8,128)(2,1)S(1)}, bf16[1024,512]{1,0:T(8,128)(2,1)S(1)}, u32[]{:S(2)}, u32[]{:S(2)}) collective-permute-start(bf16[1024,512]{1,0:T(8,128)(2,1)S(1)} %bitcast.15), channel_id=1, source_target_pairs={{0,128},{64,192},{128,0},{192,64},{256,384},{320,448},{384,256},{4... | collective-permute-start | bytes 3145736 | tf_op jit(solution)/shard_map/ppermute | solution.py:214
  127.5 43.5 %collective-permute-done.8.near_ref = bf16[1024,512]{1,0:T(8,128)(2,1)S(1)} collective-permute-done((bf16[1024,512]{1,0:T(8,128)(2,1)S(1)}, bf16[1024,512]{1,0:T(8,128)(2,1)S(1)}, u32[]{:S(2)}, u32[]{:S(2)}) %collective-permute-start.8) | collective-permute-done | bytes 1048608 | tf_op jit(solution)/shard_map/ppermute | solution.py:214
  171.1 2.0 %shard_map.119 = (bf16[1024,384]{1,0:T(8,128)(2,1)S(1)}, bf16[1024,384]{1,0:T(8,128)(2,1)}) custom-call(bf16[1024,512]{1,0:T(8,128)(2,1)S(1)} %bitcast.16, bf16[1024,512]{1,0:T(8,128)(2,1)S(1)} %collective-permute-done.8.near_ref, bf16[512,384]{1,0:T(8,128)(2,1)S(1)} %shard_map.115.refs_0_.h0_ref, bf16[512,384]{1,0:T(8,128)(2,1)S(1)} %copy-done.8), custom_call_target="tpu_custom_call" | custom-call | flops 805306368 | bytes 4456448 | tf_op jit(solution)/shard_map/pallas_call | solution.py:28
  173.1 0.9 copy-done.5
  173.9 2.4 %collective-permute-start.9 = (bf16[1024,384]{1,0:T(8,128)(2,1)}, bf16[1024,384]{1,0:T(8,128)(2,1)S(1)}, u32[]{:S(2)}, u32[]{:S(2)}) collective-permute-start(bf16[1024,384]{1,0:T(8,128)(2,1)} %get-tuple-element.37), channel_id=1, source_target_pairs={{0,64},{64,0},{128,192},{192,128},{256,320},{320,256},{384,448},{4... | collective-permute-start | bytes 2359304 | tf_op jit(solution)/shard_map/ppermute | solution.py:214
  176.5 2.0 %collective-permute-done.9.got_ref = bf16[1024,384]{1,0:T(8,128)(2,1)S(1)} collective-permute-done((bf16[1024,384]{1,0:T(8,128)(2,1)}, bf16[1024,384]{1,0:T(8,128)(2,1)S(1)}, u32[]{:S(2)}, u32[]{:S(2)}) %collective-permute-start.9) | collective-permute-done | bytes 786464 | tf_op jit(solution)/shard_map/ppermute | solution.py:214
  178.5 1.1 copy-done.6
  179.6 1.3 shard_map.120
  181.0 1.2 shard_map.118
  (35 shorter events, 4.2 us)
Async XLA Ops:
  0.6 0.7 copy-start.9
  1.3 0.9 copy-start.11
  2.2 0.9 copy-start.12
  3.1 0.7 copy-start.13
  5.3 26.3 %copy-start = (bf16[1,2048,128]{2,1,0:T(8,128)(2,1)S(1)}, bf16[1,2048,128]{2,1,0:T(8,128)(2,1)}, u32[]{:S(2)}) copy-start(bf16[1,2048,128]{2,1,0:T(8,128)(2,1)} %param.11) | copy-start | bytes 1572868
  5.3 65.8 %all-to-all-start = ((bf16[128,8,512]{2,1,0:T(8,128)(2,1)}), bf16[128,8,512]{2,1,0:T(8,128)(2,1)S(1)}, u32[]{:S(2)}, u32[]{:S(2)}) async-start(bf16[128,8,512]{2,1,0:T(8,128)(2,1)} %bitcast.3), calls=%async_computation | async-start | bytes 2097152 | tf_op jit(solution)/shard_map/all_to_all | solution.py:237
  28.4 38.6 %collective-permute-start.1 = (bf16[1024,384]{1,0:T(8,128)(2,1)}, bf16[1024,384]{1,0:T(8,128)(2,1)S(1)}, u32[]{:S(2)}, u32[]{:S(2)}) collective-permute-start(bf16[1024,384]{1,0:T(8,128)(2,1)} %shard_map.112), channel_id=1, source_target_pairs={{0,128},{64,192},{128,0},{192,64},{256,384},{320,448},{384,256},{4... | collective-permute-start | bytes 2359304 | tf_op jit(solution)/shard_map/ppermute | solution.py:214
  31.6 1.0 copy-start.1
  32.6 1.0 copy-start.2
  34.3 35.5 %collective-permute-start = (bf16[512,384]{1,0:T(8,128)(2,1)S(1)}, bf16[512,384]{1,0:T(8,128)(2,1)S(1)}, u32[]{:S(2)}, u32[]{:S(2)}) collective-permute-start(bf16[512,384]{1,0:T(8,128)(2,1)S(1)} %slice.12), channel_id=1, source_target_pairs={{0,64},{64,0},{128,192},{192,128},{256,320},{320,256},{384,448},{4... | collective-permute-start | bytes 1179656 | tf_op jit(solution)/shard_map/ppermute | solution.py:214
  67.1 4.0 %collective-permute-start.2 = (bf16[512,384]{1,0:T(8,128)(2,1)S(1)}, bf16[512,384]{1,0:T(8,128)(2,1)S(1)}, u32[]{:S(2)}, u32[]{:S(2)}) collective-permute-start(bf16[512,384]{1,0:T(8,128)(2,1)S(1)} %slice.13), channel_id=1, source_target_pairs={{0,64},{64,0},{128,192},{192,128},{256,320},{320,256},{384,448},{4... | collective-permute-start | bytes 1179656 | tf_op jit(solution)/shard_map/ppermute | solution.py:214
  71.1 3.5 %copy-start.3 = (bf16[512,384]{1,0:T(8,128)(2,1)}, bf16[512,384]{1,0:T(8,128)(2,1)S(1)}, u32[]{:S(2)}) copy-start(bf16[512,384]{1,0:T(8,128)(2,1)S(1)} %collective-permute-done.2.second_ref.refs_3_) | copy-start | bytes 1179652
  71.7 4.2 %collective-permute-start.3 = (bf16[1024,384]{1,0:T(8,128)(2,1)S(1)}, bf16[1024,384]{1,0:T(8,128)(2,1)S(1)}, u32[]{:S(2)}, u32[]{:S(2)}) collective-permute-start(bf16[1024,384]{1,0:T(8,128)(2,1)S(1)} %shard_map.114), channel_id=1, source_target_pairs={{0,64},{64,0},{128,192},{192,128},{256,320},{320,256},{384,448},{4... | collective-permute-start | bytes 2359304 | tf_op jit(solution)/shard_map/ppermute | solution.py:214
  76.0 12.2 %collective-permute-start.4 = (bf16[512,384]{1,0:T(8,128)(2,1)S(1)}, bf16[512,384]{1,0:T(8,128)(2,1)S(1)}, u32[]{:S(2)}, u32[]{:S(2)}) collective-permute-start(bf16[512,384]{1,0:T(8,128)(2,1)S(1)} %add_convert_fusion), channel_id=1, source_target_pairs={{0,128},{64,192},{128,0},{192,64},{256,384},{320,448},{384,256},{4... | collective-permute-start | bytes 1179656 | tf_op jit(solution)/shard_map/ppermute | solution.py:214
  88.4 20.0 %copy-start.4 = (bf16[512,384]{1,0:T(8,128)(2,1)S(1)}, bf16[512,384]{1,0:T(8,128)(2,1)}, u32[]{:S(2)}) copy-start(bf16[512,384]{1,0:T(8,128)(2,1)} %copy-done.3) | copy-start | bytes 1179652
  88.4 6.3 %collective-permute-start.6 = (bf16[512,384]{1,0:T(8,128)(2,1)S(1)}, bf16[512,384]{1,0:T(8,128)(2,1)S(1)}, u32[]{:S(2)}, u32[]{:S(2)}) collective-permute-start(bf16[512,384]{1,0:T(8,128)(2,1)S(1)} %shard_map.115.refs_0_.h0_ref), channel_id=1, source_target_pairs={{0,64},{64,0},{128,192},{192,128},{256,320},{320,256},{384,448},{4... | collective-permute-start | bytes 1179656 | tf_op jit(solution)/shard_map/ppermute | solution.py:214
  91.7 12.6 %collective-permute-start.5 = (bf16[512,384]{1,0:T(8,128)(2,1)S(1)}, bf16[512,384]{1,0:T(8,128)(2,1)S(1)}, u32[]{:S(2)}, u32[]{:S(2)}) collective-permute-start(bf16[512,384]{1,0:T(8,128)(2,1)S(1)} %shard_map.115.refs_0_.h0_ref), channel_id=1, source_target_pairs={{0,128},{64,192},{128,0},{192,64},{256,384},{320,448},{384,256},{4... | collective-permute-start | bytes 1179656 | tf_op jit(solution)/shard_map/ppermute | solution.py:214
  94.7 9.6 %copy-start.7 = (bf16[512,384]{1,0:T(8,128)(2,1)}, bf16[512,384]{1,0:T(8,128)(2,1)S(1)}, u32[]{:S(2)}) copy-start(bf16[512,384]{1,0:T(8,128)(2,1)S(1)} %collective-permute-done.6.refs_1_.h1_ref) | copy-start | bytes 1179652
  104.3 4.1 %collective-permute-start.7 = (bf16[512,384]{1,0:T(8,128)(2,1)S(1)}, bf16[512,384]{1,0:T(8,128)(2,1)S(1)}, u32[]{:S(2)}, u32[]{:S(2)}) collective-permute-start(bf16[512,384]{1,0:T(8,128)(2,1)S(1)} %collective-permute-done.5.refs_0_), channel_id=1, source_target_pairs={{0,64},{64,0},{128,192},{192,128},{256,320},{320,256},{384,448},{4... | collective-permute-start | bytes 1179656 | tf_op jit(solution)/shard_map/ppermute | solution.py:214
  110.0 61.1 %copy-start.8 = (bf16[512,384]{1,0:T(8,128)(2,1)S(1)}, bf16[512,384]{1,0:T(8,128)(2,1)}, u32[]{:S(2)}) copy-start(bf16[512,384]{1,0:T(8,128)(2,1)} %copy-done.7) | copy-start | bytes 1179652
  110.0 66.5 %copy-start.10 = (f32[160,2]{0,1:T(2,128)S(1)}, f32[160,2]{0,1:T(2,128)}, u32[]{:S(2)}) copy-start(f32[160,2]{0,1:T(2,128)} %param.10) | copy-start | bytes 3844
  110.0 71.0 %all-to-all-start.1 = ((bf16[128,8,512]{2,1,0:T(8,128)(2,1)}), bf16[128,8,512]{2,1,0:T(8,128)(2,1)S(1)}, u32[]{:S(2)}, u32[]{:S(2)}) async-start(bf16[128,8,512]{2,1,0:T(8,128)(2,1)} %bitcast.8), calls=%async_computation.1 | async-start | bytes 2097152 | tf_op jit(solution)/shard_map/all_to_all | solution.py:237
  125.1 46.0 %collective-permute-start.8 = (bf16[1024,512]{1,0:T(8,128)(2,1)S(1)}, bf16[1024,512]{1,0:T(8,128)(2,1)S(1)}, u32[]{:S(2)}, u32[]{:S(2)}) collective-permute-start(bf16[1024,512]{1,0:T(8,128)(2,1)S(1)} %bitcast.15), channel_id=1, source_target_pairs={{0,128},{64,192},{128,0},{192,64},{256,384},{320,448},{384,256},{4... | collective-permute-start | bytes 3145736 | tf_op jit(solution)/shard_map/ppermute | solution.py:214
  173.1 0.9 copy-start.5
  173.9 4.6 %collective-permute-start.9 = (bf16[1024,384]{1,0:T(8,128)(2,1)}, bf16[1024,384]{1,0:T(8,128)(2,1)S(1)}, u32[]{:S(2)}, u32[]{:S(2)}) collective-permute-start(bf16[1024,384]{1,0:T(8,128)(2,1)} %get-tuple-element.37), channel_id=1, source_target_pairs={{0,64},{64,0},{128,192},{192,128},{256,320},{320,256},{384,448},{4... | collective-permute-start | bytes 2359304 | tf_op jit(solution)/shard_map/ppermute | solution.py:214
  178.5 1.1 copy-start.6
